TPU v7x, 32 devices: a whole 2x2x4 slice. The times are simulated.
32 devices in a mesh: heads: 2 (over y), blocks: 16 (over z, x, core).
Axes of the slice: x: 2, y: 2, z: 4, core: 2. Of those that a mesh axis runs over, the one named last changes fastest.
Arguments:
- hidden: bfloat16 [128, 2048], P(None, 'blocks'), may hold values from -18 to 18
- w_query: bfloat16 [2048, 2048], P('blocks', 'heads'), may hold values from -1 to 1
- w_key: bfloat16 [2048, 2048], P('blocks', 'heads'), may hold values from -1 to 1
- w_value: bfloat16 [2048, 2048], P('blocks', 'heads'), may hold values from -0.125 to 0.125
- w_out: bfloat16 [2048, 2048], P('heads', 'blocks'), may hold values from -0.125 to 0.125
- cache_key: bfloat16 [4, 16384, 2048], P(None, 'blocks', 'heads'), may hold values from -80 to 80
- cache_value: bfloat16 [4, 16384, 2048], P(None, 'blocks', 'heads'), may hold values from -6 to 6
- parents: int32 [4, 32], replicated, may hold values from 0 to 30, as said below
- lengths: int32 [4], replicated, may hold values from 1 to 16352
- holder: int32 [4, 16], replicated, may hold values from 0 to 15, as said below
- selector: int32 [4, 32, 32], replicated, may hold values from 0 to 1, as said below
Outputs:
- mixed: bfloat16 [128, 2048], P('heads', 'blocks')
- key_out: bfloat16 [4, 16384, 2048], P(None, 'blocks', 'heads')
- value_out: bfloat16 [4, 16384, 2048], P(None, 'blocks', 'heads')
Inputs may be any that keep to these rules, and one draw needn't show every extreme that they name: parents[r, 0] = 0; for i >= 1, parents[r, i] is one of the four tokens before i (never below 0). Each row is a permutation of 0 to 15; for the first 2 requests holder[r, j] = j. For each request, the first rows of selector[r] are one-hot and pick the tokens of one path from the root down the tree, row a picking the token of depth a; the other rows are zero.
All inputs are finite; a program needn't handle non-finite values.
Results may differ from a plain program's by a relative error of at most 0.012.
The roundings to bfloat16 on the way count: a program that leaves them out, or rounds other values in their place, can miss the bound.
Values may be sent and summed in bfloat16 or wider, within the bound.
No kernel may reach another device: no remote copies, remote signals or barrier semaphores. Data moves between devices by JAX's collectives and lax.ppermute only.
A program may use at most 192 MiB of HBM per device.

v0:
```python
import math

import jax
import jax.numpy as jnp
from jax import lax
from jax.sharding import PartitionSpec as P

HD = 64
ROT = 32


masked_low = -1e30
rotary_base = 10000.0


def joined_2(part, axis, combine):
    gathered = jax.tree.map(lambda a: lax.all_gather(a, axis), part)

    def take(source):
        return jax.tree.map(lambda a: lax.dynamic_index_in_dim(a, source, 0, False), gathered)

    return lax.fori_loop(
        1, lax.axis_size(axis), lambda source, state: combine(state, take(source)), take(0)
    )


def ancestry(parents):
    tree_size = parents.shape[0]
    nodes = jnp.arange(tree_size, dtype=jnp.int32)
    parent_hop = ((parents[:, None] == nodes[None, :]) & (nodes[:, None] > 0)).astype(jnp.float32)
    reached = jnp.eye(tree_size, dtype=jnp.float32) + parent_hop
    for _ in range(tree_size.bit_length()):
        reached = jnp.minimum(jnp.dot(reached, reached, precision=lax.Precision.HIGHEST), 1.0)
    return reached


def rotate(values, positions):
    row_count = values.shape[0]
    shaped = values.reshape(row_count, -1, HD)
    half_rot = ROT // 2
    inverse_freq = rotary_base ** (-2.0 * jnp.arange(half_rot, dtype=jnp.float32) / ROT)
    angles = positions.astype(jnp.float32)[:, None] * inverse_freq[None, :]
    cosine = jnp.cos(angles)[:, None, :]
    sine = jnp.sin(angles)[:, None, :]
    leading = shaped[:, :, :half_rot]
    trailing = shaped[:, :, half_rot:ROT]
    turned = jnp.concatenate(
        [
            leading * cosine - trailing * sine,
            trailing * cosine + leading * sine,
            shaped[:, :, ROT:],
        ],
        axis=2,
    )
    return turned.reshape(row_count, -1)


def finish(summed, positions, local_width):
    queries = rotate(summed[:, :local_width], positions)
    keys_new = rotate(summed[:, local_width : 2 * local_width], positions)
    return jnp.concatenate([queries, keys_new, summed[:, 2 * local_width :]], axis=1).astype(
        jnp.bfloat16
    )


def finalize(cache_top, cache_sum, cache_out, tree_max, tree_sum, tree_out):
    joint_top = jnp.maximum(cache_top, tree_max)
    cache_scale = jnp.exp(cache_top - joint_top)
    tree_scale = jnp.exp(tree_max - joint_top)
    numerator = cache_out * cache_scale[..., None] + tree_out * tree_scale[..., None]
    denominator = cache_sum * cache_scale + tree_sum * tree_scale
    return numerator / denominator[..., None]


def cache_part(queries, cached_keys, cached_values, live_rows, scale):
    scores = (
        jnp.einsum("rihd,rbhd->rihb", queries, cached_keys, preferred_element_type=jnp.float32)
        * scale
    )
    mask = live_rows[:, None, None, :]
    block_max = jnp.max(jnp.where(mask, scores, masked_low), axis=3)
    exponent = jnp.where(mask, jnp.exp(scores - block_max[..., None]), 0.0)
    block_sum = jnp.sum(exponent, axis=3)
    block_out = jnp.einsum(
        "rihb,rbhd->rihd",
        exponent.astype(jnp.bfloat16),
        cached_values,
        preferred_element_type=jnp.float32,
    )
    return (block_max, block_sum, block_out)


def combine(earlier, later):
    max_early, sum_early, out_early = earlier
    max_late, sum_late, out_late = later
    joint_top = jnp.maximum(max_early, max_late)
    scale_early = jnp.exp(max_early - joint_top)
    scale_late = jnp.exp(max_late - joint_top)
    return (
        joint_top,
        sum_early * scale_early + sum_late * scale_late,
        out_early * scale_early[..., None] + out_late * scale_late[..., None],
    )


def on_device(
    hidden,
    w_query,
    w_key,
    w_value,
    w_out,
    cache_key,
    cache_value,
    parents,
    lengths,
    holder,
    selector,
):
    requests, tree_size = parents.shape
    token_count = requests * tree_size
    local_width = w_query.shape[1]
    local_heads = local_width // HD
    block_len = cache_key.shape[1]
    block_count = holder.shape[1]
    scale = 1.0 / math.sqrt(HD)
    ancestors = jax.vmap(ancestry)(parents)
    depths = (jnp.sum(ancestors, axis=2) - 1.0).astype(jnp.int32)
    positions = (lengths[:, None] + depths).reshape(-1)
    joined = jnp.concatenate([w_query, w_key, w_value], axis=1)
    summed = lax.psum(jnp.dot(hidden, joined, preferred_element_type=jnp.float32), "blocks")
    projected = finish(summed, positions, local_width)
    grouped = projected.reshape(requests, tree_size, 3, local_heads, HD)
    queries = grouped[:, :, 0]
    keys_tree = grouped[:, :, 1]
    values_tree = grouped[:, :, 2]
    block_index = lax.axis_index("blocks")
    slots = jnp.arange(block_count, dtype=jnp.int32)
    logical_block = jnp.sum(slots[None, :] * (holder == block_index).astype(jnp.int32), axis=1)
    logical = logical_block[:, None] * block_len + jnp.arange(block_len, dtype=jnp.int32)[None, :]
    live_rows = logical < lengths[:, None]
    cached_keys = cache_key.reshape(requests, block_len, local_heads, HD)
    cached_values = cache_value.reshape(requests, block_len, local_heads, HD)
    block_max, block_sum, block_out = cache_part(
        queries, cached_keys, cached_values, live_rows, scale
    )
    tree_scores = (
        jnp.einsum("rihd,rjhd->rihj", queries, keys_tree, preferred_element_type=jnp.float32)
        * scale
    )
    tree_allowed = (ancestors > 0.5)[:, :, None, :]
    tree_max = jnp.max(jnp.where(tree_allowed, tree_scores, masked_low), axis=3)
    tree_exp = jnp.where(tree_allowed, jnp.exp(tree_scores - tree_max[..., None]), 0.0)
    tree_sum = jnp.sum(tree_exp, axis=3)
    tree_out = jnp.einsum(
        "rihj,rjhd->rihd",
        tree_exp.astype(jnp.bfloat16),
        values_tree,
        preferred_element_type=jnp.float32,
    )
    cache_top, cache_sum, cache_out = joined_2((block_max, block_sum, block_out), "blocks", combine)
    finished = finalize(cache_top, cache_sum, cache_out, tree_max, tree_sum, tree_out)
    attended = finished.reshape(token_count, local_width).astype(jnp.bfloat16)
    mixed = lax.psum_scatter(
        jnp.dot(attended, w_out, preferred_element_type=jnp.float32),
        "heads",
        scatter_dimension=0,
        tiled=True,
    ).astype(jnp.bfloat16)
    accepted = jnp.sum(selector, axis=2) > 0
    key_value = projected[:, local_width:].reshape(requests, tree_size, 2 * local_width)
    fresh = jnp.einsum(
        "rat,rtf->raf", selector.astype(jnp.bfloat16), key_value, preferred_element_type=jnp.float32
    ).astype(jnp.bfloat16)
    offsets = logical - lengths[:, None]
    hits = (
        offsets[:, :, None] == jnp.arange(tree_size, dtype=jnp.int32)[None, None, :]
    ) & accepted[:, None, :]
    written = jnp.einsum(
        "rba,raf->rbf", hits.astype(jnp.bfloat16), fresh, preferred_element_type=jnp.float32
    ).astype(jnp.bfloat16)
    touched = jnp.any(hits, axis=2)[:, :, None]
    key_out = jnp.where(touched, written[:, :, :local_width], cache_key)
    value_out = jnp.where(touched, written[:, :, local_width:], cache_value)
    return (mixed, key_out, value_out)


def solution(mesh):
    return jax.shard_map(
        on_device,
        mesh=mesh,
        in_specs=(
            P(None, "blocks"),
            P("blocks", "heads"),
            P("blocks", "heads"),
            P("blocks", "heads"),
            P("heads", "blocks"),
            P(None, "blocks", "heads"),
            P(None, "blocks", "heads"),
            P(),
            P(),
            P(),
            P(),
        ),
        out_specs=(P("heads", "blocks"), P(None, "blocks", "heads"), P(None, "blocks", "heads")),
        check_vma=False,
    )
```

profile of v0, /device:TPU:0, one launch (start us, length us, event | category | flops | bytes accessed | tf_op | source)
XLA Modules:
  0.0 338.3 jit_solution(15316505488886912803)
XLA Ops:
  7.2 2.7 convolution_bitcast_fusion
  10.0 1.1 convolution_minimum_fusion.5
  11.1 0.2 convolution_minimum_fusion.4
  11.5 0.2 convolution_minimum_fusion.2
  11.9 0.3 fusion.62
  12.1 0.7 add_convert_fusion
  13.0 11.4 %copy.47 = bf16[4,1024,1024]{1,2,0:T(8,128)(2,1)} copy(bf16[4,1024,1024]{2,1,0:T(8,128)(2,1)} %param.18) | data formatting | bytes 16777216 | tf_op args[5]
  24.3 11.4 %copy.48 = bf16[4,1024,1024]{1,2,0:T(8,128)(2,1)} copy(bf16[4,1024,1024]{2,1,0:T(8,128)(2,1)} %param.19) | data formatting | bytes 16777216 | tf_op args[6]
  36.1 74.1 %all-reduce.2.cloned.1.call-done = f32[128,3072]{0,1:T(8,128)} async-done(((f32[128,3072]{0,1:T(8,128)}), f32[128,3072]{0,1:T(8,128)}) %all-reduce.2.cloned.1.call-update) | async-done | bytes 1572880 | tf_op jit(solution)/shard_map/psum | solution.py:130
  110.1 1.3 fusion.61
  111.6 1.1 slice.74
  112.8 0.3 copy.45
  113.0 1.0 convert_element_type.70
  114.1 1.4 fusion.60
  115.5 8.6 %fusion.3 = (f32[4,32,16]{1,2,0:T(8,128)S(1)}, f32[4,16,32,1024]{3,2,1,0:T(8,128)}) fusion(pred[4,1024]{1,0:T(4,128)(4,1)S(1)} %fusion.51, bf16[4,1024,16,64]{1,3,2,0:T(8,128)(2,1)} %bitcast.95, bf16[4,32,1,16,64]{4,3,2,1,0:T(8,128)(2,1)S(1)} %get-tuple-element.223), kind=kOutput, calls=%fused_computation.13 | convolution fusion | flops 274724864 | bytes 17051648 | tf_op jit(solution)/shard_map/rihd,rbhd->rihb/dot_general | solution.py:77
  124.1 8.2 %fusion.14 = f32[4,32,16,64]{3,1,2,0:T(8,128)S(1)} fusion(bf16[4,1024,16,64]{1,3,2,0:T(8,128)(2,1)} %bitcast.96, f32[4,16,32,1024]{3,2,1,0:T(8,128)} %get-tuple-element.237, f32[4,32,16]{1,2,0:T(8,128)S(1)} %get-tuple-element.236, pred[4,1024]{1,0:T(4,128)(4,1)S(1)} %fusion.51), kind=kOutput, calls=%fused_computation.26 | convolution fusion | flops 276824064 | bytes 17313792 | tf_op jit(solution)/shard_map/rihb,rbhd->rihd/dot_general | solution.py:84
  132.2 1.6 copy.49
  134.5 0.2 copy.56
  134.7 4.5 %fusion.7 = f32[4,32,16]{1,2,0:T(8,128)S(1)} fusion(f32[4,16,32,1024]{3,2,1,0:T(8,128)} %get-tuple-element.237, f32[4,32,16]{1,2,0:T(8,128)S(1)} %get-tuple-element.236, pred[4,1024]{1,0:T(4,128)(4,1)S(1)} %fusion.51), kind=kLoop, calls=%fused_computation.17 | loop fusion | flops 8386560 | bytes 8409088 | tf_op jit(solution)/shard_map/reduce_sum | solution.py:83
  139.2 23.6 %all-gather.1 = f32[64,32,16]{1,2,0:T(8,128)S(1)} all-gather(f32[4,32,16]{1,2,0:T(8,128)S(1)} %fusion.7), channel_id=3, replica_groups=mesh['heads'=2,'blocks'=16] {'blocks'}, dimensions={0}, use_global_device_ids=true | all-gather | bytes 139264 | tf_op jit(solution)/shard_map/all_gather | solution.py:17
  162.8 21.9 %all-gather = f32[64,32,16]{1,2,0:T(8,128)S(1)} all-gather(f32[4,32,16]{1,2,0:T(8,128)S(1)} %get-tuple-element.236), channel_id=2, replica_groups=mesh['heads'=2,'blocks'=16] {'blocks'}, dimensions={0}, use_global_device_ids=true | all-gather | bytes 139264 | tf_op jit(solution)/shard_map/all_gather | solution.py:17
  184.7 0.8 copy-done.2
  185.5 1.5 select_reduce_fusion
  186.9 0.3 fusion.22
  187.2 8.6 %convolution_convert_fusion = bf16[4,1024,2048]{2,1,0:T(8,128)(2,1)} fusion(bf16[4,32,2048]{2,1,0:T(8,128)(2,1)S(1)} %bitcast.97, s32[4,1024]{1,0:T(4,128)S(1)} %fusion.50, pred[4,32]{1,0:T(4,128)(4,1)S(1)} %broadcast_compare_fusion.1, s32[4,32,32]{2,1,0:T(8,128)S(1)} %copy-done.4), kind=kOutput, calls=%fused_computation.8 | convolution fusion | flops 562565120 | bytes 17334400 | tf_op jit(solution)/shard_map/rba,raf->rbf/dot_general | solution.py:178
  195.8 69.1 %all-gather.5.cloned.1.call-done = f32[64,32,16,64]{3,2,1,0:T(8,128)} async-done(((f32[4,32,16,64]{3,2,1,0:T(8,128)}), f32[64,32,16,64]{3,2,1,0:T(8,128)}) %all-gather.5.cloned.1.call-update) | async-done | bytes 8388624 | tf_op jit(solution)/shard_map/all_gather | solution.py:17
  264.9 1.3 slice.78
  266.2 43.5 %while.19 = (s32[]{:T(128)}, f32[4,32,16]{1,2,0:T(8,128)S(1)}, f32[4,32,16]{1,2,0:T(8,128)S(1)}, f32[4,32,16,64]{3,2,1,0:T(8,128)S(1)}, f32[16,4,32,16]{2,3,1,0:...) while((s32[]{:T(128)}, f32[4,32,16]{1,2,0:T(8,128)S(1)}, ...), condition=%wide.region_6.7_spmd, body=%wide.region_5.6_spmd.sunk | while | flops 405509 | bytes 1687695 | solution.py:22
  266.2 0.9 fusion.82
  267.3 1.9 fusion.83
  269.2 0.8 fusion.82
  270.2 1.9 fusion.83
  272.1 0.8 fusion.82
  273.0 1.9 fusion.83
  275.0 0.8 fusion.82
  275.9 1.9 fusion.83
  277.9 0.8 fusion.82
  278.8 1.9 fusion.83
  280.8 0.8 fusion.82
  281.7 1.9 fusion.83
  283.7 0.8 fusion.82
  284.6 1.9 fusion.83
  286.6 0.8 fusion.82
  287.5 1.9 fusion.83
  289.5 0.8 fusion.82
  290.4 1.9 fusion.83
  292.3 0.8 fusion.82
  293.3 1.9 fusion.83
  295.2 0.8 fusion.82
  296.2 1.9 fusion.83
  298.1 0.8 fusion.82
  299.1 1.9 fusion.83
  301.0 0.8 fusion.82
  302.0 1.9 fusion.83
  303.9 0.8 fusion.82
  304.9 1.9 fusion.83
  306.8 0.8 fusion.82
  307.8 1.9 fusion.83
  309.8 1.3 fusion.21
  311.0 0.2 copy.55
  311.2 0.3 convert_element_type.74
  311.6 0.8 fusion.63
  312.5 18.0 %slice_select_fusion = (bf16[4,1024,1024]{2,1,0:T(8,128)(2,1)}, bf16[4,1024,1024]{2,1,0:T(8,128)(2,1)}) fusion(bf16[4,1024,1024]{2,1,0:T(8,128)(2,1)} %param.19, bf16[4,1024,2048]{2,1,0:T(8,128)(2,1)} %convolution_convert_fusion, pred[4,1024]{1,0:T(4,128)(4,1)S(1)} %fusion.34, bf16[4,1024,1024]{2,1,0:T(8,128)(2,1)} %param.18), kind=kLoop, calls=%fused_computation.9 | loop fusion | flops 8388608 | bytes 50335744 | tf_op jit(solution)/shard_map/jit(_where)/select_n | solution.py:183
  330.4 1.4 convert_element_type.75
  (75 shorter events, 4.1 us)
Async XLA Ops:
  7.2 304.4 %copy-start = (bf16[1024,128]{1,0:T(8,128)(2,1)S(1)}, bf16[1024,128]{1,0:T(8,128)(2,1)}, u32[]{:S(2)}) copy-start(bf16[1024,128]{1,0:T(8,128)(2,1)} %param.17) | copy-start | bytes 786436
  7.2 103.0 %all-reduce.2.cloned.1.call-start = ((), (), s32[]{:S(2)}) async-start(), calls=%async_computation.1 | async-start | bytes 3145728 | tf_op jit(solution)/shard_map/psum | solution.py:130
  9.9 255.0 %all-gather.5.cloned.1.call-start = ((), (), s32[]{:S(2)}) async-start(), calls=%async_computation.3 | async-start | bytes 17825792 | tf_op jit(solution)/shard_map/all_gather | solution.py:17
  24.3 11.4 %copy-start.6 = (s32[4,16]{1,0:T(4,128)S(1)}, s32[4,16]{1,0:T(4,128)}, u32[]{:S(2)}) copy-start(s32[4,16]{1,0:T(4,128)} %param.22) | copy-start | bytes 772
  24.3 11.6 %copy-start.5 = (s32[4]{0:T(128)S(1)}, s32[4]{0:T(128)}, u32[]{:S(2)}) copy-start(s32[4]{0:T(128)} %param.21) | copy-start | bytes 52
  124.1 9.8 %copy-start.4 = (s32[4,32,32]{2,1,0:T(8,128)S(1)}, s32[4,32,32]{2,1,0:T(8,128)}, u32[]{:S(2)}) copy-start(s32[4,32,32]{2,1,0:T(8,128)} %param.23) | copy-start | bytes 49156
  133.9 196.6 %reduce-scatter.2.cloned.1.call-start = ((), (), s32[]{:S(2)}) async-start(), calls=%async_computation.2 | async-start | bytes 98304 | tf_op jit(solution)/shard_map/reduce_scatter | solution.py:163
  162.8 33.1 %copy-start.1 = (f32[64,32,16]{1,2,0:T(8,128)}, f32[64,32,16]{1,2,0:T(8,128)S(1)}, u32[]{:S(2)}) copy-start(f32[64,32,16]{1,2,0:T(8,128)S(1)} %all-gather.1) | copy-start | bytes 393220
  184.7 0.8 copy-start.2
  266.2 43.5 %copy-start.3 = (bf16[4,32,1,16,64]{4,3,2,1,0:T(8,128)(2,1)S(1)}, bf16[4,32,1,16,64]{4,3,2,1,0:T(8,128)(2,1)}, u32[]{:S(2)}) copy-start(bf16[4,32,1,16,64]{4,3,2,1,0:T(8,128)(2,1)} %get-tuple-element.221) | copy-start | bytes 786436
Sparse Core Ops, SparseCore 0:
  12.1 98.0 all-reduce.1
  134.0 130.8 all-gather.4
  312.6 8.0 reduce-scatter.1
where the time goes:
time: 341 us; the launch traced here: 338 us
  waiting for transfers between devices  143 us (42%)
  other arithmetic  66.6 us (20%)
  blocking collectives  45.5 us (13%)
  local copies, waits for them, and re-layouts  34.8 us (10%)
  matrix products  33.7 us (10%)
  between operations  14 us (4%)
    psum x1, waiting for transfers between devices, on_device(): lax.psum(jnp.dot(hidden, joined, preferred_element_type=jnp.float32), 'bl...  74.1 us
    all_gather x1, waiting for transfers between devices, joined_2(): gathered = jax.tree.map(lambda a: lax.all_gather(a, axis), part)  69.1 us
    all_gather x2, blocking collectives, joined_2(): gathered = jax.tree.map(lambda a: lax.all_gather(a, axis), part)  45.5 us
    add x15, other arithmetic, combine(): out_early * scale_early[..., None] + out_late * scale_late[..., None]  28.5 us
    unnamed x16, local copies, waits for them, and re-layouts  23.6 us
    select_n x1, other arithmetic, on_device(): value_out = jnp.where(touched, written[:, :, local_width:], cache_value)  18 us
    add x15, other arithmetic, combine(): sum_early * scale_early + sum_late * scale_late  12.3 us
    dot_general x1, matrix products, cache_part(): jnp.einsum('rihd,rbhd->rihb', queries, cached_keys, preferred_element_typ...  8.6 us
  transfers between devices with their start and end apart: 3, of which 2 were waited for; matrix products, arithmetic and copies ran while one was open for 18% of the time, Pallas kernels for 0%

commit v1 on v0

v1 whole, which is shorter than its diff:
```python
import functools
import math

import jax
import jax.numpy as jnp
from jax import lax
from jax.experimental import pallas as pl
from jax.experimental.pallas import tpu as pltpu
from jax.sharding import PartitionSpec as P

HD = 64
ROT = 32
LANES = 128


masked_low = -1e30
rotary_base = 10000.0


def swap(value, axis, bit):
    size = lax.axis_size(axis)
    return lax.ppermute(value, axis, [(i, i ^ bit) for i in range(size)])


def ancestry(parents):
    tree_size = parents.shape[0]
    nodes = jnp.arange(tree_size, dtype=jnp.int32)
    parent_hop = ((parents[:, None] == nodes[None, :]) & (nodes[:, None] > 0)).astype(jnp.float32)
    reached = jnp.eye(tree_size, dtype=jnp.float32) + parent_hop
    for _ in range(tree_size.bit_length()):
        reached = jnp.minimum(jnp.dot(reached, reached, precision=lax.Precision.HIGHEST), 1.0)
    return reached


def rotary_tables(positions):
    column = jnp.arange(LANES, dtype=jnp.int32) % HD
    half = ROT // 2
    exponent = (column % half).astype(jnp.float32)
    inverse_freq = rotary_base ** (-2.0 * exponent / ROT)
    angles = positions.astype(jnp.float32)[:, None] * inverse_freq[None, :]
    cosine = jnp.where(column < ROT, jnp.cos(angles), 1.0)
    sine = jnp.sin(angles)
    ahead = jnp.where(column < half, -sine, 0.0)
    behind = jnp.where((column >= half) & (column < ROT), sine, 0.0)
    return jnp.stack([cosine, ahead, behind])


def turn(chunk, tables):
    half = ROT // 2
    ahead = pltpu.roll(chunk, LANES - half, axis=1)
    behind = pltpu.roll(chunk, half, axis=1)
    return chunk * tables[0] + ahead * tables[1] + behind * tables[2]


def add_rotate_kernel(rotated_width, one_ref, two_ref, tables_ref, out_ref):
    for start in range(0, one_ref.shape[1], LANES):
        columns = slice(start, start + LANES)
        chunk = one_ref[:, columns] + two_ref[:, columns]
        if start < rotated_width:
            chunk = turn(chunk, tables_ref)
        out_ref[:, columns] = chunk.astype(out_ref.dtype)


def add_rotate(one, two, tables, rotated_width):
    return pl.pallas_call(
        functools.partial(add_rotate_kernel, rotated_width),
        out_shape=jax.ShapeDtypeStruct(one.shape, jnp.bfloat16),
        name="add_rotate",
    )(one, two, tables)


def head_of(extent, axis, shape, unit):
    return lax.broadcasted_iota(jnp.int32, shape, axis) // unit


def block_diagonal(queries, heads):
    tokens, width = queries.shape
    tall = jnp.concatenate([queries] * heads, axis=0)
    shape = (heads * tokens, width)
    row_head = lax.broadcasted_iota(jnp.int32, shape, 0) // tokens
    column_head = lax.broadcasted_iota(jnp.int32, shape, 1) // HD
    return jnp.where(row_head == column_head, tall, jnp.zeros_like(tall))


def diagonal_blocks(tall, heads, tokens):
    width = tall.shape[1]
    column_head = lax.broadcasted_iota(jnp.int32, (tokens, width), 1) // HD
    out = tall[:tokens]
    for head in range(1, heads):
        out = jnp.where(column_head == head, tall[head * tokens : (head + 1) * tokens], out)
    return out


def cache_kernel(slot, heads, scale, reqs, live, q_ref, k_ref, v_ref, out_ref, stat_ref):
    group = pl.program_id(0)
    tokens = q_ref.shape[0]
    queries = block_diagonal(q_ref[...], heads)
    keys = k_ref[0]
    values = v_ref[0]
    scores = lax.dot_general(
        queries, keys, (((1,), (1,)), ((), ())), preferred_element_type=jnp.float32
    ) * scale
    mask = lax.broadcasted_iota(jnp.int32, scores.shape, 1) < live[reqs[slot]]
    scores = jnp.where(mask, scores, masked_low)
    top = jnp.max(scores, axis=1, keepdims=True)
    exponent = jnp.where(mask, jnp.exp(scores - top), 0.0)
    total = jnp.sum(exponent, axis=1, keepdims=True)
    out = jnp.dot(exponent.astype(jnp.bfloat16), values, preferred_element_type=jnp.float32)
    out_ref[...] = diagonal_blocks(out, heads, tokens)
    lane = lax.broadcasted_iota(jnp.int32, (tokens, LANES), 1)
    stats = jnp.where(group == 0, jnp.zeros((tokens, LANES), jnp.float32), stat_ref[...])
    for head in range(heads):
        rows = slice(head * tokens, (head + 1) * tokens)
        where = group * heads + head
        stats = jnp.where(lane == where, top[rows], stats)
        stats = jnp.where(lane == where + HD, total[rows], stats)
    stat_ref[...] = stats


def cache_attention(slot, queries, cache_key, cache_value, reqs, live, scale):
    tokens, width = queries.shape
    block_len = cache_key.shape[1]
    group = min(256, width)
    heads = group // HD
    cache_spec = pl.BlockSpec((1, block_len, group), lambda g, reqs, live: (reqs[slot], 0, g))
    return pl.pallas_call(
        functools.partial(cache_kernel, slot, heads, scale),
        grid_spec=pltpu.PrefetchScalarGridSpec(
            num_scalar_prefetch=2,
            grid=(width // group,),
            in_specs=[pl.BlockSpec((tokens, group), lambda g, reqs, live: (0, g)), cache_spec, cache_spec],
            out_specs=[
                pl.BlockSpec((tokens, group), lambda g, reqs, live: (0, g)),
                pl.BlockSpec((tokens, LANES), lambda g, reqs, live: (0, 0)),
            ],
        ),
        out_shape=[
            jax.ShapeDtypeStruct((tokens, width), jnp.float32),
            jax.ShapeDtypeStruct((tokens, LANES), jnp.float32),
        ],
        cost_estimate=pl.CostEstimate(
            flops=4 * tokens * width * block_len * heads,
            transcendentals=tokens * (width // HD) * block_len,
            bytes_accessed=4 * block_len * width,
        ),
        name="cache_attention",
    )(reqs, live, queries, cache_key, cache_value)


def spread(stats, pair, shape):
    lane = lax.broadcasted_iota(jnp.int32, shape, 1)
    first = jnp.broadcast_to(stats[:, 2 * pair : 2 * pair + 1], shape)
    second = jnp.broadcast_to(stats[:, 2 * pair + 1 : 2 * pair + 2], shape)
    return jnp.where(lane < HD, first, second)


def merged_stats(one, two):
    top = jnp.maximum(one, two)
    scale_one = jnp.exp(one - top)
    scale_two = jnp.exp(two - top)
    total = one * pltpu.roll(scale_one, HD, axis=1) + two * pltpu.roll(scale_two, HD, axis=1)
    lane = lax.broadcasted_iota(jnp.int32, one.shape, 1)
    return jnp.where(lane < HD, top, total), scale_one, scale_two


def merge_kernel(width, one_ref, two_ref, out_ref):
    one = one_ref[:, width:]
    two = two_ref[:, width:]
    stats, scale_one, scale_two = merged_stats(one, two)
    out_ref[:, width:] = stats
    for pair in range(width // LANES):
        columns = slice(pair * LANES, (pair + 1) * LANES)
        shape = (one.shape[0], LANES)
        out_ref[:, columns] = one_ref[:, columns] * spread(scale_one, pair, shape) + two_ref[
            :, columns
        ] * spread(scale_two, pair, shape)


def merge(one, two, width):
    return pl.pallas_call(
        functools.partial(merge_kernel, width),
        out_shape=jax.ShapeDtypeStruct(one.shape, jnp.float32),
        name="merge",
    )(one, two)


def finish_kernel(width, heads, scale, one_ref, two_ref, q_ref, kv_ref, tree_ref, out_ref):
    tokens = q_ref.shape[0]
    stats, scale_one, scale_two = merged_stats(one_ref[:, width:], two_ref[:, width:])
    group = heads * HD
    allowed = jnp.concatenate([tree_ref[...]] * heads, axis=0) > 0.5
    lane = lax.broadcasted_iota(jnp.int32, (tokens, LANES), 1)
    tree_stats = jnp.zeros((tokens, LANES), jnp.float32)
    tree_outs = []
    for start in range(0, width, group):
        queries = block_diagonal(q_ref[:, start : start + group], heads)
        keys = kv_ref[:, start : start + group]
        values = kv_ref[:, width + start : width + start + group]
        scores = lax.dot_general(
            queries, keys, (((1,), (1,)), ((), ())), preferred_element_type=jnp.float32
        ) * scale
        scores = jnp.where(allowed, scores, masked_low)
        top = jnp.max(scores, axis=1, keepdims=True)
        exponent = jnp.where(allowed, jnp.exp(scores - top), 0.0)
        total = jnp.sum(exponent, axis=1, keepdims=True)
        out = jnp.dot(exponent.astype(jnp.bfloat16), values, preferred_element_type=jnp.float32)
        tree_outs.append(diagonal_blocks(out, heads, tokens))
        for head in range(heads):
            rows = slice(head * tokens, (head + 1) * tokens)
            where = start // HD + head
            tree_stats = jnp.where(lane == where, top[rows], tree_stats)
            tree_stats = jnp.where(lane == where + HD, total[rows], tree_stats)
    joint, scale_cache, scale_tree = merged_stats(stats, tree_stats)
    total = pltpu.roll(joint, HD, axis=1)
    for pair in range(width // LANES):
        columns = slice(pair * LANES, (pair + 1) * LANES)
        shape = (tokens, LANES)
        cached = one_ref[:, columns] * spread(scale_one, pair, shape) + two_ref[
            :, columns
        ] * spread(scale_two, pair, shape)
        start = pair * LANES
        tree = tree_outs[start // group][:, start % group : start % group + LANES]
        numerator = cached * spread(scale_cache, pair, shape) + tree * spread(scale_tree, pair, shape)
        out_ref[:, columns] = (numerator / spread(total, pair, shape)).astype(out_ref.dtype)


def finish(one, two, queries, key_value, tree, scale):
    tokens, width = queries.shape
    heads = min(256, width) // HD
    return pl.pallas_call(
        functools.partial(finish_kernel, width, heads, scale),
        out_shape=jax.ShapeDtypeStruct((tokens, width), jnp.bfloat16),
        name="finish",
    )(one, two, queries, key_value, tree)


def patch_kernel(firsts, starts, kv_ref, sel_ref, key_ref, value_ref, key_out, value_out):
    request = pl.program_id(0)
    step = pl.program_id(1)
    rows, width = key_ref.shape[1:]
    slots = sel_ref.shape[1]
    last = pl.num_programs(1) - 1
    block = firsts[request, step]
    row = lax.broadcasted_iota(jnp.int32, (rows, slots), 0) + block * rows - starts[request]
    depth = lax.broadcasted_iota(jnp.int32, (rows, slots), 1)
    hits = (row == depth).astype(jnp.bfloat16)
    picks = jnp.dot(hits, sel_ref[0], preferred_element_type=jnp.float32)
    touched = jnp.sum(picks, axis=1, keepdims=True) > 0.5
    written = jnp.dot(
        picks.astype(jnp.bfloat16), kv_ref[0], preferred_element_type=jnp.float32
    ).astype(jnp.bfloat16)
    key_out[0] = jnp.where(touched, written[:, :width], key_ref[0])
    value_out[0] = jnp.where(touched, written[:, width:], value_ref[0])


def patch(key_value, reqs, selector, firsts, starts, keys, values):
    requests, block_len, width = keys.shape
    tokens = selector.shape[1]
    rows = tokens
    cache_spec = pl.BlockSpec((1, rows, width), lambda r, s, firsts, starts: (r, firsts[r, s], 0))
    return pl.pallas_call(
        patch_kernel,
        grid_spec=pltpu.PrefetchScalarGridSpec(
            num_scalar_prefetch=2,
            grid=(requests, 2),
            in_specs=[
                pl.BlockSpec((1, tokens, 2 * width), lambda r, s, firsts, starts: (r, 0, 0)),
                pl.BlockSpec((1, tokens, tokens), lambda r, s, firsts, starts: (r, 0, 0)),
                cache_spec,
                cache_spec,
            ],
            out_specs=[cache_spec, cache_spec],
        ),
        out_shape=[jax.ShapeDtypeStruct(keys.shape, keys.dtype)] * 2,
        input_output_aliases={4: 0, 5: 1},
        cost_estimate=pl.CostEstimate(
            flops=0, transcendentals=0, bytes_accessed=16 * requests * rows * width
        ),
        name="patch",
    )(firsts, starts, key_value, selector, keys, values)


def on_device(
    hidden,
    w_query,
    w_key,
    w_value,
    w_out,
    cache_key,
    cache_value,
    parents,
    lengths,
    holder,
    selector,
):
    requests, tree_size = parents.shape
    width = w_query.shape[1]
    block_len = cache_key.shape[1]
    block_count = holder.shape[1]
    scale = 1.0 / math.sqrt(HD)
    axis = "blocks"
    index = lax.axis_index(axis)
    levels = requests.bit_length() - 1
    bits = block_count.bit_length() - 1
    assert 1 << levels == requests and 1 << bits == block_count and bits > levels
    split = [1 << s for s in range(levels)]
    whole = [1 << s for s in range(levels, bits)]
    own = sum(((index >> s) & 1) << (levels - 1 - s) for s in range(levels))
    reqs = own ^ jnp.arange(requests, dtype=jnp.int32)

    slots = jnp.arange(block_count, dtype=jnp.int32)
    logical = jnp.sum(slots[None, :] * (holder == index).astype(jnp.int32), axis=1)
    starts = lengths - logical * block_len
    live = jnp.clip(starts, 0, block_len)

    rows = jnp.take(hidden.reshape(requests, tree_size, -1), reqs, axis=0)
    rows = rows.reshape(requests * tree_size, -1)

    def scattered(weights):
        value = jnp.dot(rows, weights, preferred_element_type=jnp.float32)
        value = value.reshape(requests, tree_size, -1)
        for bit in split:
            half = value.shape[0] // 2
            value = value[:half] + swap(value[half:], axis, bit)
        value = value[0]
        for bit in whole[:-1]:
            value = value + swap(value, axis, bit)
        return value, swap(value, axis, whole[-1])

    ancestors = ancestry(lax.dynamic_index_in_dim(parents, own, 0, False))
    depths = (jnp.sum(ancestors, axis=1) - 1.0).astype(jnp.int32)
    positions = lax.dynamic_index_in_dim(lengths, own, 0, False) + depths
    tables = rotary_tables(positions)

    query_own = add_rotate(*scattered(w_query), tables, width)
    kv_own = add_rotate(*scattered(jnp.concatenate([w_key, w_value], axis=1)), tables, width)

    def gathered(value):
        value = value[None]
        for bit in reversed(split):
            value = jnp.concatenate([value, swap(value, axis, bit)], axis=0)
        return value

    queries = gathered(query_own)
    parts = [None] * requests
    for slot in reversed(range(requests)):
        out, stats = cache_attention(slot, queries[slot], cache_key, cache_value, reqs, live, scale)
        parts[slot] = jnp.concatenate([out, stats], axis=1)
    count = requests
    for bit in split:
        count //= 2
        received = swap(jnp.concatenate(parts[count:], axis=0), axis, bit)
        parts = [
            merge(parts[k], received[k * tree_size : (k + 1) * tree_size], width)
            for k in range(count)
        ]
    cached = parts[0]
    for bit in whole[:-1]:
        cached = merge(cached, swap(cached, axis, bit), width)
    other = swap(cached, axis, whole[-1])
    attended_own = finish(cached, other, query_own, kv_own, ancestors, scale)
    attended = gathered(attended_own).reshape(requests * tree_size, width)
    mixed = jnp.dot(attended, w_out, preferred_element_type=jnp.float32)
    mixed = jnp.take(mixed.reshape(requests, tree_size, -1), reqs, axis=0)
    mixed = mixed.reshape(requests * tree_size, -1)
    head_bit = lax.axis_size("heads") // 2
    while head_bit:
        high = (lax.axis_index("heads") & head_bit) > 0
        half = mixed.shape[0] // 2
        keep = jnp.where(high, mixed[half:], mixed[:half])
        send = jnp.where(high, mixed[:half], mixed[half:])
        mixed = keep + swap(send, "heads", head_bit)
        head_bit //= 2
    mixed = mixed.astype(jnp.bfloat16)

    fresh = jnp.take(gathered(kv_own), reqs, axis=0)
    tiles = block_len // tree_size
    first = lax.div(starts + block_len * block_count, jnp.int32(tree_size)) - tiles * block_count
    firsts = jnp.clip(first[:, None] + jnp.arange(2, dtype=jnp.int32)[None, :], 0, tiles - 1)
    key_out, value_out = patch(
        fresh, reqs, selector.astype(jnp.bfloat16), firsts, starts, cache_key, cache_value
    )
    return (mixed, key_out, value_out)


def solution(mesh):
    return jax.shard_map(
        on_device,
        mesh=mesh,
        in_specs=(
            P(None, "blocks"),
            P("blocks", "heads"),
            P("blocks", "heads"),
            P("blocks", "heads"),
            P("heads", "blocks"),
            P(None, "blocks", "heads"),
            P(None, "blocks", "heads"),
            P(),
            P(),
            P(),
            P(),
        ),
        out_specs=(P("heads", "blocks"), P(None, "blocks", "heads"), P(None, "blocks", "heads")),
        check_vma=False,
    )
```

time: 341 us -> 134 us (0.39)
  waiting for transfers between devices: 143 us -> 27.6 us
  other arithmetic: 66.6 us -> 12.2 us
  blocking collectives: 45.5 us -> 0 us
  Pallas kernels: 0 us -> 45.2 us
  matrix products: 33.7 us -> 3.21 us
  starting transfers between devices: 0.12 us -> 20.2 us
  between operations: 14 us -> 0.98 us
  local copies, waits for them, and re-layouts: 34.8 us -> 23.7 us
    psum x1 -> x0, waiting for transfers between devices: 74.1 us -> none  [on_device(): lax.psum(jnp.dot(hidden, joined, preferred_element_type=jnp.float32), 'bl...]
    all_gather x1 -> x0, waiting for transfers between devices: 69.1 us -> none  [joined_2(): gathered = jax.tree.map(lambda a: lax.all_gather(a, axis), part)]
    all_gather x2 -> x0, blocking collectives: 45.5 us -> none  [joined_2(): gathered = jax.tree.map(lambda a: lax.all_gather(a, axis), part)]
    pallas_call x0 -> x12, Pallas kernels: none -> 45.2 us  [the longest x4 24.4 us: cache_attention(): pl.pallas_call(functools.partial(cache_kernel, slot, heads, scale), grid_...]
    add x31 -> x4, other arithmetic: 40.9 us -> 0.13 us  [the longest x2 0.09 us: scattered(): value = value[:half] + swap(value[half:], axis, bit)]
    dot_general x7 -> x3, matrix products: 31.6 us -> 1.55 us  [the longest x1 1.05 us: on_device(): mixed = jnp.dot(attended, w_out, preferred_element_type=jnp.float32)]
    ppermute x0 -> x19, waiting for transfers between devices: none -> 27.6 us  [swap(): return lax.ppermute(value, axis, [(i, i ^ bit) for i in range(size)])]
    ppermute x0 -> x19, starting transfers between devices: none -> 20.2 us  [swap(): return lax.ppermute(value, axis, [(i, i ^ bit) for i in range(size)])]
  transfers between devices with their start and end apart: 3 -> 19, of which waited for: 2 -> 11; matrix products, arithmetic and copies ran while one was open for 18% -> 13% of each run, Pallas kernels for 0% -> 34%
where the time goes in v1:
time: 134 us; the launch traced here: 133 us
  Pallas kernels  45.2 us (34%)
  waiting for transfers between devices  27.6 us (21%)
  local copies, waits for them, and re-layouts  23.7 us (18%)
  starting transfers between devices  20.2 us (15%)
  other arithmetic  12.2 us (9%)
  matrix products  3.21 us (2%)
    ppermute x19, waiting for transfers between devices, swap(): return lax.ppermute(value, axis, [(i, i ^ bit) for i in range(size)])  27.6 us
    pallas_call x4, Pallas kernels, cache_attention(): pl.pallas_call(functools.partial(cache_kernel, slot, heads, scale), grid_...  24.4 us
    ppermute x19, starting transfers between devices, swap(): return lax.ppermute(value, axis, [(i, i ^ bit) for i in range(size)])  20.2 us
    unnamed x44, local copies, waits for them, and re-layouts  19 us
    pallas_call x4, Pallas kernels, merge(): pl.pallas_call(functools.partial(merge_kernel, width), out_shape=jax.Shap...  7.63 us
    pallas_call x1, Pallas kernels, patch(): pl.pallas_call(patch_kernel, grid_spec=pltpu.PrefetchScalarGridSpec(num_s...  6.77 us
    concatenate x4, other arithmetic, gathered(): value = jnp.concatenate([value, swap(value, axis, bit)], axis=0)  3.62 us
    pallas_call x2, Pallas kernels, add_rotate(): pl.pallas_call(functools.partial(add_rotate_kernel, rotated_width), out_s...  3.54 us
  transfers between devices with their start and end apart: 19, of which 11 were waited for; matrix products, arithmetic and copies ran while one was open for 13% of the time, Pallas kernels for 34%

profile of v1, /device:TPU:0, one launch (start us, length us, event | category | flops | bytes accessed | tf_op | source)
XLA Modules:
  0.0 133.0 jit_solution(6438147931900468574)
XLA Ops:
  0.6 7.8 %copy.22.k_ref.key_ref = bf16[4,1024,1024]{2,1,0:T(8,128)(2,1)} copy(bf16[4,1024,1024]{2,1,0:T(8,128)(2,1)} %param.16) | data formatting | bytes 16777216
  8.5 7.8 %copy.23.v_ref.value_ref = bf16[4,1024,1024]{2,1,0:T(8,128)(2,1)} copy(bf16[4,1024,1024]{2,1,0:T(8,128)(2,1)} %param.17) | data formatting | bytes 16777216
  16.5 0.6 gather_fusion
  17.4 0.5 collective-permute-start
  18.4 0.7 dynamic-slice_bitcast_fusion
  19.9 0.9 fusion.37
  20.8 0.6 dynamic_slice.8
  21.5 0.6 add_convert_fusion
  22.2 3.0 %collective-permute-start.1 = (f32[1,32,1024]{2,1,0:T(8,128)S(1)}, f32[1,32,1024]{2,1,0:T(8,128)S(1)}, u32[]{:S(2)}, u32[]{:S(2)}) collective-permute-start(f32[1,32,1024]{2,1,0:T(8,128)S(1)} %slice.85), channel_id=1, source_target_pairs={{0,2},{1,3},{2,0},{3,1},{4,6},{5,7},{6,4},{7,5},{8,10},{9,11},{10,... | collective-permute-start | bytes 393224 | tf_op jit(solution)/shard_map/ppermute | solution.py:22
  25.2 3.7 %collective-permute-done.1 = f32[1,32,1024]{2,1,0:T(8,128)S(1)} collective-permute-done((f32[1,32,1024]{2,1,0:T(8,128)S(1)}, f32[1,32,1024]{2,1,0:T(8,128)S(1)}, u32[]{:S(2)}, u32[]{:S(2)}) %collective-permute-start.1) | collective-permute-done | bytes 131104 | tf_op jit(solution)/shard_map/ppermute | solution.py:22
  28.9 1.9 %collective-permute-start.2 = (f32[32,1024]{1,0:T(8,128)S(1)}, f32[32,1024]{1,0:T(8,128)S(1)}, u32[]{:S(2)}, u32[]{:S(2)}) collective-permute-start(f32[32,1024]{1,0:T(8,128)S(1)} %fusion.12), channel_id=1, source_target_pairs={{0,4},{1,5},{2,6},{3,7},{4,0},{5,1},{6,2},{7,3},{8,12},{9,13},{10,... | collective-permute-start | bytes 393224 | tf_op jit(solution)/shard_map/ppermute | solution.py:22
  30.9 3.0 %collective-permute-done.2 = f32[32,1024]{1,0:T(8,128)S(1)} collective-permute-done((f32[32,1024]{1,0:T(8,128)S(1)}, f32[32,1024]{1,0:T(8,128)S(1)}, u32[]{:S(2)}, u32[]{:S(2)}) %collective-permute-start.2) | collective-permute-done | bytes 131104 | tf_op jit(solution)/shard_map/ppermute | solution.py:22
  33.9 2.9 %collective-permute-start.3 = (f32[32,1024]{1,0:T(8,128)S(1)}, f32[32,1024]{1,0:T(8,128)S(1)}, u32[]{:S(2)}, u32[]{:S(2)}) collective-permute-start(f32[32,1024]{1,0:T(8,128)S(1)} %add.113.one_ref), channel_id=1, source_target_pairs={{0,8},{1,9},{2,10},{3,11},{4,12},{5,13},{6,14},{7,15},{8,0},{9,1},... | collective-permute-start | bytes 393224 | tf_op jit(solution)/shard_map/ppermute | solution.py:22
  37.0 0.6 pad_maximum_fusion.6.tables_ref
  37.6 3.9 %collective-permute-done.3.two_ref = f32[32,1024]{1,0:T(8,128)S(1)} collective-permute-done((f32[32,1024]{1,0:T(8,128)S(1)}, f32[32,1024]{1,0:T(8,128)S(1)}, u32[]{:S(2)}, u32[]{:S(2)}) %collective-permute-start.3) | collective-permute-done | bytes 131104 | tf_op jit(solution)/shard_map/ppermute | solution.py:22
  41.5 0.7 copy-done.10
  42.1 1.7 %add_rotate.2.q_ref = bf16[32,1024]{1,0:T(8,128)(2,1)} custom-call(f32[32,1024]{1,0:T(8,128)} %copy-done.2, f32[32,1024]{1,0:T(8,128)} %copy-done.10, f32[3,32,128]{2,1,0:T(8,128)} %pad_maximum_fusion.6.tables_ref), custom_call_target="tpu_custom_call" | custom-call | tf_op jit(solution)/shard_map/add_rotate/pallas_call | solution.py:65
  43.9 1.5 %collective-permute-start.4 = (bf16[1,32,1024]{2,1,0:T(8,128)(2,1)}, bf16[1,32,1024]{2,1,0:T(8,128)(2,1)S(1)}, u32[]{:S(2)}, u32[]{:S(2)}) collective-permute-start(bf16[1,32,1024]{2,1,0:T(8,128)(2,1)} %bitcast.49), channel_id=1, source_target_pairs={{0,2},{1,3},{2,0},{3,1},{4,6},{5,7},{6,4},{7,5},{8,10},{9,11},{10,... | collective-permute-start | bytes 196616 | tf_op jit(solution)/shard_map/ppermute | solution.py:22
  45.4 2.9 %collective-permute-done.4 = bf16[1,32,1024]{2,1,0:T(8,128)(2,1)S(1)} collective-permute-done((bf16[1,32,1024]{2,1,0:T(8,128)(2,1)}, bf16[1,32,1024]{2,1,0:T(8,128)(2,1)S(1)}, u32[]{:S(2)}, u32[]{:S(2)}) %collective-permute-start.4) | collective-permute-done | bytes 65568 | tf_op jit(solution)/shard_map/ppermute | solution.py:22
  48.3 0.9 pad_maximum_fusion.4
  49.3 0.6 iota_xor_fusion
  50.0 1.6 %collective-permute-start.11 = (f32[1,32,2048]{2,1,0:T(8,128)S(1)}, f32[1,32,2048]{2,1,0:T(8,128)S(1)}, u32[]{:S(2)}, u32[]{:S(2)}) collective-permute-start(f32[1,32,2048]{2,1,0:T(8,128)S(1)} %slice.93), channel_id=1, source_target_pairs={{0,2},{1,3},{2,0},{3,1},{4,6},{5,7},{6,4},{7,5},{8,10},{9,11},{10,... | collective-permute-start | bytes 786440 | tf_op jit(solution)/shard_map/ppermute | solution.py:22
  51.6 6.0 %cache_attention.4 = (f32[32,1024]{1,0:T(8,128)}, f32[32,128]{1,0:T(8,128)}) custom-call(s32[4]{0:T(128)} %get-tuple-element.42.reqs, s32[4]{0:T(128)} %get-tuple-element.43.live, bf16[32,1024]{1,0:T(8,128)(2,1)} %add_rotate.2.q_ref, bf16[4,1024,1024]{2,1,0:T(8,128)(2,1)} %copy.22.k_ref.key_ref, bf16[4,1024,1024]{2,1,0:T(8,128)(2,1)} %copy.23.v_ref.value_ref), custom_call_target="tpu_custom_call" | custom-call | flops 536870912 | bytes 4194304 | tf_op jit(solution)/shard_map/cache_attention/pallas_call | solution.py:126
  57.6 0.7 slice_bitcast_fusion.1
  58.3 6.0 %cache_attention.6 = (f32[32,1024]{1,0:T(8,128)}, f32[32,128]{1,0:T(8,128)}) custom-call(s32[4]{0:T(128)} %get-tuple-element.42.reqs, s32[4]{0:T(128)} %get-tuple-element.43.live, bf16[32,1024]{1,0:T(8,128)(2,1)} %get-tuple-element.32.q_ref, bf16[4,1024,1024]{2,1,0:T(8,128)(2,1)} %copy.22.k_ref.key_ref, bf16[4,1024,1024]{2,1,0:T(8,128)(2,1)} %copy.23.v_ref.value_ref), custom_call_target="tpu_custom_call" | custom-call | flops 536870912 | bytes 4194304 | tf_op jit(solution)/shard_map/cache_attention/pallas_call | solution.py:126
  64.3 6.2 %cache_attention.5 = (f32[32,1024]{1,0:T(8,128)}, f32[32,128]{1,0:T(8,128)}) custom-call(s32[4]{0:T(128)} %get-tuple-element.42.reqs, s32[4]{0:T(128)} %get-tuple-element.43.live, bf16[32,1024]{1,0:T(8,128)(2,1)} %get-tuple-element.31.q_ref, bf16[4,1024,1024]{2,1,0:T(8,128)(2,1)} %copy.22.k_ref.key_ref, bf16[4,1024,1024]{2,1,0:T(8,128)(2,1)} %copy.23.v_ref.value_ref), custom_call_target="tpu_custom_call" | custom-call | flops 536870912 | bytes 4194304 | tf_op jit(solution)/shard_map/cache_attention/pallas_call | solution.py:126
  70.5 0.9 maximum_maximum_fusion
  71.8 0.7 collective-permute-start.12
  72.5 6.2 %cache_attention.7 = (f32[32,1024]{1,0:T(8,128)}, f32[32,128]{1,0:T(8,128)}) custom-call(s32[4]{0:T(128)} %get-tuple-element.42.reqs, s32[4]{0:T(128)} %get-tuple-element.43.live, bf16[32,1024]{1,0:T(8,128)(2,1)} %bitcast.53, bf16[4,1024,1024]{2,1,0:T(8,128)(2,1)} %copy.22.k_ref.key_ref, bf16[4,1024,1024]{2,1,0:T(8,128)(2,1)} %copy.23.v_ref.value_ref), custom_call_target="tpu_custom_call" | custom-call | flops 536870912 | bytes 4194304 | tf_op jit(solution)/shard_map/cache_attention/pallas_call | solution.py:126
  78.6 1.6 %pad_maximum_fusion.3.one_ref = f32[32,1152]{1,0:T(8,128)} fusion(f32[32,128]{1,0:T(8,128)} %get-tuple-element.20, f32[32,1024]{1,0:T(8,128)} %get-tuple-element.19), kind=kLoop, calls=%fused_computation.27 | loop fusion | flops 36864 | bytes 294912 | tf_op jit(solution)/shard_map/concatenate | solution.py:348
  80.4 3.4 %collective-permute-start.13 = (f32[32,2048]{1,0:T(8,128)S(1)}, f32[32,2048]{1,0:T(8,128)S(1)}, u32[]{:S(2)}, u32[]{:S(2)}) collective-permute-start(f32[32,2048]{1,0:T(8,128)S(1)} %add.122.one_ref), channel_id=1, source_target_pairs={{0,8},{1,9},{2,10},{3,11},{4,12},{5,13},{6,14},{7,15},{8,0},{9,1},... | collective-permute-start | bytes 786440 | tf_op jit(solution)/shard_map/ppermute | solution.py:22
  83.8 0.7 fusion.36
  84.5 1.9 %merge.5 = f32[32,1152]{1,0:T(8,128)} custom-call(f32[32,1152]{1,0:T(8,128)} %pad_maximum_fusion.3.one_ref, f32[32,1152]{1,0:T(8,128)} %get-tuple-element.29.two_ref), custom_call_target="tpu_custom_call" | custom-call | tf_op jit(solution)/shard_map/merge/pallas_call | solution.py:180
  86.4 0.5 collective-permute-start.7
  86.9 0.7 pad_maximum_fusion.2.one_ref
  87.6 1.9 %merge.4.one_ref = f32[32,1152]{1,0:T(8,128)} custom-call(f32[32,1152]{1,0:T(8,128)} %pad_maximum_fusion.2.one_ref, f32[32,1152]{1,0:T(8,128)} %get-tuple-element.30.two_ref), custom_call_target="tpu_custom_call" | custom-call | tf_op jit(solution)/shard_map/merge/pallas_call | solution.py:180
  89.5 2.6 %collective-permute-done.7.two_ref = f32[32,1152]{1,0:T(8,128)S(1)} collective-permute-done((f32[32,1152]{1,0:T(8,128)}, f32[32,1152]{1,0:T(8,128)S(1)}, u32[]{:S(2)}, u32[]{:S(2)}) %collective-permute-start.7) | collective-permute-done | bytes 147488 | tf_op jit(solution)/shard_map/ppermute | solution.py:22
  92.1 0.7 copy-done.9
  92.7 1.9 %merge.6.one_ref = f32[32,1152]{1,0:T(8,128)} custom-call(f32[32,1152]{1,0:T(8,128)} %merge.4.one_ref, f32[32,1152]{1,0:T(8,128)} %copy-done.9), custom_call_target="tpu_custom_call" | custom-call | tf_op jit(solution)/shard_map/merge/pallas_call | solution.py:180
  95.0 0.8 collective-permute-done.13.two_ref
  95.8 0.7 copy-done.6
  96.6 1.8 %add_rotate.3.kv_ref = bf16[32,2048]{1,0:T(8,128)(2,1)} custom-call(f32[32,2048]{1,0:T(8,128)} %copy-done.1, f32[32,2048]{1,0:T(8,128)} %copy-done.6, f32[3,32,128]{2,1,0:T(8,128)} %pad_maximum_fusion.6.tables_ref), custom_call_target="tpu_custom_call" | custom-call | tf_op jit(solution)/shard_map/add_rotate/pallas_call | solution.py:65
  98.4 0.5 collective-permute-start.17
  98.9 1.1 collective-permute-done.8.two_ref
  100.0 0.7 copy-done.7
  100.7 1.9 %merge.7.one_ref = f32[32,1152]{1,0:T(8,128)} custom-call(f32[32,1152]{1,0:T(8,128)} %merge.6.one_ref, f32[32,1152]{1,0:T(8,128)} %copy-done.7), custom_call_target="tpu_custom_call" | custom-call | tf_op jit(solution)/shard_map/merge/pallas_call | solution.py:180
  102.9 1.1 collective-permute-done.17
  103.9 0.9 pad_maximum_fusion.1
  105.0 5.9 %collective-permute-done.9.two_ref = f32[32,1152]{1,0:T(8,128)S(1)} collective-permute-done((f32[32,1152]{1,0:T(8,128)}, f32[32,1152]{1,0:T(8,128)S(1)}, u32[]{:S(2)}, u32[]{:S(2)}) %collective-permute-start.9) | collective-permute-done | bytes 147488 | tf_op jit(solution)/shard_map/ppermute | solution.py:22
  110.9 0.7 copy-done.8
  111.5 2.9 %finish.1 = bf16[32,1024]{1,0:T(8,128)(2,1)} custom-call(f32[32,1152]{1,0:T(8,128)} %merge.7.one_ref, f32[32,1152]{1,0:T(8,128)} %copy-done.8, bf16[32,1024]{1,0:T(8,128)(2,1)} %add_rotate.2.q_ref, bf16[32,2048]{1,0:T(8,128)(2,1)} %add_rotate.3.kv_ref, f32[32,32]{1,0:T(8,128)} %get-tuple-element.39.tree_ref), custom_call_target="tpu_custom_call" | custom-call | tf_op jit(solution)/shard_map/finish/pallas_call | solution.py:230
  114.4 0.7 collective-permute-start.14
  115.1 0.6 add_clamp_fusion.firsts
  115.8 0.6 convert_element_type.40.sel_ref
  116.4 2.5 %collective-permute-done.14 = bf16[1,32,1024]{2,1,0:T(8,128)(2,1)S(1)} collective-permute-done((bf16[1,32,1024]{2,1,0:T(8,128)(2,1)}, bf16[1,32,1024]{2,1,0:T(8,128)(2,1)S(1)}, u32[]{:S(2)}, u32[]{:S(2)}) %collective-permute-start.14) | collective-permute-done | bytes 65568 | tf_op jit(solution)/shard_map/ppermute | solution.py:22
  118.9 0.9 pad_maximum_fusion.5
  119.9 1.0 pad_maximum_fusion
  120.8 0.6 gather_fusion.2
  121.4 1.1 fusion.5
  122.5 0.6 gather_fusion.1
  123.1 1.6 %collective-permute-start.16 = (f32[64,128]{1,0:T(8,128)S(1)}, f32[64,128]{1,0:T(8,128)S(1)}, u32[]{:S(2)}, u32[]{:S(2)}) collective-permute-start(f32[64,128]{1,0:T(8,128)S(1)} %bitcast.59), channel_id=1, source_target_pairs={{0,16},{16,0},{1,17},{17,1},{2,18},{18,2},{3,19},{19,3},{4,20},{20... | collective-permute-start | bytes 98312 | tf_op jit(solution)/shard_map/ppermute | solution.py:22
  124.7 0.9 broadcast_select_fusion.kv_ref
  125.7 6.8 %patch.1 = (bf16[4,1024,1024]{2,1,0:T(8,128)(2,1)}, bf16[4,1024,1024]{2,1,0:T(8,128)(2,1)}) custom-call(s32[4,2]{1,0:T(4,128)} %add_clamp_fusion.firsts, s32[4]{0:T(128)} %copy-done.17, bf16[4,32,2048]{2,1,0:T(8,128)(2,1)} %broadcast_select_fusion.kv_ref, ...), custom_call_target="tpu_custom_call", output_to_operand_aliasing={{0}: (4, {}), {1}: (5, {})} | custom-call | bytes 2097152 | tf_op jit(solution)/shard_map/patch/pallas_call | solution.py:261
  132.4 0.6 fusion.13
  (85 shorter events, 3.7 us)
Async XLA Ops:
  0.6 16.5 %copy-start = (bf16[128,1024]{1,0:T(8,128)(2,1)S(1)}, bf16[128,1024]{1,0:T(8,128)(2,1)}, u32[]{:S(2)}) copy-start(bf16[128,1024]{1,0:T(8,128)(2,1)} %param.12) | copy-start | bytes 786436
  8.4 8.0 %copy-start.14 = (bf16[128,128]{1,0:T(8,128)(2,1)S(1)}, bf16[128,128]{1,0:T(8,128)(2,1)}, u32[]{:S(2)}) copy-start(bf16[128,128]{1,0:T(8,128)(2,1)} %param.11) | copy-start | bytes 98308
  8.4 9.5 %copy-start.4 = (bf16[128,1024]{1,0:T(8,128)(2,1)S(1)}, bf16[128,1024]{1,0:T(8,128)(2,1)}, u32[]{:S(2)}) copy-start(bf16[128,1024]{1,0:T(8,128)(2,1)} %param.14) | copy-start | bytes 786436
  8.4 9.5 %copy-start.5 = (bf16[128,1024]{1,0:T(8,128)(2,1)S(1)}, bf16[128,1024]{1,0:T(8,128)(2,1)}, u32[]{:S(2)}) copy-start(bf16[128,1024]{1,0:T(8,128)(2,1)} %param.13) | copy-start | bytes 786436
  8.5 12.4 %copy-start.19 = (s32[4]{0:T(128)S(1)}, s32[4]{0:T(128)}, u32[]{:S(2)}) copy-start(s32[4]{0:T(128)} %param.19) | copy-start | bytes 52
  8.5 28.4 %copy-start.18 = (s32[4,16]{1,0:T(4,128)S(1)}, s32[4,16]{1,0:T(4,128)}, u32[]{:S(2)}) copy-start(s32[4,16]{1,0:T(4,128)} %param.20) | copy-start | bytes 772
  17.4 4.7 %collective-permute-start = (f32[2,32,1024]{2,1,0:T(8,128)S(1)}, f32[2,32,1024]{2,1,0:T(8,128)S(1)}, u32[]{:S(2)}, u32[]{:S(2)}) collective-permute-start(f32[2,32,1024]{2,1,0:T(8,128)S(1)} %bitcast.57), channel_id=1, source_target_pairs={{0,1},{1,0},{2,3},{3,2},{4,5},{5,4},{6,7},{7,6},{8,9},{9,8},{10,11... | collective-permute-start | bytes 786440 | tf_op jit(solution)/shard_map/ppermute | solution.py:22
  18.3 31.6 %collective-permute-start.10 = (f32[2,32,2048]{2,1,0:T(8,128)S(1)}, f32[2,32,2048]{2,1,0:T(8,128)S(1)}, u32[]{:S(2)}, u32[]{:S(2)}) collective-permute-start(f32[2,32,2048]{2,1,0:T(8,128)S(1)} %bitcast.52), channel_id=1, source_target_pairs={{0,1},{1,0},{2,3},{3,2},{4,5},{5,4},{6,7},{7,6},{8,9},{9,8},{10,11... | collective-permute-start | bytes 1572872 | tf_op jit(solution)/shard_map/ppermute | solution.py:22
  22.2 6.7 %collective-permute-start.1 = (f32[1,32,1024]{2,1,0:T(8,128)S(1)}, f32[1,32,1024]{2,1,0:T(8,128)S(1)}, u32[]{:S(2)}, u32[]{:S(2)}) collective-permute-start(f32[1,32,1024]{2,1,0:T(8,128)S(1)} %slice.85), channel_id=1, source_target_pairs={{0,2},{1,3},{2,0},{3,1},{4,6},{5,7},{6,4},{7,5},{8,10},{9,11},{10,... | collective-permute-start | bytes 393224 | tf_op jit(solution)/shard_map/ppermute | solution.py:22
  28.9 5.0 %collective-permute-start.2 = (f32[32,1024]{1,0:T(8,128)S(1)}, f32[32,1024]{1,0:T(8,128)S(1)}, u32[]{:S(2)}, u32[]{:S(2)}) collective-permute-start(f32[32,1024]{1,0:T(8,128)S(1)} %fusion.12), channel_id=1, source_target_pairs={{0,4},{1,5},{2,6},{3,7},{4,0},{5,1},{6,2},{7,3},{8,12},{9,13},{10,... | collective-permute-start | bytes 393224 | tf_op jit(solution)/shard_map/ppermute | solution.py:22
  33.9 7.5 %copy-start.2 = (f32[32,1024]{1,0:T(8,128)}, f32[32,1024]{1,0:T(8,128)S(1)}, u32[]{:S(2)}) copy-start(f32[32,1024]{1,0:T(8,128)S(1)} %add.113.one_ref) | copy-start | bytes 393220
  33.9 7.5 %collective-permute-start.3 = (f32[32,1024]{1,0:T(8,128)S(1)}, f32[32,1024]{1,0:T(8,128)S(1)}, u32[]{:S(2)}, u32[]{:S(2)}) collective-permute-start(f32[32,1024]{1,0:T(8,128)S(1)} %add.113.one_ref), channel_id=1, source_target_pairs={{0,8},{1,9},{2,10},{3,11},{4,12},{5,13},{6,14},{7,15},{8,0},{9,1},... | collective-permute-start | bytes 393224 | tf_op jit(solution)/shard_map/ppermute | solution.py:22
  41.5 0.7 copy-start.10
  43.9 4.5 %collective-permute-start.4 = (bf16[1,32,1024]{2,1,0:T(8,128)(2,1)}, bf16[1,32,1024]{2,1,0:T(8,128)(2,1)S(1)}, u32[]{:S(2)}, u32[]{:S(2)}) collective-permute-start(bf16[1,32,1024]{2,1,0:T(8,128)(2,1)} %bitcast.49), channel_id=1, source_target_pairs={{0,2},{1,3},{2,0},{3,1},{4,6},{5,7},{6,4},{7,5},{8,10},{9,11},{10,... | collective-permute-start | bytes 196616 | tf_op jit(solution)/shard_map/ppermute | solution.py:22
  45.4 12.2 %copy-start.17 = (s32[4]{0:T(128)}, s32[4]{0:T(128)S(1)}, u32[]{:S(2)}) copy-start(s32[4]{0:T(128)S(1)} %get-tuple-element.24.starts) | copy-start | bytes 52
  48.3 9.3 %copy-start.3 = (bf16[1,32,1024]{2,1,0:T(8,128)(2,1)}, bf16[1,32,1024]{2,1,0:T(8,128)(2,1)S(1)}, u32[]{:S(2)}) copy-start(bf16[1,32,1024]{2,1,0:T(8,128)(2,1)S(1)} %collective-permute-done.4) | copy-start | bytes 196612
  49.2 8.4 %collective-permute-start.5 = (bf16[2,32,1024]{2,1,0:T(8,128)(2,1)S(1)}, bf16[2,32,1024]{2,1,0:T(8,128)(2,1)S(1)}, u32[]{:S(2)}, u32[]{:S(2)}) collective-permute-start(bf16[2,32,1024]{2,1,0:T(8,128)(2,1)S(1)} %pad_maximum_fusion.4), channel_id=1, source_target_pairs={{0,1},{1,0},{2,3},{3,2},{4,5},{5,4},{6,7},{7,6},{8,9},{9,8},{10,11... | collective-permute-start | bytes 393224 | tf_op jit(solution)/shard_map/ppermute | solution.py:22
  50.0 21.7 %collective-permute-start.11 = (f32[1,32,2048]{2,1,0:T(8,128)S(1)}, f32[1,32,2048]{2,1,0:T(8,128)S(1)}, u32[]{:S(2)}, u32[]{:S(2)}) collective-permute-start(f32[1,32,2048]{2,1,0:T(8,128)S(1)} %slice.93), channel_id=1, source_target_pairs={{0,2},{1,3},{2,0},{3,1},{4,6},{5,7},{6,4},{7,5},{8,10},{9,11},{10,... | collective-permute-start | bytes 786440 | tf_op jit(solution)/shard_map/ppermute | solution.py:22
  64.3 6.2 %copy-start.12 = (f32[32,1024]{1,0:T(8,128)S(1)}, f32[32,1024]{1,0:T(8,128)}, u32[]{:S(2)}) copy-start(f32[32,1024]{1,0:T(8,128)} %get-tuple-element.17) | copy-start | bytes 393220
  64.3 6.2 %copy-start.16 = (f32[32,128]{1,0:T(8,128)S(1)}, f32[32,128]{1,0:T(8,128)}, u32[]{:S(2)}) copy-start(f32[32,128]{1,0:T(8,128)} %get-tuple-element.18) | copy-start | bytes 49156
  71.4 12.3 %collective-permute-start.6 = (f32[64,1152]{1,0:T(8,128)S(1)}, f32[64,1152]{1,0:T(8,128)S(1)}, u32[]{:S(2)}, u32[]{:S(2)}) collective-permute-start(f32[64,1152]{1,0:T(8,128)S(1)} %maximum_maximum_fusion), channel_id=1, source_target_pairs={{0,1},{1,0},{2,3},{3,2},{4,5},{5,4},{6,7},{7,6},{8,9},{9,8},{10,11... | collective-permute-start | bytes 884744 | tf_op jit(solution)/shard_map/ppermute | solution.py:22
  71.8 8.6 %collective-permute-start.12 = (f32[32,2048]{1,0:T(8,128)S(1)}, f32[32,2048]{1,0:T(8,128)S(1)}, u32[]{:S(2)}, u32[]{:S(2)}) collective-permute-start(f32[32,2048]{1,0:T(8,128)S(1)} %fusion.4), channel_id=1, source_target_pairs={{0,4},{1,5},{2,6},{3,7},{4,0},{5,1},{6,2},{7,3},{8,12},{9,13},{10,... | collective-permute-start | bytes 786440 | tf_op jit(solution)/shard_map/ppermute | solution.py:22
  72.5 14.4 %copy-start.11 = (f32[32,1024]{1,0:T(8,128)S(1)}, f32[32,1024]{1,0:T(8,128)}, u32[]{:S(2)}) copy-start(f32[32,1024]{1,0:T(8,128)} %get-tuple-element.13) | copy-start | bytes 393220
  72.5 14.4 %copy-start.15 = (f32[32,128]{1,0:T(8,128)S(1)}, f32[32,128]{1,0:T(8,128)}, u32[]{:S(2)}) copy-start(f32[32,128]{1,0:T(8,128)} %get-tuple-element.14) | copy-start | bytes 49156
  72.5 43.3 %copy-start.13 = (s32[4,32,32]{2,1,0:T(8,128)S(1)}, s32[4,32,32]{2,1,0:T(8,128)}, u32[]{:S(2)}) copy-start(s32[4,32,32]{2,1,0:T(8,128)} %param.21) | copy-start | bytes 49156
  72.5 48.9 %copy-start.20 = (bf16[1024,128]{1,0:T(8,128)(2,1)S(1)}, bf16[1024,128]{1,0:T(8,128)(2,1)}, u32[]{:S(2)}) copy-start(bf16[1024,128]{1,0:T(8,128)(2,1)} %param.15) | copy-start | bytes 786436
  80.4 15.5 %copy-start.1 = (f32[32,2048]{1,0:T(8,128)}, f32[32,2048]{1,0:T(8,128)S(1)}, u32[]{:S(2)}) copy-start(f32[32,2048]{1,0:T(8,128)S(1)} %add.122.one_ref) | copy-start | bytes 786436
  80.4 15.5 %collective-permute-start.13 = (f32[32,2048]{1,0:T(8,128)S(1)}, f32[32,2048]{1,0:T(8,128)S(1)}, u32[]{:S(2)}, u32[]{:S(2)}) collective-permute-start(f32[32,2048]{1,0:T(8,128)S(1)} %add.122.one_ref), channel_id=1, source_target_pairs={{0,8},{1,9},{2,10},{3,11},{4,12},{5,13},{6,14},{7,15},{8,0},{9,1},... | collective-permute-start | bytes 786440 | tf_op jit(solution)/shard_map/ppermute | solution.py:22
  86.4 5.7 %collective-permute-start.7 = (f32[32,1152]{1,0:T(8,128)}, f32[32,1152]{1,0:T(8,128)S(1)}, u32[]{:S(2)}, u32[]{:S(2)}) collective-permute-start(f32[32,1152]{1,0:T(8,128)} %merge.5), channel_id=1, source_target_pairs={{0,2},{1,3},{2,0},{3,1},{4,6},{5,7},{6,4},{7,5},{8,10},{9,11},{10,... | collective-permute-start | bytes 442376 | tf_op jit(solution)/shard_map/ppermute | solution.py:22
  92.1 0.7 copy-start.9
  94.6 5.4 %collective-permute-start.8 = (f32[32,1152]{1,0:T(8,128)}, f32[32,1152]{1,0:T(8,128)S(1)}, u32[]{:S(2)}, u32[]{:S(2)}) collective-permute-start(f32[32,1152]{1,0:T(8,128)} %merge.6.one_ref), channel_id=1, source_target_pairs={{0,4},{1,5},{2,6},{3,7},{4,0},{5,1},{6,2},{7,3},{8,12},{9,13},{10,... | collective-permute-start | bytes 442376 | tf_op jit(solution)/shard_map/ppermute | solution.py:22
  95.8 0.7 copy-start.6
  98.4 5.6 %collective-permute-start.17 = (bf16[1,32,2048]{2,1,0:T(8,128)(2,1)}, bf16[1,32,2048]{2,1,0:T(8,128)(2,1)S(1)}, u32[]{:S(2)}, u32[]{:S(2)}) collective-permute-start(bf16[1,32,2048]{2,1,0:T(8,128)(2,1)} %bitcast.46), channel_id=1, source_target_pairs={{0,2},{1,3},{2,0},{3,1},{4,6},{5,7},{6,4},{7,5},{8,10},{9,11},{10,... | collective-permute-start | bytes 393224 | tf_op jit(solution)/shard_map/ppermute | solution.py:22
  100.0 0.7 copy-start.7
  102.6 8.3 %collective-permute-start.9 = (f32[32,1152]{1,0:T(8,128)}, f32[32,1152]{1,0:T(8,128)S(1)}, u32[]{:S(2)}, u32[]{:S(2)}) collective-permute-start(f32[32,1152]{1,0:T(8,128)} %merge.7.one_ref), channel_id=1, source_target_pairs={{0,8},{1,9},{2,10},{3,11},{4,12},{5,13},{6,14},{7,15},{8,0},{9,1},... | collective-permute-start | bytes 442376 | tf_op jit(solution)/shard_map/ppermute | solution.py:22
  104.9 15.0 %collective-permute-start.18 = (bf16[2,32,2048]{2,1,0:T(8,128)(2,1)S(1)}, bf16[2,32,2048]{2,1,0:T(8,128)(2,1)S(1)}, u32[]{:S(2)}, u32[]{:S(2)}) collective-permute-start(bf16[2,32,2048]{2,1,0:T(8,128)(2,1)S(1)} %pad_maximum_fusion.1), channel_id=1, source_target_pairs={{0,1},{1,0},{2,3},{3,2},{4,5},{5,4},{6,7},{7,6},{8,9},{9,8},{10,11... | collective-permute-start | bytes 786440 | tf_op jit(solution)/shard_map/ppermute | solution.py:22
  110.9 0.7 copy-start.8
  114.4 4.5 %collective-permute-start.14 = (bf16[1,32,1024]{2,1,0:T(8,128)(2,1)}, bf16[1,32,1024]{2,1,0:T(8,128)(2,1)S(1)}, u32[]{:S(2)}, u32[]{:S(2)}) collective-permute-start(bf16[1,32,1024]{2,1,0:T(8,128)(2,1)} %bitcast.54), channel_id=1, source_target_pairs={{0,2},{1,3},{2,0},{3,1},{4,6},{5,7},{6,4},{7,5},{8,10},{9,11},{10,... | collective-permute-start | bytes 196616 | tf_op jit(solution)/shard_map/ppermute | solution.py:22
  119.8 1.6 %collective-permute-start.15 = (bf16[2,32,1024]{2,1,0:T(8,128)(2,1)S(1)}, bf16[2,32,1024]{2,1,0:T(8,128)(2,1)S(1)}, u32[]{:S(2)}, u32[]{:S(2)}) collective-permute-start(bf16[2,32,1024]{2,1,0:T(8,128)(2,1)S(1)} %pad_maximum_fusion.5), channel_id=1, source_target_pairs={{0,1},{1,0},{2,3},{3,2},{4,5},{5,4},{6,7},{7,6},{8,9},{9,8},{10,11... | collective-permute-start | bytes 393224 | tf_op jit(solution)/shard_map/ppermute | solution.py:22
  123.1 9.3 %collective-permute-start.16 = (f32[64,128]{1,0:T(8,128)S(1)}, f32[64,128]{1,0:T(8,128)S(1)}, u32[]{:S(2)}, u32[]{:S(2)}) collective-permute-start(f32[64,128]{1,0:T(8,128)S(1)} %bitcast.59), channel_id=1, source_target_pairs={{0,16},{16,0},{1,17},{17,1},{2,18},{18,2},{3,19},{19,3},{4,20},{20... | collective-permute-start | bytes 98312 | tf_op jit(solution)/shard_map/ppermute | solution.py:22

commit v2 on v0

v2 whole, which is shorter than its diff:
```python
import functools
import math

import jax
import jax.numpy as jnp
from jax import lax
from jax.experimental import pallas as pl
from jax.experimental.pallas import tpu as pltpu
from jax.sharding import PartitionSpec as P

HD = 64
ROT = 32
LANES = 128


masked_low = -1e30
rotary_base = 10000.0


def swap(value, axis, bit):
    size = lax.axis_size(axis)
    return lax.ppermute(value, axis, [(i, i ^ bit) for i in range(size)])


def ancestry(parents):
    tree_size = parents.shape[0]
    nodes = jnp.arange(tree_size, dtype=jnp.int32)
    parent_hop = ((parents[:, None] == nodes[None, :]) & (nodes[:, None] > 0)).astype(jnp.float32)
    reached = jnp.eye(tree_size, dtype=jnp.float32) + parent_hop
    for _ in range(tree_size.bit_length()):
        reached = jnp.minimum(jnp.dot(reached, reached, precision=lax.Precision.HIGHEST), 1.0)
    return reached


def rotary_tables(positions):
    column = jnp.arange(LANES, dtype=jnp.int32) % HD
    half = ROT // 2
    exponent = (column % half).astype(jnp.float32)
    inverse_freq = rotary_base ** (-2.0 * exponent / ROT)
    angles = positions.astype(jnp.float32)[:, None] * inverse_freq[None, :]
    cosine = jnp.where(column < ROT, jnp.cos(angles), 1.0)
    sine = jnp.sin(angles)
    ahead = jnp.where(column < half, -sine, 0.0)
    behind = jnp.where((column >= half) & (column < ROT), sine, 0.0)
    return jnp.stack([cosine, ahead, behind])


def rotate(value, tables):
    half = ROT // 2
    tables = jnp.tile(tables, (1, 1, value.shape[1] // LANES))
    ahead = jnp.roll(value, -half, axis=1)
    behind = jnp.roll(value, half, axis=1)
    return value * tables[0] + ahead * tables[1] + behind * tables[2]


def block_diagonal(queries, heads):
    tokens, width = queries.shape
    tall = jnp.concatenate([queries] * heads, axis=0)
    shape = (heads * tokens, width)
    row_head = lax.broadcasted_iota(jnp.int32, shape, 0) // tokens
    column_head = lax.broadcasted_iota(jnp.int32, shape, 1) // HD
    return jnp.where(row_head == column_head, tall, jnp.zeros_like(tall))


def diagonal_blocks(tall, heads, tokens):
    width = tall.shape[1]
    column_head = lax.broadcasted_iota(jnp.int32, (tokens, width), 1) // HD
    out = tall[:tokens]
    for head in range(1, heads):
        out = jnp.where(column_head == head, tall[head * tokens : (head + 1) * tokens], out)
    return out


def softmax_parts(queries, keys, values, bias, heads, scale):
    scores = lax.dot_general(
        queries * jnp.asarray(scale, queries.dtype),
        keys,
        (((1,), (1,)), ((), ())),
        preferred_element_type=jnp.float32,
    )
    scores = scores + bias
    top = jnp.max(scores, axis=1, keepdims=True)
    exponent = jnp.exp(scores - top)
    total = jnp.sum(exponent, axis=1, keepdims=True)
    out = jnp.dot(exponent.astype(jnp.bfloat16), values, preferred_element_type=jnp.float32)
    return top, total, out


def put_stats(stats, first_head, heads, tokens, top, total):
    lane = lax.broadcasted_iota(jnp.int32, stats.shape, 1)
    for head in range(heads):
        rows = slice(head * tokens, (head + 1) * tokens)
        stats = jnp.where(lane == first_head + head, top[rows], stats)
        stats = jnp.where(lane == first_head + head + HD, total[rows], stats)
    return stats


def cache_kernel(scale, reqs, live, *refs):
    slots = reqs.shape[0]
    q_refs = refs[:slots]
    key_ref, value_ref, keep_ref, send_ref, key_out, value_out, key_buf, value_buf, in_sem, out_sem = refs[
        slots:
    ]
    tokens, width = q_refs[0].shape
    block_len = key_ref.shape[1]
    group = min(256, width)
    heads = group // HD
    sources, buffers, targets = (key_ref, value_ref), (key_buf, value_buf), (key_out, value_out)

    def fetch(slot, which):
        return pltpu.make_async_copy(
            sources[which].at[reqs[slot]], buffers[which].at[slot], in_sem.at[slot, which]
        )

    def store(slot, which):
        return pltpu.make_async_copy(
            buffers[which].at[slot], targets[which].at[reqs[slot]], out_sem.at[slot, which]
        )

    order = list(reversed(range(slots)))
    for slot in order:
        for which in range(2):
            fetch(slot, which).start()
    half = slots // 2
    for slot in order:
        count = live[reqs[slot]]
        row = lax.broadcasted_iota(jnp.int32, (1, block_len), 1)
        bias = jnp.where(row < count, 0.0, masked_low)
        some = count > 0
        target = send_ref if slot >= half else keep_ref
        place = slot % half
        stats = jnp.zeros((tokens, LANES), jnp.float32)
        for start in range(0, width, group):
            columns = slice(start, start + group)
            queries = block_diagonal(q_refs[slot][:, columns], heads)
            if start == 0:
                fetch(slot, 0).wait()
            keys = key_buf[slot, :, columns]
            if start == 0:
                fetch(slot, 1).wait()
            top, total, out = softmax_parts(
                queries, keys, value_buf[slot, :, columns], bias, heads, scale
            )
            target[place, :, columns] = diagonal_blocks(out, heads, tokens)
            stats = put_stats(stats, start // HD, heads, tokens, top, total)
        target[place, :, width:] = stats
        for which in range(2):
            store(slot, which).start()
    for slot in order:
        for which in range(2):
            store(slot, which).wait()


def cache_attention(queries, cache_key, cache_value, reqs, live, scale):
    slots = len(queries)
    tokens, width = queries[0].shape
    block_len = cache_key.shape[1]
    vmem = pl.BlockSpec(memory_space=pltpu.VMEM)
    smem = pl.BlockSpec(memory_space=pltpu.SMEM)
    hbm = pl.BlockSpec(memory_space=pltpu.HBM)
    part = jax.ShapeDtypeStruct((slots // 2, tokens, width + LANES), jnp.float32)
    cache = jax.ShapeDtypeStruct(cache_key.shape, cache_key.dtype)
    return pl.pallas_call(
        functools.partial(cache_kernel, scale),
        in_specs=[smem, smem] + [vmem] * slots + [hbm, hbm],
        out_specs=[vmem, vmem, hbm, hbm],
        out_shape=[part, part, cache, cache],
        scratch_shapes=[
            pltpu.VMEM(cache_key.shape, cache_key.dtype),
            pltpu.VMEM(cache_key.shape, cache_key.dtype),
            pltpu.SemaphoreType.DMA((slots, 2)),
            pltpu.SemaphoreType.DMA((slots, 2)),
        ],
        compiler_params=pltpu.CompilerParams(vmem_limit_bytes=40 * 1024 * 1024),
        cost_estimate=pl.CostEstimate(
            flops=16 * slots * tokens * width * block_len,
            transcendentals=slots * tokens * (width // HD) * block_len,
            bytes_accessed=8 * slots * block_len * width,
        ),
        name="cache_attention",
    )(reqs, live, *queries, cache_key, cache_value)


def tree_kernel(scale, q_ref, kv_ref, tree_ref, out_ref):
    tokens, width = q_ref.shape
    group = min(256, width)
    heads = group // HD
    allowed = jnp.concatenate([tree_ref[...]] * heads, axis=0) > 0.5
    bias = jnp.where(allowed, 0.0, masked_low)
    stats = jnp.zeros((tokens, LANES), jnp.float32)
    for start in range(0, width, group):
        columns = slice(start, start + group)
        queries = block_diagonal(q_ref[:, columns], heads)
        values = kv_ref[:, width + start : width + start + group]
        top, total, out = softmax_parts(queries, kv_ref[:, columns], values, bias, heads, scale)
        out_ref[:, columns] = diagonal_blocks(out, heads, tokens)
        stats = put_stats(stats, start // HD, heads, tokens, top, total)
    out_ref[:, width:] = stats


def tree_attention(queries, key_value, tree, scale):
    tokens, width = queries.shape
    return pl.pallas_call(
        functools.partial(tree_kernel, scale),
        out_shape=jax.ShapeDtypeStruct((tokens, width + LANES), jnp.float32),
        cost_estimate=pl.CostEstimate(
            flops=16 * tokens * width * tokens, transcendentals=tokens * tokens, bytes_accessed=10**6
        ),
        name="tree_attention",
    )(queries, key_value, tree)


def merged(parts, width):
    heads = width // HD
    tops = [part[..., width : width + heads] for part in parts]
    totals = [part[..., width + HD : width + HD + heads] for part in parts]
    top = functools.reduce(jnp.maximum, tops)
    scales = [jnp.exp(one - top) for one in tops]
    total = sum(one * by for one, by in zip(totals, scales))

    def spread(value):
        wide = jnp.broadcast_to(value[..., None], value.shape + (HD,))
        return wide.reshape(value.shape[:-1] + (width,))

    out = sum(part[..., :width] * spread(by) for part, by in zip(parts, scales))
    return out, top, total, spread


def merge(one, two, width):
    out, top, total, _ = merged([one, two], width)
    gap = jnp.zeros(top.shape[:-1] + (HD - top.shape[-1],), jnp.float32)
    return jnp.concatenate([out, top, gap, total, gap], axis=-1)


def patch_kernel(rows, reqs, firsts, starts, sel_ref, *refs):
    slots = reqs.shape[0]
    kv_refs = refs[:slots]
    key_ref, value_ref, key_out, value_out, key_buf, value_buf, in_sem, out_sem = refs[slots:]
    tokens = sel_ref.shape[1]
    width = key_ref.shape[2]
    sources, buffers, targets = (key_ref, value_ref), (key_buf, value_buf), (key_out, value_out)

    def window(ref, slot):
        request = reqs[slot]
        return ref.at[request, pl.ds(pl.multiple_of(firsts[request], 16), rows)]

    def fetch(slot, which):
        return pltpu.make_async_copy(
            window(sources[which], slot), buffers[which].at[slot], in_sem.at[slot, which]
        )

    def store(slot, which):
        return pltpu.make_async_copy(
            buffers[which].at[slot], window(targets[which], slot), out_sem.at[slot, which]
        )

    for slot in range(slots):
        for which in range(2):
            fetch(slot, which).start()
    for slot in range(slots):
        request = reqs[slot]
        offset = firsts[request] - starts[request]
        row = lax.broadcasted_iota(jnp.int32, (rows, tokens), 0) + offset
        depth = lax.broadcasted_iota(jnp.int32, (rows, tokens), 1)
        hits = jnp.where(row == depth, 1.0, 0.0).astype(jnp.bfloat16)
        picks = jnp.dot(hits, sel_ref[request], preferred_element_type=jnp.float32)
        touched = jnp.sum(picks, axis=1, keepdims=True) > 0.5
        picks = picks.astype(jnp.bfloat16)
        for which in range(2):
            fresh = kv_refs[slot][:, which * width : (which + 1) * width]
            written = jnp.dot(picks, fresh, preferred_element_type=jnp.float32)
            fetch(slot, which).wait()
            buffer = buffers[which]
            buffer[slot] = jnp.where(touched, written.astype(jnp.bfloat16), buffer[slot])
            store(slot, which).start()
    for slot in range(slots):
        for which in range(2):
            store(slot, which).wait()


def patch(key_values, reqs, selector, starts, keys, values):
    requests, block_len, width = keys.shape
    tokens = selector.shape[1]
    rows = tokens + 16
    firsts = jnp.clip(starts // 16 * 16, 0, block_len - rows)
    vmem = pl.BlockSpec(memory_space=pltpu.VMEM)
    smem = pl.BlockSpec(memory_space=pltpu.SMEM)
    hbm = pl.BlockSpec(memory_space=pltpu.HBM)
    return pl.pallas_call(
        functools.partial(patch_kernel, rows),
        in_specs=[smem] * 3 + [vmem] * (1 + requests) + [hbm] * 2,
        out_specs=[hbm, hbm],
        out_shape=[jax.ShapeDtypeStruct(keys.shape, keys.dtype)] * 2,
        scratch_shapes=[
            pltpu.VMEM((requests, rows, width), keys.dtype),
            pltpu.VMEM((requests, rows, width), keys.dtype),
            pltpu.SemaphoreType.DMA((requests, 2)),
            pltpu.SemaphoreType.DMA((requests, 2)),
        ],
        input_output_aliases={4 + requests: 0, 5 + requests: 1},
        compiler_params=pltpu.CompilerParams(vmem_limit_bytes=8 * 1024 * 1024),
        cost_estimate=pl.CostEstimate(
            flops=0, transcendentals=0, bytes_accessed=8 * requests * rows * width
        ),
        name="patch",
    )(reqs, firsts, starts, selector, *key_values, keys, values)


def on_device(
    hidden,
    w_query,
    w_key,
    w_value,
    w_out,
    cache_key,
    cache_value,
    parents,
    lengths,
    holder,
    selector,
):
    requests, tree_size = parents.shape
    width = w_query.shape[1]
    block_len = cache_key.shape[1]
    block_count = holder.shape[1]
    scale = 1.0 / math.sqrt(HD)
    axis = "blocks"
    index = lax.axis_index(axis)
    levels = requests.bit_length() - 1
    bits = block_count.bit_length() - 1
    assert 1 << levels == requests and 1 << bits == block_count and bits > levels
    split = [1 << s for s in range(levels)]
    whole = [1 << s for s in range(levels, bits)]
    own = sum(((index >> s) & 1) << (levels - 1 - s) for s in range(levels))
    reqs = own ^ jnp.arange(requests, dtype=jnp.int32)

    slots = jnp.arange(block_count, dtype=jnp.int32)
    logical = jnp.sum(slots[None, :] * (holder == index).astype(jnp.int32), axis=1)
    starts = lengths - logical * block_len
    live = jnp.clip(starts, 0, block_len)

    blocks_of = hidden.reshape(requests, tree_size, -1)
    rows = [lax.dynamic_index_in_dim(blocks_of, reqs[k], 0, False) for k in range(requests)]
    half = requests // 2
    send_rows = jnp.concatenate(rows[half:], axis=0)
    keep_rows = jnp.concatenate(rows[:half], axis=0)

    def scattered(weights):
        sent = jnp.dot(send_rows, weights, preferred_element_type=jnp.float32)
        sent = swap(sent, axis, split[0])
        value = jnp.dot(keep_rows, weights, preferred_element_type=jnp.float32) + sent
        for bit in split[1:]:
            middle = value.shape[0] // 2
            value = value[:middle] + swap(value[middle:], axis, bit)
        return value

    def reduced(value):
        for bit in whole:
            value = value + swap(value, axis, bit)
        return value

    def gathered(value):
        values = [value]
        for bit in reversed(split):
            values = values + [swap(one, axis, bit) for one in values]
        return values

    query_part = scattered(w_query)
    late_parents, late_lengths = lax.optimization_barrier((parents, lengths))
    ancestors = ancestry(lax.dynamic_index_in_dim(late_parents, own, 0, False))
    depths = (jnp.sum(ancestors, axis=1) - 1.0).astype(jnp.int32)
    positions = lax.dynamic_index_in_dim(late_lengths, own, 0, False) + depths
    tables = rotary_tables(positions)

    query_own = rotate(reduced(query_part), tables).astype(jnp.bfloat16)
    key_value = reduced(scattered(jnp.concatenate([w_key, w_value], axis=1)))
    kv_own = jnp.concatenate([rotate(key_value[:, :width], tables), key_value[:, width:]], axis=1)
    kv_own = kv_own.astype(jnp.bfloat16)

    queries = gathered(query_own)
    keep, send, keys_copied, values_copied = cache_attention(
        queries, cache_key, cache_value, reqs, live, scale
    )
    cached = merge(keep, swap(send, axis, split[0]), width)
    for bit in split[1:]:
        middle = cached.shape[0] // 2
        cached = merge(cached[:middle], swap(cached[middle:], axis, bit), width)
    cached = cached[0]
    for bit in whole[:-1]:
        cached = merge(cached, swap(cached, axis, bit), width)
    tree = tree_attention(query_own, kv_own, ancestors, scale)
    out, _, total, spread = merged([cached, swap(cached, axis, whole[-1]), tree], width)
    attended_own = (out / spread(total)).astype(jnp.bfloat16)

    mixed = [
        jnp.dot(one, w_out, preferred_element_type=jnp.float32) for one in gathered(attended_own)
    ]
    natural = []
    for request in range(requests):
        row = mixed[0]
        for k in range(1, requests):
            row = jnp.where(own == request ^ k, mixed[k], row)
        natural.append(row)
    mixed = jnp.concatenate(natural, axis=0)
    head_bit = lax.axis_size("heads") // 2
    while head_bit:
        high = (lax.axis_index("heads") & head_bit) > 0
        middle = mixed.shape[0] // 2
        kept = jnp.where(high, mixed[middle:], mixed[:middle])
        sent = jnp.where(high, mixed[:middle], mixed[middle:])
        mixed = kept + swap(sent, "heads", head_bit)
        head_bit //= 2
    mixed = mixed.astype(jnp.bfloat16)

    key_out, value_out = patch(
        gathered(kv_own), reqs, selector.astype(jnp.bfloat16), starts, keys_copied, values_copied
    )
    return (mixed, key_out, value_out)


def solution(mesh):
    return jax.shard_map(
        on_device,
        mesh=mesh,
        in_specs=(
            P(None, "blocks"),
            P("blocks", "heads"),
            P("blocks", "heads"),
            P("blocks", "heads"),
            P("heads", "blocks"),
            P(None, "blocks", "heads"),
            P(None, "blocks", "heads"),
            P(),
            P(),
            P(),
            P(),
        ),
        out_specs=(P("heads", "blocks"), P(None, "blocks", "heads"), P(None, "blocks", "heads")),
        check_vma=False,
    )
```

time: 341 us -> 111 us (0.33)
  waiting for transfers between devices: 143 us -> 42.4 us
  other arithmetic: 66.6 us -> 4.89 us
  blocking collectives: 45.5 us -> 0 us
  matrix products: 33.7 us -> 3.06 us
  local copies, waits for them, and re-layouts: 34.8 us -> 9.76 us
  starting transfers between devices: 0.12 us -> 23.7 us
  Pallas kernels: 0 us -> 17.4 us
  between operations: 14 us -> 8.87 us
    psum x1 -> x0, waiting for transfers between devices: 74.1 us -> none  [on_device(): lax.psum(jnp.dot(hidden, joined, preferred_element_type=jnp.float32), 'bl...]
    all_gather x1 -> x0, waiting for transfers between devices: 69.1 us -> none  [joined_2(): gathered = jax.tree.map(lambda a: lax.all_gather(a, axis), part)]
    all_gather x2 -> x0, blocking collectives: 45.5 us -> none  [joined_2(): gathered = jax.tree.map(lambda a: lax.all_gather(a, axis), part)]
    ppermute x0 -> x22, waiting for transfers between devices: none -> 42.4 us  [swap(): return lax.ppermute(value, axis, [(i, i ^ bit) for i in range(size)])]
    add x31 -> x13, other arithmetic: 40.9 us -> 1.43 us  [the longest x4 1.12 us: merged(): total = sum((one * by for one, by in zip(totals, scales)))]
    dot_general x7 -> x8, matrix products: 31.6 us -> 1.41 us  [the longest x4 0.62 us: on_device(): jnp.dot(one, w_out, preferred_element_type=jnp.float32)]
    ppermute x0 -> x22, starting transfers between devices: none -> 23.7 us  [swap(): return lax.ppermute(value, axis, [(i, i ^ bit) for i in range(size)])]
    unnamed x16 -> x17, local copies, waits for them, and re-layouts: 23.6 us -> 1.9 us
  transfers between devices with their start and end apart: 3 -> 22, of which waited for: 2 -> 14; matrix products, arithmetic and copies ran while one was open for 18% -> 11% of each run, Pallas kernels for 0% -> 5%
where the time goes in v2:
time: 111 us; the launch traced here: 110 us
  waiting for transfers between devices  42.4 us (38%)
  starting transfers between devices  23.7 us (21%)
  Pallas kernels  17.4 us (16%)
  local copies, waits for them, and re-layouts  9.76 us (9%)
  between operations  8.87 us (8%)
  other arithmetic  4.89 us (4%)
  matrix products  3.06 us (3%)
    ppermute x22, waiting for transfers between devices, swap(): return lax.ppermute(value, axis, [(i, i ^ bit) for i in range(size)])  42.4 us
    ppermute x22, starting transfers between devices, swap(): return lax.ppermute(value, axis, [(i, i ^ bit) for i in range(size)])  23.7 us
    pallas_call x1, Pallas kernels, cache_attention(): pl.pallas_call(functools.partial(cache_kernel, scale), in_specs=[smem, sm...  11.5 us
    pallas_call x1, Pallas kernels, patch(): pl.pallas_call(functools.partial(patch_kernel, rows), in_specs=[smem] * 3...  3.69 us
    pallas_call x1, Pallas kernels, tree_attention(): pl.pallas_call(functools.partial(tree_kernel, scale), out_shape=jax.Shape...  2.22 us
  transfers between devices with their start and end apart: 22, of which 14 were waited for; matrix products, arithmetic and copies ran while one was open for 11% of the time, Pallas kernels for 5%

profile of v2, /device:TPU:0, one launch (start us, length us, event | category | flops | bytes accessed | tf_op | source)
XLA Modules:
  0.0 110.1 jit_solution(9026097692193758529)
XLA Ops:
  0.7 0.6 fusion.47
  9.0 0.8 dynamic-slice_bitcast_fusion.3
  9.8 0.2 fusion.29
  10.0 0.5 collective-permute-start
  10.5 1.0 constant_dynamic-update-slice_fusion.1
  11.4 1.0 constant_dynamic-update-slice_fusion
  12.4 0.2 fusion.28
  12.8 0.8 fusion.34
  13.6 0.2 convolution_minimum_fusion.5
  13.8 0.1 convolution_minimum_fusion.4
  14.0 0.1 convolution_minimum_fusion.3
  14.1 0.1 convolution_minimum_fusion.2
  14.3 0.1 convolution_minimum_fusion.1
  14.4 0.9 fusion.48
  15.3 1.2 %dynamic_slice.25 = s32[1]{0:T(128)} dynamic-slice(s32[4]{0:T(128)} %param.19, s32[]{:T(128)S(6)} %select_n.148), dynamic_slice_sizes={1} | dynamic-slice | bytes 12 | tf_op jit(solution)/shard_map/jit(dynamic_index_in_dim)/dynamic_slice | solution.py:372
  16.6 0.7 add_convert_fusion.1
  17.2 0.2 convolution_add_fusion.1
  17.4 3.0 %collective-permute-start.1 = (f32[32,1024]{1,0:T(8,128)S(1)}, f32[32,1024]{1,0:T(8,128)S(1)}, u32[]{:S(2)}, u32[]{:S(2)}) collective-permute-start(f32[32,1024]{1,0:T(8,128)S(1)} %slice.208), channel_id=1, source_target_pairs={{0,2},{1,3},{2,0},{3,1},{4,6},{5,7},{6,4},{7,5},{8,10},{9,11},{10,... | collective-permute-start | bytes 393224 | tf_op jit(solution)/shard_map/ppermute | solution.py:22
  20.5 0.2 convolution_add_fusion
  20.8 3.9 %collective-permute-done.1 = f32[32,1024]{1,0:T(8,128)S(1)} collective-permute-done((f32[32,1024]{1,0:T(8,128)S(1)}, f32[32,1024]{1,0:T(8,128)S(1)}, u32[]{:S(2)}, u32[]{:S(2)}) %collective-permute-start.1) | collective-permute-done | bytes 131104 | tf_op jit(solution)/shard_map/ppermute | solution.py:22
  24.8 2.2 %collective-permute-start.2 = (f32[32,1024]{1,0:T(8,128)S(1)}, f32[32,1024]{1,0:T(8,128)S(1)}, u32[]{:S(2)}, u32[]{:S(2)}) collective-permute-start(f32[32,1024]{1,0:T(8,128)S(1)} %slice_add_fusion.1), channel_id=1, source_target_pairs={{0,4},{1,5},{2,6},{3,7},{4,0},{5,1},{6,2},{7,3},{8,12},{9,13},{10,... | collective-permute-start | bytes 393224 | tf_op jit(solution)/shard_map/ppermute | solution.py:22
  27.0 2.9 %collective-permute-done.2 = f32[32,1024]{1,0:T(8,128)S(1)} collective-permute-done((f32[32,1024]{1,0:T(8,128)S(1)}, f32[32,1024]{1,0:T(8,128)S(1)}, u32[]{:S(2)}, u32[]{:S(2)}) %collective-permute-start.2) | collective-permute-done | bytes 131104 | tf_op jit(solution)/shard_map/ppermute | solution.py:22
  29.9 3.1 %collective-permute-start.3 = (f32[32,1024]{1,0:T(8,128)S(1)}, f32[32,1024]{1,0:T(8,128)S(1)}, u32[]{:S(2)}, u32[]{:S(2)}) collective-permute-start(f32[32,1024]{1,0:T(8,128)S(1)} %add.141), channel_id=1, source_target_pairs={{0,8},{1,9},{2,10},{3,11},{4,12},{5,13},{6,14},{7,15},{8,0},{9,1},... | collective-permute-start | bytes 393224 | tf_op jit(solution)/shard_map/ppermute | solution.py:22
  33.1 1.6 %collective-permute-start.13 = (f32[32,2048]{1,0:T(8,128)S(1)}, f32[32,2048]{1,0:T(8,128)S(1)}, u32[]{:S(2)}, u32[]{:S(2)}) collective-permute-start(f32[32,2048]{1,0:T(8,128)S(1)} %slice_add_fusion), channel_id=1, source_target_pairs={{0,4},{1,5},{2,6},{3,7},{4,0},{5,1},{6,2},{7,3},{8,12},{9,13},{10,... | collective-permute-start | bytes 786440 | tf_op jit(solution)/shard_map/ppermute | solution.py:22
  34.7 0.1 fusion.18
  34.9 0.8 select_reduce_fusion
  35.7 0.5 collective-permute-done.3
  36.2 4.0 %collective-permute-done.13 = f32[32,2048]{1,0:T(8,128)S(1)} collective-permute-done((f32[32,2048]{1,0:T(8,128)S(1)}, f32[32,2048]{1,0:T(8,128)S(1)}, u32[]{:S(2)}, u32[]{:S(2)}) %collective-permute-start.13) | collective-permute-done | bytes 262176 | tf_op jit(solution)/shard_map/ppermute | solution.py:22
  40.3 1.8 %collective-permute-start.14 = (f32[32,2048]{1,0:T(8,128)S(1)}, f32[32,2048]{1,0:T(8,128)S(1)}, u32[]{:S(2)}, u32[]{:S(2)}) collective-permute-start(f32[32,2048]{1,0:T(8,128)S(1)} %add.159), channel_id=1, source_target_pairs={{0,8},{1,9},{2,10},{3,11},{4,12},{5,13},{6,14},{7,15},{8,0},{9,1},... | collective-permute-start | bytes 786440 | tf_op jit(solution)/shard_map/ppermute | solution.py:22
  42.2 10.8 %collective-permute-done.14 = f32[32,2048]{1,0:T(8,128)S(1)} collective-permute-done((f32[32,2048]{1,0:T(8,128)S(1)}, f32[32,2048]{1,0:T(8,128)S(1)}, u32[]{:S(2)}, u32[]{:S(2)}) %collective-permute-start.14) | collective-permute-done | bytes 262176 | tf_op jit(solution)/shard_map/ppermute | solution.py:22
  53.3 0.2 fusion.4
  53.5 1.5 %collective-permute-start.4 = (bf16[32,1024]{1,0:T(8,128)(2,1)S(1)}, bf16[32,1024]{1,0:T(8,128)(2,1)S(1)}, u32[]{:S(2)}, u32[]{:S(2)}) collective-permute-start(bf16[32,1024]{1,0:T(8,128)(2,1)S(1)} %get-tuple-element.36.refs_0_.q_ref), channel_id=1, source_target_pairs={{0,2},{1,3},{2,0},{3,1},{4,6},{5,7},{6,4},{7,5},{8,10},{9,11},{10,... | collective-permute-start | bytes 196616 | tf_op jit(solution)/shard_map/ppermute | solution.py:22
  55.1 2.7 %collective-permute-done.4.refs_1_ = bf16[32,1024]{1,0:T(8,128)(2,1)S(1)} collective-permute-done((bf16[32,1024]{1,0:T(8,128)(2,1)S(1)}, bf16[32,1024]{1,0:T(8,128)(2,1)S(1)}, u32[]{:S(2)}, u32[]{:S(2)}) %collective-permute-start.4) | collective-permute-done | bytes 65568 | tf_op jit(solution)/shard_map/ppermute | solution.py:22
  57.8 1.2 %collective-permute-done.6.refs_3_ = bf16[32,1024]{1,0:T(8,128)(2,1)S(1)} collective-permute-done((bf16[32,1024]{1,0:T(8,128)(2,1)S(1)}, bf16[32,1024]{1,0:T(8,128)(2,1)S(1)}, u32[]{:S(2)}, u32[]{:S(2)}) %collective-permute-start.6) | collective-permute-done | bytes 65568 | tf_op jit(solution)/shard_map/ppermute | solution.py:22
  59.1 11.5 %cache_attention.1 = (f32[2,32,1152]{2,1,0:T(8,128)S(1)}, f32[2,32,1152]{2,1,0:T(8,128)S(1)}, bf16[4,1024,1024]{2,1,0:T(8,128)(2,1)}, bf16[4,1024,1024]{2,1,0:T(8,128)(2,1)}) custom-call(s32[4]{0:T(128)S(1)} %iota_xor_fusion.reqs, s32[4]{0:T(128)S(1)} %broadcast_clamp_fusion.live, bf16[32,1024]{1,0:T(8,128)(2,1)S(1)} %get-tuple-element.36.refs_0_.q_ref, ...), custom_call_target="tpu_custom_call" | custom-call | flops 2147483648 | bytes 33554432 | tf_op jit(solution)/shard_map/cache_attention/pallas_call | solution.py:163
  70.6 0.2 collective-permute-start.7
  70.9 1.4 %collective-permute-done.7 = f32[2,32,1152]{2,1,0:T(8,128)S(1)} collective-permute-done((f32[2,32,1152]{2,1,0:T(8,128)S(1)}, f32[2,32,1152]{2,1,0:T(8,128)S(1)}, u32[]{:S(2)}, u32[]{:S(2)}) %collective-permute-start.7) | collective-permute-done | bytes 294944 | tf_op jit(solution)/shard_map/ppermute | solution.py:22
  72.4 0.2 broadcast_in_dim.106
  72.6 0.2 reshape.235
  72.7 0.2 broadcast_in_dim.107
  72.9 0.2 reshape.236
  73.3 1.5 %collective-permute-start.8 = (f32[1,32,1152]{2,1,0:T(8,128)S(1)}, f32[1,32,1152]{2,1,0:T(8,128)S(1)}, u32[]{:S(2)}, u32[]{:S(2)}) collective-permute-start(f32[1,32,1152]{2,1,0:T(8,128)S(1)} %slice.218), channel_id=1, source_target_pairs={{0,2},{1,3},{2,0},{3,1},{4,6},{5,7},{6,4},{7,5},{8,10},{9,11},{10,... | collective-permute-start | bytes 442376 | tf_op jit(solution)/shard_map/ppermute | solution.py:22
  74.9 4.4 %collective-permute-done.8 = f32[1,32,1152]{2,1,0:T(8,128)S(1)} collective-permute-done((f32[1,32,1152]{2,1,0:T(8,128)S(1)}, f32[1,32,1152]{2,1,0:T(8,128)S(1)}, u32[]{:S(2)}, u32[]{:S(2)}) %collective-permute-start.8) | collective-permute-done | bytes 147488 | tf_op jit(solution)/shard_map/ppermute | solution.py:22
  79.5 0.1 broadcast_in_dim.111
  80.1 0.7 collective-permute-start.9
  80.8 4.4 %collective-permute-done.9 = f32[32,1152]{1,0:T(8,128)S(1)} collective-permute-done((f32[32,1152]{1,0:T(8,128)S(1)}, f32[32,1152]{1,0:T(8,128)S(1)}, u32[]{:S(2)}, u32[]{:S(2)}) %collective-permute-start.9) | collective-permute-done | bytes 147488 | tf_op jit(solution)/shard_map/ppermute | solution.py:22
  86.0 2.3 %collective-permute-start.10 = (f32[32,1152]{1,0:T(8,128)S(1)}, f32[32,1152]{1,0:T(8,128)S(1)}, u32[]{:S(2)}, u32[]{:S(2)}) collective-permute-start(f32[32,1152]{1,0:T(8,128)S(1)} %concatenate.49), channel_id=1, source_target_pairs={{0,8},{1,9},{2,10},{3,11},{4,12},{5,13},{6,14},{7,15},{8,0},{9,1},... | collective-permute-start | bytes 442376 | tf_op jit(solution)/shard_map/ppermute | solution.py:22
  88.3 1.6 %collective-permute-start.19 = (bf16[32,2048]{1,0:T(8,128)(2,1)S(1)}, bf16[32,2048]{1,0:T(8,128)(2,1)S(1)}, u32[]{:S(2)}, u32[]{:S(2)}) collective-permute-start(bf16[32,2048]{1,0:T(8,128)(2,1)S(1)} %pad_maximum_fusion.kv_ref.refs_0_), channel_id=1, source_target_pairs={{0,2},{1,3},{2,0},{3,1},{4,6},{5,7},{6,4},{7,5},{8,10},{9,11},{10,... | collective-permute-start | bytes 393224 | tf_op jit(solution)/shard_map/ppermute | solution.py:22
  89.9 2.2 %tree_attention.1 = f32[32,1152]{1,0:T(8,128)} custom-call(bf16[32,1024]{1,0:T(8,128)(2,1)} %copy-done.4, bf16[32,2048]{1,0:T(8,128)(2,1)} %copy-done.2, f32[32,32]{1,0:T(8,128)} %get-tuple-element.63.tree_ref), custom_call_target="tpu_custom_call" | custom-call | flops 16777216 | bytes 1000000 | tf_op jit(solution)/shard_map/tree_attention/pallas_call | solution.py:203
  92.1 1.2 %collective-permute-done.19.refs_1_ = bf16[32,2048]{1,0:T(8,128)(2,1)S(1)} collective-permute-done((bf16[32,2048]{1,0:T(8,128)(2,1)S(1)}, bf16[32,2048]{1,0:T(8,128)(2,1)S(1)}, u32[]{:S(2)}, u32[]{:S(2)}) %collective-permute-start.19) | collective-permute-done | bytes 131104 | tf_op jit(solution)/shard_map/ppermute | solution.py:22
  93.3 0.8 collective-permute-done.10
  94.2 0.9 fusion.19
  96.1 1.0 fusion.12
  97.1 1.6 %collective-permute-start.15 = (bf16[32,1024]{1,0:T(8,128)(2,1)S(1)}, bf16[32,1024]{1,0:T(8,128)(2,1)S(1)}, u32[]{:S(2)}, u32[]{:S(2)}) collective-permute-start(bf16[32,1024]{1,0:T(8,128)(2,1)S(1)} %fusion.12), channel_id=1, source_target_pairs={{0,2},{1,3},{2,0},{3,1},{4,6},{5,7},{6,4},{7,5},{8,10},{9,11},{10,... | collective-permute-start | bytes 196616 | tf_op jit(solution)/shard_map/ppermute | solution.py:22
  98.7 0.2 fusion.51
  98.8 2.8 %collective-permute-done.15 = bf16[32,1024]{1,0:T(8,128)(2,1)S(1)} collective-permute-done((bf16[32,1024]{1,0:T(8,128)(2,1)S(1)}, bf16[32,1024]{1,0:T(8,128)(2,1)S(1)}, u32[]{:S(2)}, u32[]{:S(2)}) %collective-permute-start.15) | collective-permute-done | bytes 65568 | tf_op jit(solution)/shard_map/ppermute | solution.py:22
  101.6 0.2 fusion.50
  101.9 0.2 fusion.49
  102.0 1.1 collective-permute-done.16
  103.1 0.2 select_select_fusion.3
  103.3 1.6 %collective-permute-start.18 = (f32[64,128]{1,0:T(8,128)S(1)}, f32[64,128]{1,0:T(8,128)S(1)}, u32[]{:S(2)}, u32[]{:S(2)}) collective-permute-start(f32[64,128]{1,0:T(8,128)S(1)} %fusion.14), channel_id=1, source_target_pairs={{0,16},{16,0},{1,17},{17,1},{2,18},{18,2},{3,19},{19,3},{4,20},{20... | collective-permute-start | bytes 98312 | tf_op jit(solution)/shard_map/ppermute | solution.py:22
  104.9 0.9 copy-done.3
  105.8 3.7 %patch.1 = (bf16[4,1024,1024]{2,1,0:T(8,128)(2,1)}, bf16[4,1024,1024]{2,1,0:T(8,128)(2,1)}) custom-call(s32[4]{0:T(128)S(1)} %iota_xor_fusion.reqs, s32[4]{0:T(128)S(1)} %get-tuple-element.19.firsts, s32[4]{0:T(128)S(1)} %get-tuple-element.20.starts, ...), custom_call_target="tpu_custom_call", output_to_operand_aliasing={{0}: (8, {}), {1}: (9, {})} | custom-call | bytes 1572864 | tf_op jit(solution)/shard_map/patch/pallas_call | solution.py:289
  109.5 0.6 add_convert_fusion
  (86 shorter events, 3.7 us)
Async XLA Ops:
  0.6 9.1 %copy-start = (bf16[128,1024]{1,0:T(8,128)(2,1)S(1)}, bf16[128,1024]{1,0:T(8,128)(2,1)}, u32[]{:S(2)}) copy-start(bf16[128,1024]{1,0:T(8,128)(2,1)} %param.12) | copy-start | bytes 786436
  0.6 54.4 %copy-start.7 = (s32[4]{0:T(128)S(1)}, s32[4]{0:T(128)}, u32[]{:S(2)}) copy-start(s32[4]{0:T(128)} %param.19) | copy-start | bytes 52
  10.0 7.3 %collective-permute-start = (f32[64,1024]{1,0:T(8,128)S(1)}, f32[64,1024]{1,0:T(8,128)S(1)}, u32[]{:S(2)}, u32[]{:S(2)}) collective-permute-start(f32[64,1024]{1,0:T(8,128)S(1)} %fusion.29), channel_id=1, source_target_pairs={{0,1},{1,0},{2,3},{3,2},{4,5},{5,4},{6,7},{7,6},{8,9},{9,8},{10,11... | collective-permute-start | bytes 786440 | tf_op jit(solution)/shard_map/ppermute | solution.py:22
  12.6 7.8 %collective-permute-start.11 = (f32[64,2048]{1,0:T(8,128)S(1)}, f32[64,2048]{1,0:T(8,128)S(1)}, u32[]{:S(2)}, u32[]{:S(2)}) collective-permute-start(f32[64,2048]{1,0:T(8,128)S(1)} %fusion.28), channel_id=1, source_target_pairs={{0,1},{1,0},{2,3},{3,2},{4,5},{5,4},{6,7},{7,6},{8,9},{9,8},{10,11... | collective-permute-start | bytes 1572872 | tf_op jit(solution)/shard_map/ppermute | solution.py:22
  12.8 46.3 %copy-start.1 = (bf16[4,1024,1024]{2,1,0:T(8,128)(2,1)S(1)}, bf16[4,1024,1024]{2,1,0:T(8,128)(2,1)}, u32[]{:S(2)}) copy-start(bf16[4,1024,1024]{2,1,0:T(8,128)(2,1)} %refs_4_.1) | copy-start | bytes 25165828
  17.4 7.3 %collective-permute-start.1 = (f32[32,1024]{1,0:T(8,128)S(1)}, f32[32,1024]{1,0:T(8,128)S(1)}, u32[]{:S(2)}, u32[]{:S(2)}) collective-permute-start(f32[32,1024]{1,0:T(8,128)S(1)} %slice.208), channel_id=1, source_target_pairs={{0,2},{1,3},{2,0},{3,1},{4,6},{5,7},{6,4},{7,5},{8,10},{9,11},{10,... | collective-permute-start | bytes 393224 | tf_op jit(solution)/shard_map/ppermute | solution.py:22
  20.7 12.3 %collective-permute-start.12 = (f32[32,2048]{1,0:T(8,128)S(1)}, f32[32,2048]{1,0:T(8,128)S(1)}, u32[]{:S(2)}, u32[]{:S(2)}) collective-permute-start(f32[32,2048]{1,0:T(8,128)S(1)} %slice.231), channel_id=1, source_target_pairs={{0,2},{1,3},{2,0},{3,1},{4,6},{5,7},{6,4},{7,5},{8,10},{9,11},{10,... | collective-permute-start | bytes 786440 | tf_op jit(solution)/shard_map/ppermute | solution.py:22
  24.8 5.2 %collective-permute-start.2 = (f32[32,1024]{1,0:T(8,128)S(1)}, f32[32,1024]{1,0:T(8,128)S(1)}, u32[]{:S(2)}, u32[]{:S(2)}) collective-permute-start(f32[32,1024]{1,0:T(8,128)S(1)} %slice_add_fusion.1), channel_id=1, source_target_pairs={{0,4},{1,5},{2,6},{3,7},{4,0},{5,1},{6,2},{7,3},{8,12},{9,13},{10,... | collective-permute-start | bytes 393224 | tf_op jit(solution)/shard_map/ppermute | solution.py:22
  29.9 6.2 %collective-permute-start.3 = (f32[32,1024]{1,0:T(8,128)S(1)}, f32[32,1024]{1,0:T(8,128)S(1)}, u32[]{:S(2)}, u32[]{:S(2)}) collective-permute-start(f32[32,1024]{1,0:T(8,128)S(1)} %add.141), channel_id=1, source_target_pairs={{0,8},{1,9},{2,10},{3,11},{4,12},{5,13},{6,14},{7,15},{8,0},{9,1},... | collective-permute-start | bytes 393224 | tf_op jit(solution)/shard_map/ppermute | solution.py:22
  33.1 7.1 %collective-permute-start.13 = (f32[32,2048]{1,0:T(8,128)S(1)}, f32[32,2048]{1,0:T(8,128)S(1)}, u32[]{:S(2)}, u32[]{:S(2)}) collective-permute-start(f32[32,2048]{1,0:T(8,128)S(1)} %slice_add_fusion), channel_id=1, source_target_pairs={{0,4},{1,5},{2,6},{3,7},{4,0},{5,1},{6,2},{7,3},{8,12},{9,13},{10,... | collective-permute-start | bytes 786440 | tf_op jit(solution)/shard_map/ppermute | solution.py:22
  40.3 12.7 %collective-permute-start.14 = (f32[32,2048]{1,0:T(8,128)S(1)}, f32[32,2048]{1,0:T(8,128)S(1)}, u32[]{:S(2)}, u32[]{:S(2)}) collective-permute-start(f32[32,2048]{1,0:T(8,128)S(1)} %add.159), channel_id=1, source_target_pairs={{0,8},{1,9},{2,10},{3,11},{4,12},{5,13},{6,14},{7,15},{8,0},{9,1},... | collective-permute-start | bytes 786440 | tf_op jit(solution)/shard_map/ppermute | solution.py:22
  53.5 17.1 %copy-start.4 = (bf16[32,1024]{1,0:T(8,128)(2,1)}, bf16[32,1024]{1,0:T(8,128)(2,1)S(1)}, u32[]{:S(2)}) copy-start(bf16[32,1024]{1,0:T(8,128)(2,1)S(1)} %get-tuple-element.36.refs_0_.q_ref) | copy-start | bytes 196612
  53.5 4.3 %collective-permute-start.4 = (bf16[32,1024]{1,0:T(8,128)(2,1)S(1)}, bf16[32,1024]{1,0:T(8,128)(2,1)S(1)}, u32[]{:S(2)}, u32[]{:S(2)}) collective-permute-start(bf16[32,1024]{1,0:T(8,128)(2,1)S(1)} %get-tuple-element.36.refs_0_.q_ref), channel_id=1, source_target_pairs={{0,2},{1,3},{2,0},{3,1},{4,6},{5,7},{6,4},{7,5},{8,10},{9,11},{10,... | collective-permute-start | bytes 196616 | tf_op jit(solution)/shard_map/ppermute | solution.py:22
  55.0 2.8 %collective-permute-start.5 = (bf16[32,1024]{1,0:T(8,128)(2,1)S(1)}, bf16[32,1024]{1,0:T(8,128)(2,1)S(1)}, u32[]{:S(2)}, u32[]{:S(2)}) collective-permute-start(bf16[32,1024]{1,0:T(8,128)(2,1)S(1)} %get-tuple-element.36.refs_0_.q_ref), channel_id=1, source_target_pairs={{0,1},{1,0},{2,3},{3,2},{4,5},{5,4},{6,7},{7,6},{8,9},{9,8},{10,11... | collective-permute-start | bytes 196616 | tf_op jit(solution)/shard_map/ppermute | solution.py:22
  57.8 1.3 %collective-permute-start.6 = (bf16[32,1024]{1,0:T(8,128)(2,1)S(1)}, bf16[32,1024]{1,0:T(8,128)(2,1)S(1)}, u32[]{:S(2)}, u32[]{:S(2)}) collective-permute-start(bf16[32,1024]{1,0:T(8,128)(2,1)S(1)} %collective-permute-done.4.refs_1_), channel_id=1, source_target_pairs={{0,1},{1,0},{2,3},{3,2},{4,5},{5,4},{6,7},{7,6},{8,9},{9,8},{10,11... | collective-permute-start | bytes 196616 | tf_op jit(solution)/shard_map/ppermute | solution.py:22
  70.6 28.1 %copy-start.5 = (bf16[1024,128]{1,0:T(8,128)(2,1)S(1)}, bf16[1024,128]{1,0:T(8,128)(2,1)}, u32[]{:S(2)}) copy-start(bf16[1024,128]{1,0:T(8,128)(2,1)} %param.15) | copy-start | bytes 786436
  70.6 34.3 %copy-start.6 = (s32[4,32,32]{2,1,0:T(8,128)S(1)}, s32[4,32,32]{2,1,0:T(8,128)}, u32[]{:S(2)}) copy-start(s32[4,32,32]{2,1,0:T(8,128)} %param.21) | copy-start | bytes 49156
  70.6 1.6 %collective-permute-start.7 = (f32[2,32,1152]{2,1,0:T(8,128)S(1)}, f32[2,32,1152]{2,1,0:T(8,128)S(1)}, u32[]{:S(2)}, u32[]{:S(2)}) collective-permute-start(f32[2,32,1152]{2,1,0:T(8,128)S(1)} %get-tuple-element.14), channel_id=1, source_target_pairs={{0,1},{1,0},{2,3},{3,2},{4,5},{5,4},{6,7},{7,6},{8,9},{9,8},{10,11... | collective-permute-start | bytes 884744 | tf_op jit(solution)/shard_map/ppermute | solution.py:22
  73.3 6.0 %collective-permute-start.8 = (f32[1,32,1152]{2,1,0:T(8,128)S(1)}, f32[1,32,1152]{2,1,0:T(8,128)S(1)}, u32[]{:S(2)}, u32[]{:S(2)}) collective-permute-start(f32[1,32,1152]{2,1,0:T(8,128)S(1)} %slice.218), channel_id=1, source_target_pairs={{0,2},{1,3},{2,0},{3,1},{4,6},{5,7},{6,4},{7,5},{8,10},{9,11},{10,... | collective-permute-start | bytes 442376 | tf_op jit(solution)/shard_map/ppermute | solution.py:22
  80.1 5.2 %collective-permute-start.9 = (f32[32,1152]{1,0:T(8,128)S(1)}, f32[32,1152]{1,0:T(8,128)S(1)}, u32[]{:S(2)}, u32[]{:S(2)}) collective-permute-start(f32[32,1152]{1,0:T(8,128)S(1)} %bitcast.79), channel_id=1, source_target_pairs={{0,4},{1,5},{2,6},{3,7},{4,0},{5,1},{6,2},{7,3},{8,12},{9,13},{10,... | collective-permute-start | bytes 442376 | tf_op jit(solution)/shard_map/ppermute | solution.py:22
  86.0 8.2 %collective-permute-start.10 = (f32[32,1152]{1,0:T(8,128)S(1)}, f32[32,1152]{1,0:T(8,128)S(1)}, u32[]{:S(2)}, u32[]{:S(2)}) collective-permute-start(f32[32,1152]{1,0:T(8,128)S(1)} %concatenate.49), channel_id=1, source_target_pairs={{0,8},{1,9},{2,10},{3,11},{4,12},{5,13},{6,14},{7,15},{8,0},{9,1},... | collective-permute-start | bytes 442376 | tf_op jit(solution)/shard_map/ppermute | solution.py:22
  88.3 1.6 %copy-start.2 = (bf16[32,2048]{1,0:T(8,128)(2,1)}, bf16[32,2048]{1,0:T(8,128)(2,1)S(1)}, u32[]{:S(2)}) copy-start(bf16[32,2048]{1,0:T(8,128)(2,1)S(1)} %pad_maximum_fusion.kv_ref.refs_0_) | copy-start | bytes 393220
  88.3 5.0 %collective-permute-start.19 = (bf16[32,2048]{1,0:T(8,128)(2,1)S(1)}, bf16[32,2048]{1,0:T(8,128)(2,1)S(1)}, u32[]{:S(2)}, u32[]{:S(2)}) collective-permute-start(bf16[32,2048]{1,0:T(8,128)(2,1)S(1)} %pad_maximum_fusion.kv_ref.refs_0_), channel_id=1, source_target_pairs={{0,2},{1,3},{2,0},{3,1},{4,6},{5,7},{6,4},{7,5},{8,10},{9,11},{10,... | collective-permute-start | bytes 393224 | tf_op jit(solution)/shard_map/ppermute | solution.py:22
  89.9 15.0 %collective-permute-start.20 = (bf16[32,2048]{1,0:T(8,128)(2,1)S(1)}, bf16[32,2048]{1,0:T(8,128)(2,1)S(1)}, u32[]{:S(2)}, u32[]{:S(2)}) collective-permute-start(bf16[32,2048]{1,0:T(8,128)(2,1)S(1)} %pad_maximum_fusion.kv_ref.refs_0_), channel_id=1, source_target_pairs={{0,1},{1,0},{2,3},{3,2},{4,5},{5,4},{6,7},{7,6},{8,9},{9,8},{10,11... | collective-permute-start | bytes 393224 | tf_op jit(solution)/shard_map/ppermute | solution.py:22
  93.3 11.6 %collective-permute-start.21 = (bf16[32,2048]{1,0:T(8,128)(2,1)S(1)}, bf16[32,2048]{1,0:T(8,128)(2,1)S(1)}, u32[]{:S(2)}, u32[]{:S(2)}) collective-permute-start(bf16[32,2048]{1,0:T(8,128)(2,1)S(1)} %collective-permute-done.19.refs_1_), channel_id=1, source_target_pairs={{0,1},{1,0},{2,3},{3,2},{4,5},{5,4},{6,7},{7,6},{8,9},{9,8},{10,11... | collective-permute-start | bytes 393224 | tf_op jit(solution)/shard_map/ppermute | solution.py:22
  97.0 4.8 %collective-permute-start.17 = (bf16[32,1024]{1,0:T(8,128)(2,1)S(1)}, bf16[32,1024]{1,0:T(8,128)(2,1)S(1)}, u32[]{:S(2)}, u32[]{:S(2)}) collective-permute-start(bf16[32,1024]{1,0:T(8,128)(2,1)S(1)} %fusion.12), channel_id=1, source_target_pairs={{0,1},{1,0},{2,3},{3,2},{4,5},{5,4},{6,7},{7,6},{8,9},{9,8},{10,11... | collective-permute-start | bytes 196616 | tf_op jit(solution)/shard_map/ppermute | solution.py:22
  97.1 4.5 %collective-permute-start.15 = (bf16[32,1024]{1,0:T(8,128)(2,1)S(1)}, bf16[32,1024]{1,0:T(8,128)(2,1)S(1)}, u32[]{:S(2)}, u32[]{:S(2)}) collective-permute-start(bf16[32,1024]{1,0:T(8,128)(2,1)S(1)} %fusion.12), channel_id=1, source_target_pairs={{0,2},{1,3},{2,0},{3,1},{4,6},{5,7},{6,4},{7,5},{8,10},{9,11},{10,... | collective-permute-start | bytes 196616 | tf_op jit(solution)/shard_map/ppermute | solution.py:22
  101.8 1.3 %collective-permute-start.16 = (bf16[32,1024]{1,0:T(8,128)(2,1)S(1)}, bf16[32,1024]{1,0:T(8,128)(2,1)S(1)}, u32[]{:S(2)}, u32[]{:S(2)}) collective-permute-start(bf16[32,1024]{1,0:T(8,128)(2,1)S(1)} %collective-permute-done.15), channel_id=1, source_target_pairs={{0,1},{1,0},{2,3},{3,2},{4,5},{5,4},{6,7},{7,6},{8,9},{9,8},{10,11... | collective-permute-start | bytes 196616 | tf_op jit(solution)/shard_map/ppermute | solution.py:22
  103.3 6.2 %collective-permute-start.18 = (f32[64,128]{1,0:T(8,128)S(1)}, f32[64,128]{1,0:T(8,128)S(1)}, u32[]{:S(2)}, u32[]{:S(2)}) collective-permute-start(f32[64,128]{1,0:T(8,128)S(1)} %fusion.14), channel_id=1, source_target_pairs={{0,16},{16,0},{1,17},{17,1},{2,18},{18,2},{3,19},{19,3},{4,20},{20... | collective-permute-start | bytes 98312 | tf_op jit(solution)/shard_map/ppermute | solution.py:22
  104.9 0.9 copy-start.3

commit v3 on v2

--- a/solution.py
+++ b/solution.py
@@ -126,7 +126,6 @@
         count = live[reqs[slot]]
         row = lax.broadcasted_iota(jnp.int32, (1, block_len), 1)
         bias = jnp.where(row < count, 0.0, masked_low)
-        some = count > 0
         target = send_ref if slot >= half else keep_ref
         place = slot % half
         stats = jnp.zeros((tokens, LANES), jnp.float32)
@@ -171,7 +170,7 @@
             pltpu.SemaphoreType.DMA((slots, 2)),
             pltpu.SemaphoreType.DMA((slots, 2)),
         ],
-        compiler_params=pltpu.CompilerParams(vmem_limit_bytes=40 * 1024 * 1024),
+        compiler_params=pltpu.CompilerParams(vmem_limit_bytes=58 * 1024 * 1024),
         cost_estimate=pl.CostEstimate(
             flops=16 * slots * tokens * width * block_len,
             transcendentals=slots * tokens * (width // HD) * block_len,
@@ -210,26 +209,31 @@
     )(queries, key_value, tree)
 
 
-def merged(parts, width):
+def spread(value, width):
+    wide = jnp.broadcast_to(value[..., None], value.shape + (HD,))
+    return wide.reshape(value.shape[:-1] + (width,))
+
+
+def merged_stats(parts, width):
     heads = width // HD
     tops = [part[..., width : width + heads] for part in parts]
     totals = [part[..., width + HD : width + HD + heads] for part in parts]
     top = functools.reduce(jnp.maximum, tops)
     scales = [jnp.exp(one - top) for one in tops]
     total = sum(one * by for one, by in zip(totals, scales))
-
-    def spread(value):
-        wide = jnp.broadcast_to(value[..., None], value.shape + (HD,))
-        return wide.reshape(value.shape[:-1] + (width,))
-
-    out = sum(part[..., :width] * spread(by) for part, by in zip(parts, scales))
-    return out, top, total, spread
+    return scales, top, total
 
 
 def merge(one, two, width):
-    out, top, total, _ = merged([one, two], width)
+    scales, top, total = merged_stats([one, two], width)
+    out = sum(part[..., :width] * spread(by, width) for part, by in zip([one, two], scales))
     gap = jnp.zeros(top.shape[:-1] + (HD - top.shape[-1],), jnp.float32)
     return jnp.concatenate([out, top, gap, total, gap], axis=-1)
+
+
+def blended(parts, width):
+    scales, _, total = merged_stats(parts, width)
+    return sum(part[..., :width] * spread(by / total, width) for part, by in zip(parts, scales))
 
 
 def patch_kernel(rows, reqs, firsts, starts, sel_ref, *refs):
@@ -332,6 +336,7 @@
     split = [1 << s for s in range(levels)]
     whole = [1 << s for s in range(levels, bits)]
     own = sum(((index >> s) & 1) << (levels - 1 - s) for s in range(levels))
+    own = own.astype(jnp.int32)
     reqs = own ^ jnp.arange(requests, dtype=jnp.int32)
 
     slots = jnp.arange(block_count, dtype=jnp.int32)
@@ -339,24 +344,10 @@
     starts = lengths - logical * block_len
     live = jnp.clip(starts, 0, block_len)
 
-    blocks_of = hidden.reshape(requests, tree_size, -1)
-    rows = [lax.dynamic_index_in_dim(blocks_of, reqs[k], 0, False) for k in range(requests)]
-    half = requests // 2
-    send_rows = jnp.concatenate(rows[half:], axis=0)
-    keep_rows = jnp.concatenate(rows[:half], axis=0)
-
-    def scattered(weights):
-        sent = jnp.dot(send_rows, weights, preferred_element_type=jnp.float32)
-        sent = swap(sent, axis, split[0])
-        value = jnp.dot(keep_rows, weights, preferred_element_type=jnp.float32) + sent
+    def scattered(value):
         for bit in split[1:]:
             middle = value.shape[0] // 2
             value = value[:middle] + swap(value[middle:], axis, bit)
-        return value
-
-    def reduced(value):
-        for bit in whole:
-            value = value + swap(value, axis, bit)
         return value
 
     def gathered(value):
@@ -365,21 +356,56 @@
             values = values + [swap(one, axis, bit) for one in values]
         return values
 
-    query_part = scattered(w_query)
-    late_parents, late_lengths = lax.optimization_barrier((parents, lengths))
+    def tied(value, *others):
+        return lax.optimization_barrier((value,) + others)
+
+    def after(value, *others):
+        return tied(value, *others)[0]
+
+    half = requests // 2 * tree_size
+    blocks_of = hidden.reshape(requests, tree_size, -1)
+    rows = [lax.dynamic_index_in_dim(blocks_of, own ^ k, 0, False) for k in range(requests)]
+    rows = jnp.concatenate(rows, axis=0)
+
+    def first_sum(rows, weights):
+        parts = [jnp.dot(rows, w, preferred_element_type=jnp.float32) for w in weights]
+        sent = swap(jnp.concatenate([part[half:] for part in parts], axis=1), axis, split[0])
+        return jnp.concatenate([part[:half] for part in parts], axis=1) + sent
+
+    query_half = first_sum(rows, [w_query])
+    kv_half = first_sum(after(rows, query_half), [w_key, w_value])
+    query_sum = scattered(query_half)
+    kv_half = after(kv_half, query_sum)
+    late_parents, _ = tied(parents, query_sum)
     ancestors = ancestry(lax.dynamic_index_in_dim(late_parents, own, 0, False))
-    depths = (jnp.sum(ancestors, axis=1) - 1.0).astype(jnp.int32)
+    query_sum = query_sum + swap(query_sum, axis, whole[0])
+    query_sum, kv_half, ancestors = tied(query_sum, kv_half, ancestors)
+    late_lengths, late_ancestors, _ = tied(lengths, ancestors, query_sum)
+    depths = (jnp.sum(late_ancestors, axis=1) - 1.0).astype(jnp.int32)
     positions = lax.dynamic_index_in_dim(late_lengths, own, 0, False) + depths
     tables = rotary_tables(positions)
 
-    query_own = rotate(reduced(query_part), tables).astype(jnp.bfloat16)
-    key_value = reduced(scattered(jnp.concatenate([w_key, w_value], axis=1)))
-    kv_own = jnp.concatenate([rotate(key_value[:, :width], tables), key_value[:, width:]], axis=1)
-    kv_own = kv_own.astype(jnp.bfloat16)
-
+    kv_sum = scattered(kv_half)
+    for bit in whole[1:]:
+        query_sum = query_sum + swap(query_sum, axis, bit)
+    query_own = rotate(query_sum, tables).astype(jnp.bfloat16)
     queries = gathered(query_own)
+    takes_value = (index & whole[0]) > 0
+    key_part, value_part = kv_sum[:, :width], kv_sum[:, width:]
+    part = jnp.where(takes_value, value_part, key_part)
+    part = part + swap(jnp.where(takes_value, key_part, value_part), axis, whole[0])
+    *queries, part = tied(*queries, part)
+
     keep, send, keys_copied, values_copied = cache_attention(
         queries, cache_key, cache_value, reqs, live, scale
+    )
+    for bit in whole[1:]:
+        part = part + swap(part, axis, bit)
+    keep, send, part = tied(keep, send, part)
+    part = jnp.where(takes_value, part, rotate(part, tables)).astype(jnp.bfloat16)
+    far = swap(part, axis, whole[0])
+    kv_own = jnp.concatenate(
+        [jnp.where(takes_value, far, part), jnp.where(takes_value, part, far)], axis=1
     )
     cached = merge(keep, swap(send, axis, split[0]), width)
     for bit in split[1:]:
@@ -389,12 +415,16 @@
     for bit in whole[:-1]:
         cached = merge(cached, swap(cached, axis, bit), width)
     tree = tree_attention(query_own, kv_own, ancestors, scale)
-    out, _, total, spread = merged([cached, swap(cached, axis, whole[-1]), tree], width)
-    attended_own = (out / spread(total)).astype(jnp.bfloat16)
-
-    mixed = [
-        jnp.dot(one, w_out, preferred_element_type=jnp.float32) for one in gathered(attended_own)
-    ]
+    key_out, value_out = patch(
+        gathered(kv_own), reqs, selector.astype(jnp.bfloat16), starts, keys_copied, values_copied
+    )
+    other = swap(cached, axis, whole[-1])
+    other, tree = tied(other, tree)
+    attended_own = blended([cached, other, tree], width).astype(jnp.bfloat16)
+    everyone = gathered(attended_own)
+    everyone[1], key_out, value_out = tied(everyone[1], key_out, value_out)
+
+    mixed = [jnp.dot(one, w_out, preferred_element_type=jnp.float32) for one in everyone]
     natural = []
     for request in range(requests):
         row = mixed[0]
@@ -412,9 +442,6 @@
         head_bit //= 2
     mixed = mixed.astype(jnp.bfloat16)
 
-    key_out, value_out = patch(
-        gathered(kv_own), reqs, selector.astype(jnp.bfloat16), starts, keys_copied, values_copied
-    )
     return (mixed, key_out, value_out)
 
 

time: 111 us -> 85.8 us (0.77)
  waiting for transfers between devices: 42.4 us -> 22.5 us
  between operations: 8.87 us -> 1.27 us
  local copies, waits for them, and re-layouts: 9.76 us -> 6.4 us
  Pallas kernels: 17.4 us -> 19.3 us
  other arithmetic: 4.89 us -> 6.51 us
  starting transfers between devices: 23.7 us -> 25.3 us
    ppermute x22 -> x23, waiting for transfers between devices: 42.4 us -> 22.5 us  [swap(): return lax.ppermute(value, axis, [(i, i ^ bit) for i in range(size)])]
    pallas_call x1, Pallas kernels: 11.5 us -> 13.4 us  [cache_attention(): pl.pallas_call(functools.partial(cache_kernel, scale), in_specs=[smem, sm...]
    dot_general x4 -> x3, matrix products: 0.78 us -> 2.53 us  [first_sum(): jnp.dot(rows, w, preferred_element_type=jnp.float32)]
    ppermute x22 -> x23, starting transfers between devices: 23.7 us -> 25.3 us  [swap(): return lax.ppermute(value, axis, [(i, i ^ bit) for i in range(size)])]
    add x11 -> x12, other arithmetic: 1.38 us -> 2.35 us  [the longest x3 1.09 us: merge(): sum((part[..., :width] * spread(by, width) for part, by in zip([one, two]...]
  transfers between devices with their start and end apart: 22 -> 23, of which waited for: 14 -> 10; matrix products, arithmetic and copies ran while one was open for 11% -> 14% of each run, Pallas kernels for 5% -> 23%
where the time goes in v3:
time: 85.8 us; the launch traced here: 85.4 us
  starting transfers between devices  25.3 us (29%)
  waiting for transfers between devices  22.5 us (26%)
  Pallas kernels  19.3 us (22%)
  other arithmetic  6.51 us (8%)
  local copies, waits for them, and re-layouts  6.4 us (7%)
  matrix products  4.1 us (5%)
  between operations  1.27 us (1%)
    ppermute x23, starting transfers between devices, swap(): return lax.ppermute(value, axis, [(i, i ^ bit) for i in range(size)])  25.3 us
    ppermute x23, waiting for transfers between devices, swap(): return lax.ppermute(value, axis, [(i, i ^ bit) for i in range(size)])  22.5 us
    pallas_call x1, Pallas kernels, cache_attention(): pl.pallas_call(functools.partial(cache_kernel, scale), in_specs=[smem, sm...  13.4 us
    pallas_call x1, Pallas kernels, patch(): pl.pallas_call(functools.partial(patch_kernel, rows), in_specs=[smem] * 3...  3.69 us
    dot_general x3, matrix products, first_sum(): jnp.dot(rows, w, preferred_element_type=jnp.float32)  2.53 us
    pallas_call x1, Pallas kernels, tree_attention(): pl.pallas_call(functools.partial(tree_kernel, scale), out_shape=jax.Shape...  2.23 us
  transfers between devices with their start and end apart: 23, of which 10 were waited for; matrix products, arithmetic and copies ran while one was open for 14% of the time, Pallas kernels for 23%

profile of v3, /device:TPU:0, one launch (start us, length us, event | category | flops | bytes accessed | tf_op | source)
XLA Modules:
  0.0 85.4 jit_solution(11767936941373386912)
XLA Ops:
  0.7 0.8 dynamic-slice_bitcast_fusion.3
  1.6 0.2 fusion.35
  1.8 0.5 collective-permute-start
  2.4 0.8 select_reduce_fusion
  3.2 0.7 multiply_clamp_fusion
  3.9 2.6 %collective-permute-start.1 = (f32[32,1024]{1,0:T(8,128)S(1)}, f32[32,1024]{1,0:T(8,128)S(1)}, u32[]{:S(2)}, u32[]{:S(2)}) collective-permute-start(f32[32,1024]{1,0:T(8,128)S(1)} %slice.213), channel_id=1, source_target_pairs={{0,2},{1,3},{2,0},{3,1},{4,6},{5,7},{6,4},{7,5},{8,10},{9,11},{10,... | collective-permute-start | bytes 393224 | tf_op jit(solution)/shard_map/ppermute | solution.py:22
  6.5 1.2 %fusion.42 = f32[128,1024]{1,0:T(8,128)S(1)} fusion(bf16[128,128]{1,0:T(8,128)(2,1)S(1)} %pad_maximum_fusion.2, bf16[128,1024]{1,0:T(8,128)(2,1)} %param.13), kind=kOutput, calls=%fused_computation.123 | convolution fusion | flops 33554432 | bytes 819200 | tf_op jit(solution)/shard_map/dot_general | solution.py:371
  7.7 1.2 %fusion.43 = f32[128,1024]{1,0:T(8,128)S(1)} fusion(bf16[128,128]{1,0:T(8,128)(2,1)S(1)} %pad_maximum_fusion.2, bf16[128,1024]{1,0:T(8,128)(2,1)} %param.14), kind=kOutput, calls=%fused_computation.124 | convolution fusion | flops 33554432 | bytes 819200 | tf_op jit(solution)/shard_map/dot_general | solution.py:371
  9.0 0.3 collective-permute-start.3
  9.2 1.4 %collective-permute-done.1 = f32[32,1024]{1,0:T(8,128)S(1)} collective-permute-done((f32[32,1024]{1,0:T(8,128)S(1)}, f32[32,1024]{1,0:T(8,128)S(1)}, u32[]{:S(2)}, u32[]{:S(2)}) %collective-permute-start.1) | collective-permute-done | bytes 131104 | tf_op jit(solution)/shard_map/ppermute | solution.py:22
  10.7 1.9 %collective-permute-start.2 = (f32[32,1024]{1,0:T(8,128)S(1)}, f32[32,1024]{1,0:T(8,128)S(1)}, u32[]{:S(2)}, u32[]{:S(2)}) collective-permute-start(f32[32,1024]{1,0:T(8,128)S(1)} %slice_add_fusion.2), channel_id=1, source_target_pairs={{0,4},{1,5},{2,6},{3,7},{4,0},{5,1},{6,2},{7,3},{8,12},{9,13},{10,... | collective-permute-start | bytes 393224 | tf_op jit(solution)/shard_map/ppermute | solution.py:22
  12.6 0.7 fusion.30
  13.3 0.2 convolution_minimum_fusion.5
  13.5 0.1 convolution_minimum_fusion.4
  13.6 0.1 convolution_minimum_fusion.3
  13.8 0.1 convolution_minimum_fusion.2
  13.9 0.1 convolution_minimum_fusion.1
  14.1 0.1 convolution_minimum_fusion.tree_ref
  14.3 1.8 %collective-permute-done.2 = f32[32,1024]{1,0:T(8,128)S(1)} collective-permute-done((f32[32,1024]{1,0:T(8,128)S(1)}, f32[32,1024]{1,0:T(8,128)S(1)}, u32[]{:S(2)}, u32[]{:S(2)}) %collective-permute-start.2) | collective-permute-done | bytes 131104 | tf_op jit(solution)/shard_map/ppermute | solution.py:22
  16.1 2.7 %collective-permute-start.4 = (f32[32,1024]{1,0:T(8,128)S(1)}, f32[32,1024]{1,0:T(8,128)S(1)}, u32[]{:S(2)}, u32[]{:S(2)}) collective-permute-start(f32[32,1024]{1,0:T(8,128)S(1)} %add.139), channel_id=1, source_target_pairs={{0,8},{1,9},{2,10},{3,11},{4,12},{5,13},{6,14},{7,15},{8,0},{9,1},... | collective-permute-start | bytes 393224 | tf_op jit(solution)/shard_map/ppermute | solution.py:22
  18.8 0.6 dynamic_slice.26
  19.4 1.6 %collective-permute-start.8 = (f32[32,2048]{1,0:T(8,128)S(1)}, f32[32,2048]{1,0:T(8,128)S(1)}, u32[]{:S(2)}, u32[]{:S(2)}) collective-permute-start(f32[32,2048]{1,0:T(8,128)S(1)} %slice.178), channel_id=1, source_target_pairs={{0,2},{1,3},{2,0},{3,1},{4,6},{5,7},{6,4},{7,5},{8,10},{9,11},{10,... | collective-permute-start | bytes 786440 | tf_op jit(solution)/shard_map/ppermute | solution.py:22
  21.1 0.7 add_convert_fusion.2
  21.8 0.1 fusion.15
  21.9 2.4 %collective-permute-done.4 = f32[32,1024]{1,0:T(8,128)S(1)} collective-permute-done((f32[32,1024]{1,0:T(8,128)S(1)}, f32[32,1024]{1,0:T(8,128)S(1)}, u32[]{:S(2)}, u32[]{:S(2)}) %collective-permute-start.4) | collective-permute-done | bytes 131104 | tf_op jit(solution)/shard_map/ppermute | solution.py:22
  24.7 1.4 %collective-permute-start.5 = (bf16[32,1024]{1,0:T(8,128)(2,1)S(1)}, bf16[32,1024]{1,0:T(8,128)(2,1)S(1)}, u32[]{:S(2)}, u32[]{:S(2)}) collective-permute-start(bf16[32,1024]{1,0:T(8,128)(2,1)S(1)} %fusion.2.refs_0_.q_ref), channel_id=1, source_target_pairs={{0,2},{1,3},{2,0},{3,1},{4,6},{5,7},{6,4},{7,5},{8,10},{9,11},{10,... | collective-permute-start | bytes 196616 | tf_op jit(solution)/shard_map/ppermute | solution.py:22
  26.1 0.2 collective-permute-done.8
  26.3 2.3 %collective-permute-start.9 = (f32[32,1024]{1,0:T(8,128)S(1)}, f32[32,1024]{1,0:T(8,128)S(1)}, u32[]{:S(2)}, u32[]{:S(2)}) collective-permute-start(f32[32,1024]{1,0:T(8,128)S(1)} %slice_select_fusion), channel_id=1, source_target_pairs={{0,4},{1,5},{2,6},{3,7},{4,0},{5,1},{6,2},{7,3},{8,12},{9,13},{10,... | collective-permute-start | bytes 393224 | tf_op jit(solution)/shard_map/ppermute | solution.py:22
  28.6 0.6 iota_xor_fusion
  29.2 0.5 collective-permute-start.7
  29.7 1.9 %collective-permute-done.9 = f32[32,1024]{1,0:T(8,128)S(1)} collective-permute-done((f32[32,1024]{1,0:T(8,128)S(1)}, f32[32,1024]{1,0:T(8,128)S(1)}, u32[]{:S(2)}, u32[]{:S(2)}) %collective-permute-start.9) | collective-permute-done | bytes 131104 | tf_op jit(solution)/shard_map/ppermute | solution.py:22
  31.6 1.7 %collective-permute-start.10 = (f32[32,1024]{1,0:T(8,128)S(1)}, f32[32,1024]{1,0:T(8,128)S(1)}, u32[]{:S(2)}, u32[]{:S(2)}) collective-permute-start(f32[32,1024]{1,0:T(8,128)S(1)} %select_add_fusion), channel_id=1, source_target_pairs={{0,8},{1,9},{2,10},{3,11},{4,12},{5,13},{6,14},{7,15},{8,0},{9,1},... | collective-permute-start | bytes 393224 | tf_op jit(solution)/shard_map/ppermute | solution.py:22
  33.3 13.4 %cache_attention.1 = (f32[2,32,1152]{2,1,0:T(8,128)}, f32[2,32,1152]{2,1,0:T(8,128)}, bf16[4,1024,1024]{2,1,0:T(8,128)(2,1)}, bf16[4,1024,1024]{2,1,0:T(8,128)(2,1)}) custom-call(s32[4]{0:T(128)} %get-tuple-element.105.reqs, s32[4]{0:T(128)} %get-tuple-element.106.live, bf16[32,1024]{1,0:T(8,128)(2,1)} %copy-done.6, bf16[32,1024]{1,0:T(8,128)(2,1)} %copy-done.8, ...), custom_call_target="tpu_custom_call" | custom-call | flops 2147483648 | bytes 33554432 | tf_op jit(solution)/shard_map/cache_attention/pallas_call | solution.py:162
  47.2 2.1 %collective-permute-start.15 = (bf16[32,1024]{1,0:T(8,128)(2,1)S(1)}, bf16[32,1024]{1,0:T(8,128)(2,1)S(1)}, u32[]{:S(2)}, u32[]{:S(2)}) collective-permute-start(bf16[32,1024]{1,0:T(8,128)(2,1)S(1)} %fusion.5), channel_id=1, source_target_pairs={{0,4},{1,5},{2,6},{3,7},{4,0},{5,1},{6,2},{7,3},{8,12},{9,13},{10,... | collective-permute-start | bytes 196616 | tf_op jit(solution)/shard_map/ppermute | solution.py:22
  49.3 0.9 %fusion.10 = (f32[2,32,16]{2,1,0:T(8,128)S(1)}, f32[2,32,16]{2,1,0:T(8,128)S(1)}, f32[2,32,16]{2,1,0:T(8,128)S(1)}, f32[2,32,16]{2,1,0:T(8,128)S(1)}) fusion(f32[2,32,1152]{2,1,0:T(8,128)S(1)} %collective-permute-done.11, f32[2,32,1152]{2,1,0:T(8,128)} %get-tuple-element.45), kind=kLoop, calls=%fused_computation.39 | loop fusion | flops 6144 | bytes 32768 | tf_op jit(solution)/shard_map/add | solution.py:223
  50.2 0.2 broadcast_in_dim.101
  50.4 0.2 reshape.232
  50.6 0.2 broadcast_in_dim.100
  50.8 0.2 reshape.231
  50.9 1.0 %fusion = f32[2,32,1024]{2,1,0:T(8,128)S(1)} fusion(f32[2,32,1024]{2,1,0:T(8,128)S(1)} %reshape.232, f32[2,32,1152]{2,1,0:T(8,128)S(1)} %collective-permute-done.11, f32[2,32,1024]{2,1,0:T(8,128)S(1)} %reshape.231, f32[2,32,1152]{2,1,0:T(8,128)} %get-tuple-element.45), kind=kLoop, calls=%fused_computation.9 | loop fusion | flops 196608 | bytes 1310720 | tf_op jit(solution)/shard_map/add | solution.py:229
  52.1 0.6 collective-permute-start.12
  52.7 5.4 %collective-permute-done.12 = f32[1,32,1152]{2,1,0:T(8,128)S(1)} collective-permute-done((f32[1,32,1152]{2,1,0:T(8,128)S(1)}, f32[1,32,1152]{2,1,0:T(8,128)S(1)}, u32[]{:S(2)}, u32[]{:S(2)}) %collective-permute-start.12) | collective-permute-done | bytes 147488 | tf_op jit(solution)/shard_map/ppermute | solution.py:22
  58.4 0.1 broadcast_in_dim.108
  58.6 0.1 broadcast_in_dim.105
  58.9 1.4 %collective-permute-start.13 = (f32[32,1152]{1,0:T(8,128)S(1)}, f32[32,1152]{1,0:T(8,128)S(1)}, u32[]{:S(2)}, u32[]{:S(2)}) collective-permute-start(f32[32,1152]{1,0:T(8,128)S(1)} %bitcast.84), channel_id=1, source_target_pairs={{0,4},{1,5},{2,6},{3,7},{4,0},{5,1},{6,2},{7,3},{8,12},{9,13},{10,... | collective-permute-start | bytes 442376 | tf_op jit(solution)/shard_map/ppermute | solution.py:22
  60.3 0.6 collective-permute-start.19
  60.9 3.2 %collective-permute-done.13 = f32[32,1152]{1,0:T(8,128)S(1)} collective-permute-done((f32[32,1152]{1,0:T(8,128)S(1)}, f32[32,1152]{1,0:T(8,128)S(1)}, u32[]{:S(2)}, u32[]{:S(2)}) %collective-permute-start.13) | collective-permute-done | bytes 147488 | tf_op jit(solution)/shard_map/ppermute | solution.py:22
  64.5 0.1 reshape.233
  64.8 1.3 %collective-permute-start.14 = (f32[32,1152]{1,0:T(8,128)S(1)}, f32[32,1152]{1,0:T(8,128)S(1)}, u32[]{:S(2)}, u32[]{:S(2)}) collective-permute-start(f32[32,1152]{1,0:T(8,128)S(1)} %concatenate.49), channel_id=1, source_target_pairs={{0,8},{1,9},{2,10},{3,11},{4,12},{5,13},{6,14},{7,15},{8,0},{9,1},... | collective-permute-start | bytes 442376 | tf_op jit(solution)/shard_map/ppermute | solution.py:22
  66.1 0.5 collective-permute-start.21
  66.7 2.2 %tree_attention.1 = f32[32,1152]{1,0:T(8,128)} custom-call(bf16[32,1024]{1,0:T(8,128)(2,1)} %copy-done.6, bf16[32,2048]{1,0:T(8,128)(2,1)} %copy-done.1, f32[32,32]{1,0:T(8,128)} %copy-done.7), custom_call_target="tpu_custom_call" | custom-call | flops 16777216 | bytes 1000000 | tf_op jit(solution)/shard_map/tree_attention/pallas_call | solution.py:202
  68.9 0.9 %copy-done.2 = bf16[32,2048]{1,0:T(8,128)(2,1)S(1)} copy-done((bf16[32,2048]{1,0:T(8,128)(2,1)S(1)}, bf16[32,2048]{1,0:T(8,128)(2,1)}, u32[]{:S(2)}) %copy-start.2) | copy-done | bytes 131096
  69.8 3.7 %patch.1 = (bf16[4,1024,1024]{2,1,0:T(8,128)(2,1)}, bf16[4,1024,1024]{2,1,0:T(8,128)(2,1)}) custom-call(s32[4]{0:T(128)S(1)} %copy-done.3, s32[4]{0:T(128)S(1)} %get-tuple-element.57.firsts, s32[4]{0:T(128)S(1)} %get-tuple-element.58.starts, bf16[4,32,32]{2,1,0:T(8,128)(2,1)S(1)} %convert_element_type.51.sel_ref, ...), custom_call_target="tpu_custom_call", output_to_operand_aliasing={{0}: (8, {}), {1}: (9, {})} | custom-call | bytes 1572864 | tf_op jit(solution)/shard_map/patch/pallas_call | solution.py:293
  73.8 0.1 reshape.237
  74.6 1.6 %collective-permute-start.16 = (bf16[32,1024]{1,0:T(8,128)(2,1)S(1)}, bf16[32,1024]{1,0:T(8,128)(2,1)S(1)}, u32[]{:S(2)}, u32[]{:S(2)}) collective-permute-start(bf16[32,1024]{1,0:T(8,128)(2,1)S(1)} %add_convert_fusion), channel_id=1, source_target_pairs={{0,2},{1,3},{2,0},{3,1},{4,6},{5,7},{6,4},{7,5},{8,10},{9,11},{10,... | collective-permute-start | bytes 196616 | tf_op jit(solution)/shard_map/ppermute | solution.py:22
  76.2 0.2 fusion.46
  76.3 2.8 %collective-permute-done.16 = bf16[32,1024]{1,0:T(8,128)(2,1)S(1)} collective-permute-done((bf16[32,1024]{1,0:T(8,128)(2,1)S(1)}, bf16[32,1024]{1,0:T(8,128)(2,1)S(1)}, u32[]{:S(2)}, u32[]{:S(2)}) %collective-permute-start.16) | collective-permute-done | bytes 65568 | tf_op jit(solution)/shard_map/ppermute | solution.py:22
  79.1 0.2 fusion.45
  79.3 0.2 fusion.44
  79.5 1.1 %collective-permute-done.17 = bf16[32,1024]{1,0:T(8,128)(2,1)S(1)} collective-permute-done((bf16[32,1024]{1,0:T(8,128)(2,1)S(1)}, bf16[32,1024]{1,0:T(8,128)(2,1)S(1)}, u32[]{:S(2)}, u32[]{:S(2)}) %collective-permute-start.17) | collective-permute-done | bytes 65568 | tf_op jit(solution)/shard_map/ppermute | solution.py:22
  80.6 0.2 select_select_fusion.3
  80.8 1.6 %collective-permute-start.22 = (f32[64,128]{1,0:T(8,128)S(1)}, f32[64,128]{1,0:T(8,128)S(1)}, u32[]{:S(2)}, u32[]{:S(2)}) collective-permute-start(f32[64,128]{1,0:T(8,128)S(1)} %fusion.11), channel_id=1, source_target_pairs={{0,16},{16,0},{1,17},{17,1},{2,18},{18,2},{3,19},{19,3},{4,20},{20... | collective-permute-start | bytes 98312 | tf_op jit(solution)/shard_map/ppermute | solution.py:22
  82.4 2.4 %collective-permute-done.22 = f32[64,128]{1,0:T(8,128)S(1)} collective-permute-done((f32[64,128]{1,0:T(8,128)S(1)}, f32[64,128]{1,0:T(8,128)S(1)}, u32[]{:S(2)}, u32[]{:S(2)}) %collective-permute-start.22) | collective-permute-done | bytes 32800 | tf_op jit(solution)/shard_map/ppermute | solution.py:22
  84.8 0.6 add_convert_fusion.1
  (101 shorter events, 3.6 us)
Async XLA Ops:
  0.6 1.0 %copy-start = (bf16[128,1024]{1,0:T(8,128)(2,1)S(1)}, bf16[128,1024]{1,0:T(8,128)(2,1)}, u32[]{:S(2)}) copy-start(bf16[128,1024]{1,0:T(8,128)(2,1)} %param.12) | copy-start | bytes 786436
  0.6 18.2 %copy-start.12 = (s32[4]{0:T(128)S(1)}, s32[4]{0:T(128)}, u32[]{:S(2)}) copy-start(s32[4]{0:T(128)} %param.19) | copy-start | bytes 52
  1.8 2.0 %collective-permute-start = (f32[64,1024]{1,0:T(8,128)S(1)}, f32[64,1024]{1,0:T(8,128)S(1)}, u32[]{:S(2)}, u32[]{:S(2)}) collective-permute-start(f32[64,1024]{1,0:T(8,128)S(1)} %slice.211), channel_id=1, source_target_pairs={{0,1},{1,0},{2,3},{3,2},{4,5},{5,4},{6,7},{7,6},{8,9},{9,8},{10,11... | collective-permute-start | bytes 786440 | tf_op jit(solution)/shard_map/ppermute | solution.py:22
  3.9 6.7 %collective-permute-start.1 = (f32[32,1024]{1,0:T(8,128)S(1)}, f32[32,1024]{1,0:T(8,128)S(1)}, u32[]{:S(2)}, u32[]{:S(2)}) collective-permute-start(f32[32,1024]{1,0:T(8,128)S(1)} %slice.213), channel_id=1, source_target_pairs={{0,2},{1,3},{2,0},{3,1},{4,6},{5,7},{6,4},{7,5},{8,10},{9,11},{10,... | collective-permute-start | bytes 393224 | tf_op jit(solution)/shard_map/ppermute | solution.py:22
  9.0 7.1 %collective-permute-start.3 = (f32[64,2048]{1,0:T(8,128)S(1)}, f32[64,2048]{1,0:T(8,128)S(1)}, u32[]{:S(2)}, u32[]{:S(2)}) collective-permute-start(f32[64,2048]{1,0:T(8,128)S(1)} %pad_maximum_fusion), channel_id=1, source_target_pairs={{0,1},{1,0},{2,3},{3,2},{4,5},{5,4},{6,7},{7,6},{8,9},{9,8},{10,11... | collective-permute-start | bytes 1572872 | tf_op jit(solution)/shard_map/ppermute | solution.py:22
  10.7 5.4 %collective-permute-start.2 = (f32[32,1024]{1,0:T(8,128)S(1)}, f32[32,1024]{1,0:T(8,128)S(1)}, u32[]{:S(2)}, u32[]{:S(2)}) collective-permute-start(f32[32,1024]{1,0:T(8,128)S(1)} %slice_add_fusion.2), channel_id=1, source_target_pairs={{0,4},{1,5},{2,6},{3,7},{4,0},{5,1},{6,2},{7,3},{8,12},{9,13},{10,... | collective-permute-start | bytes 393224 | tf_op jit(solution)/shard_map/ppermute | solution.py:22
  14.2 32.5 %copy-start.7 = (f32[32,32]{1,0:T(8,128)}, f32[32,32]{1,0:T(8,128)S(1)}, u32[]{:S(2)}) copy-start(f32[32,32]{1,0:T(8,128)S(1)} %convolution_minimum_fusion.tree_ref) | copy-start | bytes 12292
  16.1 8.2 %collective-permute-start.4 = (f32[32,1024]{1,0:T(8,128)S(1)}, f32[32,1024]{1,0:T(8,128)S(1)}, u32[]{:S(2)}, u32[]{:S(2)}) collective-permute-start(f32[32,1024]{1,0:T(8,128)S(1)} %add.139), channel_id=1, source_target_pairs={{0,8},{1,9},{2,10},{3,11},{4,12},{5,13},{6,14},{7,15},{8,0},{9,1},... | collective-permute-start | bytes 393224 | tf_op jit(solution)/shard_map/ppermute | solution.py:22
  19.4 6.8 %collective-permute-start.8 = (f32[32,2048]{1,0:T(8,128)S(1)}, f32[32,2048]{1,0:T(8,128)S(1)}, u32[]{:S(2)}, u32[]{:S(2)}) collective-permute-start(f32[32,2048]{1,0:T(8,128)S(1)} %slice.178), channel_id=1, source_target_pairs={{0,2},{1,3},{2,0},{3,1},{4,6},{5,7},{6,4},{7,5},{8,10},{9,11},{10,... | collective-permute-start | bytes 786440 | tf_op jit(solution)/shard_map/ppermute | solution.py:22
  24.7 8.6 %copy-start.6 = (bf16[32,1024]{1,0:T(8,128)(2,1)}, bf16[32,1024]{1,0:T(8,128)(2,1)S(1)}, u32[]{:S(2)}) copy-start(bf16[32,1024]{1,0:T(8,128)(2,1)S(1)} %fusion.2.refs_0_.q_ref) | copy-start | bytes 196612
  24.7 4.5 %collective-permute-start.5 = (bf16[32,1024]{1,0:T(8,128)(2,1)S(1)}, bf16[32,1024]{1,0:T(8,128)(2,1)S(1)}, u32[]{:S(2)}, u32[]{:S(2)}) collective-permute-start(bf16[32,1024]{1,0:T(8,128)(2,1)S(1)} %fusion.2.refs_0_.q_ref), channel_id=1, source_target_pairs={{0,2},{1,3},{2,0},{3,1},{4,6},{5,7},{6,4},{7,5},{8,10},{9,11},{10,... | collective-permute-start | bytes 196616 | tf_op jit(solution)/shard_map/ppermute | solution.py:22
  26.3 5.3 %collective-permute-start.9 = (f32[32,1024]{1,0:T(8,128)S(1)}, f32[32,1024]{1,0:T(8,128)S(1)}, u32[]{:S(2)}, u32[]{:S(2)}) collective-permute-start(f32[32,1024]{1,0:T(8,128)S(1)} %slice_select_fusion), channel_id=1, source_target_pairs={{0,4},{1,5},{2,6},{3,7},{4,0},{5,1},{6,2},{7,3},{8,12},{9,13},{10,... | collective-permute-start | bytes 393224 | tf_op jit(solution)/shard_map/ppermute | solution.py:22
  29.2 2.4 %collective-permute-start.6 = (bf16[32,1024]{1,0:T(8,128)(2,1)S(1)}, bf16[32,1024]{1,0:T(8,128)(2,1)S(1)}, u32[]{:S(2)}, u32[]{:S(2)}) collective-permute-start(bf16[32,1024]{1,0:T(8,128)(2,1)S(1)} %fusion.2.refs_0_.q_ref), channel_id=1, source_target_pairs={{0,1},{1,0},{2,3},{3,2},{4,5},{5,4},{6,7},{7,6},{8,9},{9,8},{10,11... | collective-permute-start | bytes 196616 | tf_op jit(solution)/shard_map/ppermute | solution.py:22
  29.2 4.1 %copy-start.8 = (bf16[32,1024]{1,0:T(8,128)(2,1)}, bf16[32,1024]{1,0:T(8,128)(2,1)S(1)}, u32[]{:S(2)}) copy-start(bf16[32,1024]{1,0:T(8,128)(2,1)S(1)} %collective-permute-done.5.refs_1_) | copy-start | bytes 196612
  29.2 2.4 %collective-permute-start.7 = (bf16[32,1024]{1,0:T(8,128)(2,1)S(1)}, bf16[32,1024]{1,0:T(8,128)(2,1)S(1)}, u32[]{:S(2)}, u32[]{:S(2)}) collective-permute-start(bf16[32,1024]{1,0:T(8,128)(2,1)S(1)} %collective-permute-done.5.refs_1_), channel_id=1, source_target_pairs={{0,1},{1,0},{2,3},{3,2},{4,5},{5,4},{6,7},{7,6},{8,9},{9,8},{10,11... | collective-permute-start | bytes 196616 | tf_op jit(solution)/shard_map/ppermute | solution.py:22
  31.6 1.7 %copy-start.9 = (bf16[32,1024]{1,0:T(8,128)(2,1)}, bf16[32,1024]{1,0:T(8,128)(2,1)S(1)}, u32[]{:S(2)}) copy-start(bf16[32,1024]{1,0:T(8,128)(2,1)S(1)} %collective-permute-done.6.refs_2_) | copy-start | bytes 196612
  31.6 1.7 %copy-start.10 = (bf16[32,1024]{1,0:T(8,128)(2,1)}, bf16[32,1024]{1,0:T(8,128)(2,1)S(1)}, u32[]{:S(2)}) copy-start(bf16[32,1024]{1,0:T(8,128)(2,1)S(1)} %collective-permute-done.7.refs_3_) | copy-start | bytes 196612
  31.6 15.1 %collective-permute-start.10 = (f32[32,1024]{1,0:T(8,128)S(1)}, f32[32,1024]{1,0:T(8,128)S(1)}, u32[]{:S(2)}, u32[]{:S(2)}) collective-permute-start(f32[32,1024]{1,0:T(8,128)S(1)} %select_add_fusion), channel_id=1, source_target_pairs={{0,8},{1,9},{2,10},{3,11},{4,12},{5,13},{6,14},{7,15},{8,0},{9,1},... | collective-permute-start | bytes 393224 | tf_op jit(solution)/shard_map/ppermute | solution.py:22
  46.7 19.9 %copy-start.11 = (s32[4,32,32]{2,1,0:T(8,128)S(1)}, s32[4,32,32]{2,1,0:T(8,128)}, u32[]{:S(2)}) copy-start(s32[4,32,32]{2,1,0:T(8,128)} %param.21) | copy-start | bytes 49156
  46.8 22.2 %copy-start.3 = (s32[4]{0:T(128)S(1)}, s32[4]{0:T(128)}, u32[]{:S(2)}) copy-start(s32[4]{0:T(128)} %get-tuple-element.105.reqs) | copy-start | bytes 52
  46.8 2.5 %collective-permute-start.11 = (f32[2,32,1152]{2,1,0:T(8,128)}, f32[2,32,1152]{2,1,0:T(8,128)S(1)}, u32[]{:S(2)}, u32[]{:S(2)}) collective-permute-start(f32[2,32,1152]{2,1,0:T(8,128)} %get-tuple-element.46), channel_id=1, source_target_pairs={{0,1},{1,0},{2,3},{3,2},{4,5},{5,4},{6,7},{7,6},{8,9},{9,8},{10,11... | collective-permute-start | bytes 884744 | tf_op jit(solution)/shard_map/ppermute | solution.py:22
  47.2 5.5 %collective-permute-start.15 = (bf16[32,1024]{1,0:T(8,128)(2,1)S(1)}, bf16[32,1024]{1,0:T(8,128)(2,1)S(1)}, u32[]{:S(2)}, u32[]{:S(2)}) collective-permute-start(bf16[32,1024]{1,0:T(8,128)(2,1)S(1)} %fusion.5), channel_id=1, source_target_pairs={{0,4},{1,5},{2,6},{3,7},{4,0},{5,1},{6,2},{7,3},{8,12},{9,13},{10,... | collective-permute-start | bytes 196616 | tf_op jit(solution)/shard_map/ppermute | solution.py:22
  52.1 6.0 %collective-permute-start.12 = (f32[1,32,1152]{2,1,0:T(8,128)S(1)}, f32[1,32,1152]{2,1,0:T(8,128)S(1)}, u32[]{:S(2)}, u32[]{:S(2)}) collective-permute-start(f32[1,32,1152]{2,1,0:T(8,128)S(1)} %slice.229), channel_id=1, source_target_pairs={{0,2},{1,3},{2,0},{3,1},{4,6},{5,7},{6,4},{7,5},{8,10},{9,11},{10,... | collective-permute-start | bytes 442376 | tf_op jit(solution)/shard_map/ppermute | solution.py:22
  58.9 5.2 %collective-permute-start.13 = (f32[32,1152]{1,0:T(8,128)S(1)}, f32[32,1152]{1,0:T(8,128)S(1)}, u32[]{:S(2)}, u32[]{:S(2)}) collective-permute-start(f32[32,1152]{1,0:T(8,128)S(1)} %bitcast.84), channel_id=1, source_target_pairs={{0,4},{1,5},{2,6},{3,7},{4,0},{5,1},{6,2},{7,3},{8,12},{9,13},{10,... | collective-permute-start | bytes 442376 | tf_op jit(solution)/shard_map/ppermute | solution.py:22
  60.3 6.4 %copy-start.1 = (bf16[32,2048]{1,0:T(8,128)(2,1)}, bf16[32,2048]{1,0:T(8,128)(2,1)S(1)}, u32[]{:S(2)}) copy-start(bf16[32,2048]{1,0:T(8,128)(2,1)S(1)} %pad_maximum_fusion.1.kv_ref.refs_0_) | copy-start | bytes 393220
  60.3 5.9 %collective-permute-start.19 = (bf16[32,2048]{1,0:T(8,128)(2,1)S(1)}, bf16[32,2048]{1,0:T(8,128)(2,1)S(1)}, u32[]{:S(2)}, u32[]{:S(2)}) collective-permute-start(bf16[32,2048]{1,0:T(8,128)(2,1)S(1)} %pad_maximum_fusion.1.kv_ref.refs_0_), channel_id=1, source_target_pairs={{0,2},{1,3},{2,0},{3,1},{4,6},{5,7},{6,4},{7,5},{8,10},{9,11},{10,... | collective-permute-start | bytes 393224 | tf_op jit(solution)/shard_map/ppermute | solution.py:22
  64.8 8.7 %collective-permute-start.14 = (f32[32,1152]{1,0:T(8,128)S(1)}, f32[32,1152]{1,0:T(8,128)S(1)}, u32[]{:S(2)}, u32[]{:S(2)}) collective-permute-start(f32[32,1152]{1,0:T(8,128)S(1)} %concatenate.49), channel_id=1, source_target_pairs={{0,8},{1,9},{2,10},{3,11},{4,12},{5,13},{6,14},{7,15},{8,0},{9,1},... | collective-permute-start | bytes 442376 | tf_op jit(solution)/shard_map/ppermute | solution.py:22
  66.1 2.8 %collective-permute-start.20 = (bf16[32,2048]{1,0:T(8,128)(2,1)S(1)}, bf16[32,2048]{1,0:T(8,128)(2,1)S(1)}, u32[]{:S(2)}, u32[]{:S(2)}) collective-permute-start(bf16[32,2048]{1,0:T(8,128)(2,1)S(1)} %pad_maximum_fusion.1.kv_ref.refs_0_), channel_id=1, source_target_pairs={{0,1},{1,0},{2,3},{3,2},{4,5},{5,4},{6,7},{7,6},{8,9},{9,8},{10,11... | collective-permute-start | bytes 393224 | tf_op jit(solution)/shard_map/ppermute | solution.py:22
  66.1 2.8 %collective-permute-start.21 = (bf16[32,2048]{1,0:T(8,128)(2,1)S(1)}, bf16[32,2048]{1,0:T(8,128)(2,1)S(1)}, u32[]{:S(2)}, u32[]{:S(2)}) collective-permute-start(bf16[32,2048]{1,0:T(8,128)(2,1)S(1)} %collective-permute-done.19.refs_1_), channel_id=1, source_target_pairs={{0,1},{1,0},{2,3},{3,2},{4,5},{5,4},{6,7},{7,6},{8,9},{9,8},{10,11... | collective-permute-start | bytes 393224 | tf_op jit(solution)/shard_map/ppermute | solution.py:22
  68.9 0.9 %copy-start.2 = (bf16[32,2048]{1,0:T(8,128)(2,1)S(1)}, bf16[32,2048]{1,0:T(8,128)(2,1)}, u32[]{:S(2)}) copy-start(bf16[32,2048]{1,0:T(8,128)(2,1)} %copy-done.1) | copy-start | bytes 393220
  69.8 3.7 %copy-start.5 = (f32[32,1152]{1,0:T(8,128)S(1)}, f32[32,1152]{1,0:T(8,128)}, u32[]{:S(2)}) copy-start(f32[32,1152]{1,0:T(8,128)} %tree_attention.1) | copy-start | bytes 442372
  69.8 6.3 %copy-start.4 = (bf16[1024,128]{1,0:T(8,128)(2,1)S(1)}, bf16[1024,128]{1,0:T(8,128)(2,1)}, u32[]{:S(2)}) copy-start(bf16[1024,128]{1,0:T(8,128)(2,1)} %param.15) | copy-start | bytes 786436
  74.5 4.8 %collective-permute-start.18 = (bf16[32,1024]{1,0:T(8,128)(2,1)S(1)}, bf16[32,1024]{1,0:T(8,128)(2,1)S(1)}, u32[]{:S(2)}, u32[]{:S(2)}) collective-permute-start(bf16[32,1024]{1,0:T(8,128)(2,1)S(1)} %add_convert_fusion), channel_id=1, source_target_pairs={{0,1},{1,0},{2,3},{3,2},{4,5},{5,4},{6,7},{7,6},{8,9},{9,8},{10,11... | collective-permute-start | bytes 196616 | tf_op jit(solution)/shard_map/ppermute | solution.py:22
  74.6 4.5 %collective-permute-start.16 = (bf16[32,1024]{1,0:T(8,128)(2,1)S(1)}, bf16[32,1024]{1,0:T(8,128)(2,1)S(1)}, u32[]{:S(2)}, u32[]{:S(2)}) collective-permute-start(bf16[32,1024]{1,0:T(8,128)(2,1)S(1)} %add_convert_fusion), channel_id=1, source_target_pairs={{0,2},{1,3},{2,0},{3,1},{4,6},{5,7},{6,4},{7,5},{8,10},{9,11},{10,... | collective-permute-start | bytes 196616 | tf_op jit(solution)/shard_map/ppermute | solution.py:22
  79.3 1.3 %collective-permute-start.17 = (bf16[32,1024]{1,0:T(8,128)(2,1)S(1)}, bf16[32,1024]{1,0:T(8,128)(2,1)S(1)}, u32[]{:S(2)}, u32[]{:S(2)}) collective-permute-start(bf16[32,1024]{1,0:T(8,128)(2,1)S(1)} %collective-permute-done.16), channel_id=1, source_target_pairs={{0,1},{1,0},{2,3},{3,2},{4,5},{5,4},{6,7},{7,6},{8,9},{9,8},{10,11... | collective-permute-start | bytes 196616 | tf_op jit(solution)/shard_map/ppermute | solution.py:22
  80.8 4.0 %collective-permute-start.22 = (f32[64,128]{1,0:T(8,128)S(1)}, f32[64,128]{1,0:T(8,128)S(1)}, u32[]{:S(2)}, u32[]{:S(2)}) collective-permute-start(f32[64,128]{1,0:T(8,128)S(1)} %fusion.11), channel_id=1, source_target_pairs={{0,16},{16,0},{1,17},{17,1},{2,18},{18,2},{3,19},{19,3},{4,20},{20... | collective-permute-start | bytes 98312 | tf_op jit(solution)/shard_map/ppermute | solution.py:22

commit v4 on v3

--- a/solution.py
+++ b/solution.py
@@ -170,7 +170,7 @@
             pltpu.SemaphoreType.DMA((slots, 2)),
             pltpu.SemaphoreType.DMA((slots, 2)),
         ],
-        compiler_params=pltpu.CompilerParams(vmem_limit_bytes=58 * 1024 * 1024),
+        compiler_params=pltpu.CompilerParams(vmem_limit_bytes=48 * 1024 * 1024),
         cost_estimate=pl.CostEstimate(
             flops=16 * slots * tokens * width * block_len,
             transcendentals=slots * tokens * (width // HD) * block_len,
@@ -202,6 +202,7 @@
     return pl.pallas_call(
         functools.partial(tree_kernel, scale),
         out_shape=jax.ShapeDtypeStruct((tokens, width + LANES), jnp.float32),
+        compiler_params=pltpu.CompilerParams(vmem_limit_bytes=8 * 1024 * 1024),
         cost_estimate=pl.CostEstimate(
             flops=16 * tokens * width * tokens, transcendentals=tokens * tokens, bytes_accessed=10**6
         ),
@@ -209,31 +210,55 @@
     )(queries, key_value, tree)
 
 
-def spread(value, width):
-    wide = jnp.broadcast_to(value[..., None], value.shape + (HD,))
-    return wide.reshape(value.shape[:-1] + (width,))
-
-
-def merged_stats(parts, width):
-    heads = width // HD
-    tops = [part[..., width : width + heads] for part in parts]
-    totals = [part[..., width + HD : width + HD + heads] for part in parts]
-    top = functools.reduce(jnp.maximum, tops)
-    scales = [jnp.exp(one - top) for one in tops]
-    total = sum(one * by for one, by in zip(totals, scales))
+def spread(value, pair, shape):
+    lane = lax.broadcasted_iota(jnp.int32, shape, 1)
+    first = jnp.broadcast_to(value[:, 2 * pair : 2 * pair + 1], shape)
+    second = jnp.broadcast_to(value[:, 2 * pair + 1 : 2 * pair + 2], shape)
+    return jnp.where(lane < HD, first, second)
+
+
+def merged_stats(stats):
+    top = functools.reduce(jnp.maximum, stats)
+    scales = [jnp.exp(one - top) for one in stats]
+    total = sum(one * pltpu.roll(by, HD, axis=1) for one, by in zip(stats, scales))
     return scales, top, total
 
 
+def merge_kernel(width, finish, *refs):
+    *parts, out_ref = refs
+    scales, top, total = merged_stats([part[:, width:] for part in parts])
+    if finish:
+        total = pltpu.roll(total, HD, axis=1)
+        scales = [by / total for by in scales]
+    else:
+        lane = lax.broadcasted_iota(jnp.int32, top.shape, 1)
+        out_ref[:, width:] = jnp.where(lane < HD, top, total)
+    shape = (top.shape[0], LANES)
+    for pair in range(width // LANES):
+        columns = slice(pair * LANES, (pair + 1) * LANES)
+        out = sum(part[:, columns] * spread(by, pair, shape) for part, by in zip(parts, scales))
+        out_ref[:, columns] = out.astype(out_ref.dtype)
+
+
+def merged(parts, width, finish):
+    rows = parts[0].shape[0]
+    if finish:
+        shape = jax.ShapeDtypeStruct((rows, width), jnp.bfloat16)
+    else:
+        shape = jax.ShapeDtypeStruct((rows, width + LANES), jnp.float32)
+    return pl.pallas_call(
+        functools.partial(merge_kernel, width, finish),
+        out_shape=shape,
+        compiler_params=pltpu.CompilerParams(vmem_limit_bytes=4 * 1024 * 1024),
+        cost_estimate=pl.CostEstimate(
+            flops=4 * rows * width, transcendentals=rows * LANES, bytes_accessed=12 * rows * width
+        ),
+        name="merge",
+    )(*parts)
+
+
 def merge(one, two, width):
-    scales, top, total = merged_stats([one, two], width)
-    out = sum(part[..., :width] * spread(by, width) for part, by in zip([one, two], scales))
-    gap = jnp.zeros(top.shape[:-1] + (HD - top.shape[-1],), jnp.float32)
-    return jnp.concatenate([out, top, gap, total, gap], axis=-1)
-
-
-def blended(parts, width):
-    scales, _, total = merged_stats(parts, width)
-    return sum(part[..., :width] * spread(by / total, width) for part, by in zip(parts, scales))
+    return merged([one, two], width, False)
 
 
 def patch_kernel(rows, reqs, firsts, starts, sel_ref, *refs):
@@ -339,10 +364,6 @@
     own = own.astype(jnp.int32)
     reqs = own ^ jnp.arange(requests, dtype=jnp.int32)
 
-    slots = jnp.arange(block_count, dtype=jnp.int32)
-    logical = jnp.sum(slots[None, :] * (holder == index).astype(jnp.int32), axis=1)
-    starts = lengths - logical * block_len
-    live = jnp.clip(starts, 0, block_len)
 
     def scattered(value):
         for bit in split[1:]:
@@ -380,6 +401,11 @@
     ancestors = ancestry(lax.dynamic_index_in_dim(late_parents, own, 0, False))
     query_sum = query_sum + swap(query_sum, axis, whole[0])
     query_sum, kv_half, ancestors = tied(query_sum, kv_half, ancestors)
+    late_holder = after(holder, query_sum)
+    slots = jnp.arange(block_count, dtype=jnp.int32)
+    logical = jnp.sum(slots[None, :] * (late_holder == index).astype(jnp.int32), axis=1)
+    starts = lengths - logical * block_len
+    live = jnp.clip(starts, 0, block_len)
     late_lengths, late_ancestors, _ = tied(lengths, ancestors, query_sum)
     depths = (jnp.sum(late_ancestors, axis=1) - 1.0).astype(jnp.int32)
     positions = lax.dynamic_index_in_dim(late_lengths, own, 0, False) + depths
@@ -407,11 +433,12 @@
     kv_own = jnp.concatenate(
         [jnp.where(takes_value, far, part), jnp.where(takes_value, part, far)], axis=1
     )
+    keep = keep.reshape(-1, width + LANES)
+    send = send.reshape(-1, width + LANES)
     cached = merge(keep, swap(send, axis, split[0]), width)
     for bit in split[1:]:
         middle = cached.shape[0] // 2
         cached = merge(cached[:middle], swap(cached[middle:], axis, bit), width)
-    cached = cached[0]
     for bit in whole[:-1]:
         cached = merge(cached, swap(cached, axis, bit), width)
     tree = tree_attention(query_own, kv_own, ancestors, scale)
@@ -420,7 +447,7 @@
     )
     other = swap(cached, axis, whole[-1])
     other, tree = tied(other, tree)
-    attended_own = blended([cached, other, tree], width).astype(jnp.bfloat16)
+    attended_own = merged([cached, other, tree], width, True)
     everyone = gathered(attended_own)
     everyone[1], key_out, value_out = tied(everyone[1], key_out, value_out)
 

time: 85.8 us -> 78.8 us (0.918)
  waiting for transfers between devices: 22.5 us -> 28.3 us
  other arithmetic: 6.51 us -> 2.25 us
  local copies, waits for them, and re-layouts: 6.4 us -> 2.71 us
  starting transfers between devices: 25.3 us -> 22.2 us
  Pallas kernels: 19.3 us -> 17.9 us
    ppermute x23, waiting for transfers between devices: 22.5 us -> 28.3 us  [swap(): return lax.ppermute(value, axis, [(i, i ^ bit) for i in range(size)])]
    ppermute x23, starting transfers between devices: 25.3 us -> 22.2 us  [swap(): return lax.ppermute(value, axis, [(i, i ^ bit) for i in range(size)])]
    add x6 -> x0, other arithmetic: 2.17 us -> none  [the longest x3 1.09 us: merge(): sum((part[..., :width] * spread(by, width) for part, by in zip([one, two]...]
    pallas_call x1, Pallas kernels: 2.23 us -> 0.66 us  [tree_attention(): pl.pallas_call(functools.partial(tree_kernel, scale), out_shape=jax.Shape...]
    broadcast_in_dim x14 -> x0, local copies, waits for them, and re-layouts: 1.5 us -> none  [the longest x11 1.49 us: spread(): wide = jnp.broadcast_to(value[..., None], value.shape + (HD,))]
    pallas_call x0 -> x4, Pallas kernels: none -> 1.45 us  [merged(): pl.pallas_call(functools.partial(merge_kernel, width, finish), out_shape=...]
    pallas_call x1, Pallas kernels: 13.4 us -> 12.1 us  [cache_attention(): pl.pallas_call(functools.partial(cache_kernel, scale), in_specs=[smem, sm...]
    reshape x7 -> x0, local copies, waits for them, and re-layouts: 0.99 us -> none  [spread(): return wide.reshape(value.shape[:-1] + (width,))]
  transfers between devices with their start and end apart: 23 -> 23, of which waited for: 10 -> 16; matrix products, arithmetic and copies ran while one was open for 14% -> 9% of each run, Pallas kernels for 23% -> 22%
where the time goes in v4:
time: 78.8 us; the launch traced here: 78.6 us
  waiting for transfers between devices  28.3 us (36%)
  starting transfers between devices  22.2 us (28%)
  Pallas kernels  17.9 us (23%)
  matrix products  4.1 us (5%)
  local copies, waits for them, and re-layouts  2.71 us (3%)
  other arithmetic  2.25 us (3%)
  between operations  1.11 us (1%)
    ppermute x23, waiting for transfers between devices, swap(): return lax.ppermute(value, axis, [(i, i ^ bit) for i in range(size)])  28.3 us
    ppermute x23, starting transfers between devices, swap(): return lax.ppermute(value, axis, [(i, i ^ bit) for i in range(size)])  22.2 us
    pallas_call x1, Pallas kernels, cache_attention(): pl.pallas_call(functools.partial(cache_kernel, scale), in_specs=[smem, sm...  12.1 us
    pallas_call x1, Pallas kernels, patch(): pl.pallas_call(functools.partial(patch_kernel, rows), in_specs=[smem] * 3...  3.69 us
    dot_general x3, matrix products, first_sum(): jnp.dot(rows, w, preferred_element_type=jnp.float32)  2.53 us
  transfers between devices with their start and end apart: 23, of which 16 were waited for; matrix products, arithmetic and copies ran while one was open for 9% of the time, Pallas kernels for 22%

profile of v4, /device:TPU:0, one launch (start us, length us, event | category | flops | bytes accessed | tf_op | source)
XLA Modules:
  0.0 78.6 jit_solution(17232809434672867591)
XLA Ops:
  0.7 0.8 %dynamic-slice_bitcast_fusion.3 = (bf16[32,128]{1,0:T(8,128)(2,1)S(1)}, bf16[32,128]{1,0:T(8,128)(2,1)S(1)}, bf16[32,128]{1,0:T(8,128)(2,1)S(1)}, bf16[32,128]{1,0:T(8,128)(2,1)S(1)}) fusion(bf16[4,32,128]{2,1,0:T(8,128)(2,1)} %bitcast.79, s32[]{:T(128)S(6)} %select_n.167, s32[]{:T(128)S(6)} %select_n.170, s32[]{:T(128)S(6)} %select_n.169, s32[]{:T(128)S(6)} %select_n.168), kind=kLoop, calls=%fused_computation.54 | loop fusion | bytes 65552 | tf_op jit(solution)/shard_map/jit(dynamic_index_in_dim)/squeeze | solution.py:388
  1.5 0.1 copy-done
  1.6 0.2 fusion.24
  1.8 0.5 collective-permute-start
  2.4 1.1 %collective-permute-done = f32[64,1024]{1,0:T(8,128)S(1)} collective-permute-done((f32[64,1024]{1,0:T(8,128)S(1)}, f32[64,1024]{1,0:T(8,128)S(1)}, u32[]{:S(2)}, u32[]{:S(2)}) %collective-permute-start) | collective-permute-done | bytes 262176 | tf_op jit(solution)/shard_map/ppermute | solution.py:22
  3.6 2.9 %collective-permute-start.1 = (f32[32,1024]{1,0:T(8,128)S(1)}, f32[32,1024]{1,0:T(8,128)S(1)}, u32[]{:S(2)}, u32[]{:S(2)}) collective-permute-start(f32[32,1024]{1,0:T(8,128)S(1)} %slice.114), channel_id=1, source_target_pairs={{0,2},{1,3},{2,0},{3,1},{4,6},{5,7},{6,4},{7,5},{8,10},{9,11},{10,... | collective-permute-start | bytes 393224 | tf_op jit(solution)/shard_map/ppermute | solution.py:22
  6.5 1.2 %fusion.32 = f32[128,1024]{1,0:T(8,128)S(1)} fusion(bf16[128,128]{1,0:T(8,128)(2,1)S(1)} %pad_maximum_fusion.2, bf16[128,1024]{1,0:T(8,128)(2,1)} %param.13), kind=kOutput, calls=%fused_computation.88 | convolution fusion | flops 33554432 | bytes 819200 | tf_op jit(solution)/shard_map/dot_general | solution.py:392
  7.7 1.2 %fusion.33 = f32[128,1024]{1,0:T(8,128)S(1)} fusion(bf16[128,128]{1,0:T(8,128)(2,1)S(1)} %pad_maximum_fusion.2, bf16[128,1024]{1,0:T(8,128)(2,1)} %param.14), kind=kOutput, calls=%fused_computation.89 | convolution fusion | flops 33554432 | bytes 819200 | tf_op jit(solution)/shard_map/dot_general | solution.py:392
  9.0 1.3 %collective-permute-done.1 = f32[32,1024]{1,0:T(8,128)S(1)} collective-permute-done((f32[32,1024]{1,0:T(8,128)S(1)}, f32[32,1024]{1,0:T(8,128)S(1)}, u32[]{:S(2)}, u32[]{:S(2)}) %collective-permute-start.1) | collective-permute-done | bytes 131104 | tf_op jit(solution)/shard_map/ppermute | solution.py:22
  10.3 1.9 %collective-permute-start.2 = (f32[32,1024]{1,0:T(8,128)S(1)}, f32[32,1024]{1,0:T(8,128)S(1)}, u32[]{:S(2)}, u32[]{:S(2)}) collective-permute-start(f32[32,1024]{1,0:T(8,128)S(1)} %slice_add_fusion.2), channel_id=1, source_target_pairs={{0,4},{1,5},{2,6},{3,7},{4,0},{5,1},{6,2},{7,3},{8,12},{9,13},{10,... | collective-permute-start | bytes 393224 | tf_op jit(solution)/shard_map/ppermute | solution.py:22
  12.2 0.7 fusion.19
  12.9 0.2 convolution_minimum_fusion.5
  13.1 0.1 convolution_minimum_fusion.4
  13.3 0.1 convolution_minimum_fusion.3
  13.4 0.1 convolution_minimum_fusion.2
  13.6 0.1 convolution_minimum_fusion.1
  13.7 0.1 convolution_minimum_fusion.tree_ref
  13.9 1.5 %collective-permute-done.2 = f32[32,1024]{1,0:T(8,128)S(1)} collective-permute-done((f32[32,1024]{1,0:T(8,128)S(1)}, f32[32,1024]{1,0:T(8,128)S(1)}, u32[]{:S(2)}, u32[]{:S(2)}) %collective-permute-start.2) | collective-permute-done | bytes 131104 | tf_op jit(solution)/shard_map/ppermute | solution.py:22
  15.5 2.8 %collective-permute-start.4 = (f32[32,1024]{1,0:T(8,128)S(1)}, f32[32,1024]{1,0:T(8,128)S(1)}, u32[]{:S(2)}, u32[]{:S(2)}) collective-permute-start(f32[32,1024]{1,0:T(8,128)S(1)} %add.109), channel_id=1, source_target_pairs={{0,8},{1,9},{2,10},{3,11},{4,12},{5,13},{6,14},{7,15},{8,0},{9,1},... | collective-permute-start | bytes 393224 | tf_op jit(solution)/shard_map/ppermute | solution.py:22
  18.4 0.1 select_reduce_fusion
  18.5 0.6 dynamic_slice.26
  19.1 1.6 %collective-permute-start.8 = (f32[32,2048]{1,0:T(8,128)S(1)}, f32[32,2048]{1,0:T(8,128)S(1)}, u32[]{:S(2)}, u32[]{:S(2)}) collective-permute-start(f32[32,2048]{1,0:T(8,128)S(1)} %slice.102), channel_id=1, source_target_pairs={{0,2},{1,3},{2,0},{3,1},{4,6},{5,7},{6,4},{7,5},{8,10},{9,11},{10,... | collective-permute-start | bytes 786440 | tf_op jit(solution)/shard_map/ppermute | solution.py:22
  20.6 0.1 reduce_sum.19
  20.8 0.7 add_convert_fusion.1
  21.4 0.1 fusion.11
  21.6 1.8 %collective-permute-done.4 = f32[32,1024]{1,0:T(8,128)S(1)} collective-permute-done((f32[32,1024]{1,0:T(8,128)S(1)}, f32[32,1024]{1,0:T(8,128)S(1)}, u32[]{:S(2)}, u32[]{:S(2)}) %collective-permute-start.4) | collective-permute-done | bytes 131104 | tf_op jit(solution)/shard_map/ppermute | solution.py:22
  23.4 0.1 fusion.31
  23.7 0.1 fusion.1.refs_0_.q_ref
  23.8 1.2 %collective-permute-start.5 = (bf16[32,1024]{1,0:T(8,128)(2,1)S(1)}, bf16[32,1024]{1,0:T(8,128)(2,1)S(1)}, u32[]{:S(2)}, u32[]{:S(2)}) collective-permute-start(bf16[32,1024]{1,0:T(8,128)(2,1)S(1)} %fusion.1.refs_0_.q_ref), channel_id=1, source_target_pairs={{0,2},{1,3},{2,0},{3,1},{4,6},{5,7},{6,4},{7,5},{8,10},{9,11},{10,... | collective-permute-start | bytes 196616 | tf_op jit(solution)/shard_map/ppermute | solution.py:22
  25.0 1.3 %collective-permute-done.8 = f32[32,2048]{1,0:T(8,128)S(1)} collective-permute-done((f32[32,2048]{1,0:T(8,128)S(1)}, f32[32,2048]{1,0:T(8,128)S(1)}, u32[]{:S(2)}, u32[]{:S(2)}) %collective-permute-start.8) | collective-permute-done | bytes 262176 | tf_op jit(solution)/shard_map/ppermute | solution.py:22
  26.3 1.4 %collective-permute-start.9 = (f32[32,1024]{1,0:T(8,128)S(1)}, f32[32,1024]{1,0:T(8,128)S(1)}, u32[]{:S(2)}, u32[]{:S(2)}) collective-permute-start(f32[32,1024]{1,0:T(8,128)S(1)} %slice_select_fusion), channel_id=1, source_target_pairs={{0,4},{1,5},{2,6},{3,7},{4,0},{5,1},{6,2},{7,3},{8,12},{9,13},{10,... | collective-permute-start | bytes 393224 | tf_op jit(solution)/shard_map/ppermute | solution.py:22
  27.7 0.4 collective-permute-done.5.refs_1_
  28.2 3.1 %collective-permute-done.9 = f32[32,1024]{1,0:T(8,128)S(1)} collective-permute-done((f32[32,1024]{1,0:T(8,128)S(1)}, f32[32,1024]{1,0:T(8,128)S(1)}, u32[]{:S(2)}, u32[]{:S(2)}) %collective-permute-start.9) | collective-permute-done | bytes 131104 | tf_op jit(solution)/shard_map/ppermute | solution.py:22
  31.4 0.8 %collective-permute-start.10 = (f32[32,1024]{1,0:T(8,128)S(1)}, f32[32,1024]{1,0:T(8,128)S(1)}, u32[]{:S(2)}, u32[]{:S(2)}) collective-permute-start(f32[32,1024]{1,0:T(8,128)S(1)} %select_add_fusion), channel_id=1, source_target_pairs={{0,8},{1,9},{2,10},{3,11},{4,12},{5,13},{6,14},{7,15},{8,0},{9,1},... | collective-permute-start | bytes 393224 | tf_op jit(solution)/shard_map/ppermute | solution.py:22
  32.2 12.1 %cache_attention.1 = (f32[2,32,1152]{2,1,0:T(8,128)S(1)}, f32[2,32,1152]{2,1,0:T(8,128)S(1)}, bf16[4,1024,1024]{2,1,0:T(8,128)(2,1)}, bf16[4,1024,1024]{2,1,0:T(8,128)(2,1)}) custom-call(s32[4]{0:T(128)S(1)} %iota_xor_fusion.reqs, s32[4]{0:T(128)S(1)} %broadcast_clamp_fusion.live, bf16[32,1024]{1,0:T(8,128)(2,1)S(1)} %fusion.1.refs_0_.q_ref, ...), custom_call_target="tpu_custom_call" | custom-call | flops 2147483648 | bytes 33554432 | tf_op jit(solution)/shard_map/cache_attention/pallas_call | solution.py:162
  44.6 0.1 fusion.4
  44.8 2.1 %collective-permute-start.15 = (bf16[32,1024]{1,0:T(8,128)(2,1)S(1)}, bf16[32,1024]{1,0:T(8,128)(2,1)S(1)}, u32[]{:S(2)}, u32[]{:S(2)}) collective-permute-start(bf16[32,1024]{1,0:T(8,128)(2,1)S(1)} %fusion.4), channel_id=1, source_target_pairs={{0,4},{1,5},{2,6},{3,7},{4,0},{5,1},{6,2},{7,3},{8,12},{9,13},{10,... | collective-permute-start | bytes 196616 | tf_op jit(solution)/shard_map/ppermute | solution.py:22
  46.9 0.4 merge.4
  47.3 0.6 collective-permute-start.12
  47.9 1.7 %collective-permute-done.15 = bf16[32,1024]{1,0:T(8,128)(2,1)S(1)} collective-permute-done((bf16[32,1024]{1,0:T(8,128)(2,1)S(1)}, bf16[32,1024]{1,0:T(8,128)(2,1)S(1)}, u32[]{:S(2)}, u32[]{:S(2)}) %collective-permute-start.15) | collective-permute-done | bytes 65568 | tf_op jit(solution)/shard_map/ppermute | solution.py:22
  49.6 3.7 %collective-permute-done.12.refs_1_ = f32[32,1152]{1,0:T(8,128)S(1)} collective-permute-done((f32[32,1152]{1,0:T(8,128)S(1)}, f32[32,1152]{1,0:T(8,128)S(1)}, u32[]{:S(2)}, u32[]{:S(2)}) %collective-permute-start.12) | collective-permute-done | bytes 147488 | tf_op jit(solution)/shard_map/ppermute | solution.py:22
  53.3 0.3 merge.5.refs_0_
  53.6 1.2 %collective-permute-start.13 = (f32[32,1152]{1,0:T(8,128)S(1)}, f32[32,1152]{1,0:T(8,128)S(1)}, u32[]{:S(2)}, u32[]{:S(2)}) collective-permute-start(f32[32,1152]{1,0:T(8,128)S(1)} %merge.5.refs_0_), channel_id=1, source_target_pairs={{0,4},{1,5},{2,6},{3,7},{4,0},{5,1},{6,2},{7,3},{8,12},{9,13},{10,... | collective-permute-start | bytes 442376 | tf_op jit(solution)/shard_map/ppermute | solution.py:22
  54.8 0.6 collective-permute-start.19
  55.4 3.4 %collective-permute-done.13.refs_1_ = f32[32,1152]{1,0:T(8,128)S(1)} collective-permute-done((f32[32,1152]{1,0:T(8,128)S(1)}, f32[32,1152]{1,0:T(8,128)S(1)}, u32[]{:S(2)}, u32[]{:S(2)}) %collective-permute-start.13) | collective-permute-done | bytes 147488 | tf_op jit(solution)/shard_map/ppermute | solution.py:22
  58.8 0.3 merge.6.refs_0_
  59.1 1.5 %collective-permute-start.14 = (f32[32,1152]{1,0:T(8,128)S(1)}, f32[32,1152]{1,0:T(8,128)S(1)}, u32[]{:S(2)}, u32[]{:S(2)}) collective-permute-start(f32[32,1152]{1,0:T(8,128)S(1)} %merge.6.refs_0_), channel_id=1, source_target_pairs={{0,8},{1,9},{2,10},{3,11},{4,12},{5,13},{6,14},{7,15},{8,0},{9,1},... | collective-permute-start | bytes 442376 | tf_op jit(solution)/shard_map/ppermute | solution.py:22
  60.6 0.5 collective-permute-start.21
  61.2 0.7 tree_attention.1.refs_2_
  61.8 0.1 collective-permute-done.20.refs_2_
  62.0 0.2 collective-permute-done.21.refs_3_
  62.2 3.7 %patch.1 = (bf16[4,1024,1024]{2,1,0:T(8,128)(2,1)}, bf16[4,1024,1024]{2,1,0:T(8,128)(2,1)}) custom-call(s32[4]{0:T(128)S(1)} %iota_xor_fusion.reqs, s32[4]{0:T(128)S(1)} %get-tuple-element.59.firsts, s32[4]{0:T(128)S(1)} %get-tuple-element.60.starts, ...), custom_call_target="tpu_custom_call", output_to_operand_aliasing={{0}: (8, {}), {1}: (9, {})} | custom-call | bytes 1572864 | tf_op jit(solution)/shard_map/patch/pallas_call | solution.py:318
  65.9 1.4 %collective-permute-done.14.refs_1_ = f32[32,1152]{1,0:T(8,128)S(1)} collective-permute-done((f32[32,1152]{1,0:T(8,128)S(1)}, f32[32,1152]{1,0:T(8,128)S(1)}, u32[]{:S(2)}, u32[]{:S(2)}) %collective-permute-start.14) | collective-permute-done | bytes 147488 | tf_op jit(solution)/shard_map/ppermute | solution.py:22
  67.2 0.5 merge.7
  67.8 0.6 collective-permute-start.16
  68.4 0.2 fusion.36
  68.6 3.7 %collective-permute-done.16 = bf16[32,1024]{1,0:T(8,128)(2,1)S(1)} collective-permute-done((bf16[32,1024]{1,0:T(8,128)(2,1)S(1)}, bf16[32,1024]{1,0:T(8,128)(2,1)S(1)}, u32[]{:S(2)}, u32[]{:S(2)}) %collective-permute-start.16) | collective-permute-done | bytes 65568 | tf_op jit(solution)/shard_map/ppermute | solution.py:22
  72.3 0.2 fusion.35
  72.6 0.2 fusion.34
  72.7 1.1 %collective-permute-done.17 = bf16[32,1024]{1,0:T(8,128)(2,1)S(1)} collective-permute-done((bf16[32,1024]{1,0:T(8,128)(2,1)S(1)}, bf16[32,1024]{1,0:T(8,128)(2,1)S(1)}, u32[]{:S(2)}, u32[]{:S(2)}) %collective-permute-start.17) | collective-permute-done | bytes 65568 | tf_op jit(solution)/shard_map/ppermute | solution.py:22
  73.8 0.2 select_select_fusion.3
  74.0 1.6 %collective-permute-start.22 = (f32[64,128]{1,0:T(8,128)S(1)}, f32[64,128]{1,0:T(8,128)S(1)}, u32[]{:S(2)}, u32[]{:S(2)}) collective-permute-start(f32[64,128]{1,0:T(8,128)S(1)} %fusion.7), channel_id=1, source_target_pairs={{0,16},{16,0},{1,17},{17,1},{2,18},{18,2},{3,19},{19,3},{4,20},{20... | collective-permute-start | bytes 98312 | tf_op jit(solution)/shard_map/ppermute | solution.py:22
  75.6 2.4 %collective-permute-done.22 = f32[64,128]{1,0:T(8,128)S(1)} collective-permute-done((f32[64,128]{1,0:T(8,128)S(1)}, f32[64,128]{1,0:T(8,128)S(1)}, u32[]{:S(2)}, u32[]{:S(2)}) %collective-permute-start.22) | collective-permute-done | bytes 32800 | tf_op jit(solution)/shard_map/ppermute | solution.py:22
  78.0 0.6 add_convert_fusion
  (56 shorter events, 1.2 us)
Async XLA Ops:
  0.6 1.0 %copy-start = (bf16[128,1024]{1,0:T(8,128)(2,1)S(1)}, bf16[128,1024]{1,0:T(8,128)(2,1)}, u32[]{:S(2)}) copy-start(bf16[128,1024]{1,0:T(8,128)(2,1)} %param.12) | copy-start | bytes 786436
  0.6 17.7 %copy-start.3 = (s32[4,16]{1,0:T(4,128)S(1)}, s32[4,16]{1,0:T(4,128)}, u32[]{:S(2)}) copy-start(s32[4,16]{1,0:T(4,128)} %param.20) | copy-start | bytes 772
  0.7 17.8 %copy-start.4 = (s32[4]{0:T(128)S(1)}, s32[4]{0:T(128)}, u32[]{:S(2)}) copy-start(s32[4]{0:T(128)} %param.19) | copy-start | bytes 52
  1.8 1.7 %collective-permute-start = (f32[64,1024]{1,0:T(8,128)S(1)}, f32[64,1024]{1,0:T(8,128)S(1)}, u32[]{:S(2)}, u32[]{:S(2)}) collective-permute-start(f32[64,1024]{1,0:T(8,128)S(1)} %slice.112), channel_id=1, source_target_pairs={{0,1},{1,0},{2,3},{3,2},{4,5},{5,4},{6,7},{7,6},{8,9},{9,8},{10,11... | collective-permute-start | bytes 786440 | tf_op jit(solution)/shard_map/ppermute | solution.py:22
  3.6 6.7 %collective-permute-start.1 = (f32[32,1024]{1,0:T(8,128)S(1)}, f32[32,1024]{1,0:T(8,128)S(1)}, u32[]{:S(2)}, u32[]{:S(2)}) collective-permute-start(f32[32,1024]{1,0:T(8,128)S(1)} %slice.114), channel_id=1, source_target_pairs={{0,2},{1,3},{2,0},{3,1},{4,6},{5,7},{6,4},{7,5},{8,10},{9,11},{10,... | collective-permute-start | bytes 393224 | tf_op jit(solution)/shard_map/ppermute | solution.py:22
  9.0 6.5 %collective-permute-start.3 = (f32[64,2048]{1,0:T(8,128)S(1)}, f32[64,2048]{1,0:T(8,128)S(1)}, u32[]{:S(2)}, u32[]{:S(2)}) collective-permute-start(f32[64,2048]{1,0:T(8,128)S(1)} %pad_maximum_fusion), channel_id=1, source_target_pairs={{0,1},{1,0},{2,3},{3,2},{4,5},{5,4},{6,7},{7,6},{8,9},{9,8},{10,11... | collective-permute-start | bytes 1572872 | tf_op jit(solution)/shard_map/ppermute | solution.py:22
  10.3 5.1 %collective-permute-start.2 = (f32[32,1024]{1,0:T(8,128)S(1)}, f32[32,1024]{1,0:T(8,128)S(1)}, u32[]{:S(2)}, u32[]{:S(2)}) collective-permute-start(f32[32,1024]{1,0:T(8,128)S(1)} %slice_add_fusion.2), channel_id=1, source_target_pairs={{0,4},{1,5},{2,6},{3,7},{4,0},{5,1},{6,2},{7,3},{8,12},{9,13},{10,... | collective-permute-start | bytes 393224 | tf_op jit(solution)/shard_map/ppermute | solution.py:22
  15.5 7.9 %collective-permute-start.4 = (f32[32,1024]{1,0:T(8,128)S(1)}, f32[32,1024]{1,0:T(8,128)S(1)}, u32[]{:S(2)}, u32[]{:S(2)}) collective-permute-start(f32[32,1024]{1,0:T(8,128)S(1)} %add.109), channel_id=1, source_target_pairs={{0,8},{1,9},{2,10},{3,11},{4,12},{5,13},{6,14},{7,15},{8,0},{9,1},... | collective-permute-start | bytes 393224 | tf_op jit(solution)/shard_map/ppermute | solution.py:22
  19.1 7.1 %collective-permute-start.8 = (f32[32,2048]{1,0:T(8,128)S(1)}, f32[32,2048]{1,0:T(8,128)S(1)}, u32[]{:S(2)}, u32[]{:S(2)}) collective-permute-start(f32[32,2048]{1,0:T(8,128)S(1)} %slice.102), channel_id=1, source_target_pairs={{0,2},{1,3},{2,0},{3,1},{4,6},{5,7},{6,4},{7,5},{8,10},{9,11},{10,... | collective-permute-start | bytes 786440 | tf_op jit(solution)/shard_map/ppermute | solution.py:22
  23.8 4.3 %collective-permute-start.5 = (bf16[32,1024]{1,0:T(8,128)(2,1)S(1)}, bf16[32,1024]{1,0:T(8,128)(2,1)S(1)}, u32[]{:S(2)}, u32[]{:S(2)}) collective-permute-start(bf16[32,1024]{1,0:T(8,128)(2,1)S(1)} %fusion.1.refs_0_.q_ref), channel_id=1, source_target_pairs={{0,2},{1,3},{2,0},{3,1},{4,6},{5,7},{6,4},{7,5},{8,10},{9,11},{10,... | collective-permute-start | bytes 196616 | tf_op jit(solution)/shard_map/ppermute | solution.py:22
  26.3 5.0 %collective-permute-start.9 = (f32[32,1024]{1,0:T(8,128)S(1)}, f32[32,1024]{1,0:T(8,128)S(1)}, u32[]{:S(2)}, u32[]{:S(2)}) collective-permute-start(f32[32,1024]{1,0:T(8,128)S(1)} %slice_select_fusion), channel_id=1, source_target_pairs={{0,4},{1,5},{2,6},{3,7},{4,0},{5,1},{6,2},{7,3},{8,12},{9,13},{10,... | collective-permute-start | bytes 393224 | tf_op jit(solution)/shard_map/ppermute | solution.py:22
  27.7 3.7 %collective-permute-start.6 = (bf16[32,1024]{1,0:T(8,128)(2,1)S(1)}, bf16[32,1024]{1,0:T(8,128)(2,1)S(1)}, u32[]{:S(2)}, u32[]{:S(2)}) collective-permute-start(bf16[32,1024]{1,0:T(8,128)(2,1)S(1)} %fusion.1.refs_0_.q_ref), channel_id=1, source_target_pairs={{0,1},{1,0},{2,3},{3,2},{4,5},{5,4},{6,7},{7,6},{8,9},{9,8},{10,11... | collective-permute-start | bytes 196616 | tf_op jit(solution)/shard_map/ppermute | solution.py:22
  28.1 3.3 %collective-permute-start.7 = (bf16[32,1024]{1,0:T(8,128)(2,1)S(1)}, bf16[32,1024]{1,0:T(8,128)(2,1)S(1)}, u32[]{:S(2)}, u32[]{:S(2)}) collective-permute-start(bf16[32,1024]{1,0:T(8,128)(2,1)S(1)} %collective-permute-done.5.refs_1_), channel_id=1, source_target_pairs={{0,1},{1,0},{2,3},{3,2},{4,5},{5,4},{6,7},{7,6},{8,9},{9,8},{10,11... | collective-permute-start | bytes 196616 | tf_op jit(solution)/shard_map/ppermute | solution.py:22
  31.3 29.8 %copy-start.2 = (s32[4,32,32]{2,1,0:T(8,128)S(1)}, s32[4,32,32]{2,1,0:T(8,128)}, u32[]{:S(2)}) copy-start(s32[4,32,32]{2,1,0:T(8,128)} %param.21) | copy-start | bytes 49156
  31.4 13.0 %collective-permute-start.10 = (f32[32,1024]{1,0:T(8,128)S(1)}, f32[32,1024]{1,0:T(8,128)S(1)}, u32[]{:S(2)}, u32[]{:S(2)}) collective-permute-start(f32[32,1024]{1,0:T(8,128)S(1)} %select_add_fusion), channel_id=1, source_target_pairs={{0,8},{1,9},{2,10},{3,11},{4,12},{5,13},{6,14},{7,15},{8,0},{9,1},... | collective-permute-start | bytes 393224 | tf_op jit(solution)/shard_map/ppermute | solution.py:22
  44.4 2.5 %collective-permute-start.11 = (f32[64,1152]{1,0:T(8,128)S(1)}, f32[64,1152]{1,0:T(8,128)S(1)}, u32[]{:S(2)}, u32[]{:S(2)}) collective-permute-start(f32[64,1152]{1,0:T(8,128)S(1)} %bitcast.72), channel_id=1, source_target_pairs={{0,1},{1,0},{2,3},{3,2},{4,5},{5,4},{6,7},{7,6},{8,9},{9,8},{10,11... | collective-permute-start | bytes 884744 | tf_op jit(solution)/shard_map/ppermute | solution.py:22
  44.8 4.8 %collective-permute-start.15 = (bf16[32,1024]{1,0:T(8,128)(2,1)S(1)}, bf16[32,1024]{1,0:T(8,128)(2,1)S(1)}, u32[]{:S(2)}, u32[]{:S(2)}) collective-permute-start(bf16[32,1024]{1,0:T(8,128)(2,1)S(1)} %fusion.4), channel_id=1, source_target_pairs={{0,4},{1,5},{2,6},{3,7},{4,0},{5,1},{6,2},{7,3},{8,12},{9,13},{10,... | collective-permute-start | bytes 196616 | tf_op jit(solution)/shard_map/ppermute | solution.py:22
  47.3 6.0 %collective-permute-start.12 = (f32[32,1152]{1,0:T(8,128)S(1)}, f32[32,1152]{1,0:T(8,128)S(1)}, u32[]{:S(2)}, u32[]{:S(2)}) collective-permute-start(f32[32,1152]{1,0:T(8,128)S(1)} %get-tuple-element.65), channel_id=1, source_target_pairs={{0,2},{1,3},{2,0},{3,1},{4,6},{5,7},{6,4},{7,5},{8,10},{9,11},{10,... | collective-permute-start | bytes 442376 | tf_op jit(solution)/shard_map/ppermute | solution.py:22
  53.6 5.2 %collective-permute-start.13 = (f32[32,1152]{1,0:T(8,128)S(1)}, f32[32,1152]{1,0:T(8,128)S(1)}, u32[]{:S(2)}, u32[]{:S(2)}) collective-permute-start(f32[32,1152]{1,0:T(8,128)S(1)} %merge.5.refs_0_), channel_id=1, source_target_pairs={{0,4},{1,5},{2,6},{3,7},{4,0},{5,1},{6,2},{7,3},{8,12},{9,13},{10,... | collective-permute-start | bytes 442376 | tf_op jit(solution)/shard_map/ppermute | solution.py:22
  54.8 5.8 %collective-permute-start.19 = (bf16[32,2048]{1,0:T(8,128)(2,1)S(1)}, bf16[32,2048]{1,0:T(8,128)(2,1)S(1)}, u32[]{:S(2)}, u32[]{:S(2)}) collective-permute-start(bf16[32,2048]{1,0:T(8,128)(2,1)S(1)} %pad_maximum_fusion.1.kv_ref.refs_0_), channel_id=1, source_target_pairs={{0,2},{1,3},{2,0},{3,1},{4,6},{5,7},{6,4},{7,5},{8,10},{9,11},{10,... | collective-permute-start | bytes 393224 | tf_op jit(solution)/shard_map/ppermute | solution.py:22
  59.1 8.1 %collective-permute-start.14 = (f32[32,1152]{1,0:T(8,128)S(1)}, f32[32,1152]{1,0:T(8,128)S(1)}, u32[]{:S(2)}, u32[]{:S(2)}) collective-permute-start(f32[32,1152]{1,0:T(8,128)S(1)} %merge.6.refs_0_), channel_id=1, source_target_pairs={{0,8},{1,9},{2,10},{3,11},{4,12},{5,13},{6,14},{7,15},{8,0},{9,1},... | collective-permute-start | bytes 442376 | tf_op jit(solution)/shard_map/ppermute | solution.py:22
  60.6 1.3 %collective-permute-start.20 = (bf16[32,2048]{1,0:T(8,128)(2,1)S(1)}, bf16[32,2048]{1,0:T(8,128)(2,1)S(1)}, u32[]{:S(2)}, u32[]{:S(2)}) collective-permute-start(bf16[32,2048]{1,0:T(8,128)(2,1)S(1)} %pad_maximum_fusion.1.kv_ref.refs_0_), channel_id=1, source_target_pairs={{0,1},{1,0},{2,3},{3,2},{4,5},{5,4},{6,7},{7,6},{8,9},{9,8},{10,11... | collective-permute-start | bytes 393224 | tf_op jit(solution)/shard_map/ppermute | solution.py:22
  60.6 1.5 %collective-permute-start.21 = (bf16[32,2048]{1,0:T(8,128)(2,1)S(1)}, bf16[32,2048]{1,0:T(8,128)(2,1)S(1)}, u32[]{:S(2)}, u32[]{:S(2)}) collective-permute-start(bf16[32,2048]{1,0:T(8,128)(2,1)S(1)} %collective-permute-done.19.refs_1_), channel_id=1, source_target_pairs={{0,1},{1,0},{2,3},{3,2},{4,5},{5,4},{6,7},{7,6},{8,9},{9,8},{10,11... | collective-permute-start | bytes 393224 | tf_op jit(solution)/shard_map/ppermute | solution.py:22
  62.2 6.2 %copy-start.1 = (bf16[1024,128]{1,0:T(8,128)(2,1)S(1)}, bf16[1024,128]{1,0:T(8,128)(2,1)}, u32[]{:S(2)}) copy-start(bf16[1024,128]{1,0:T(8,128)(2,1)} %param.15) | copy-start | bytes 786436
  67.7 4.8 %collective-permute-start.18 = (bf16[32,1024]{1,0:T(8,128)(2,1)S(1)}, bf16[32,1024]{1,0:T(8,128)(2,1)S(1)}, u32[]{:S(2)}, u32[]{:S(2)}) collective-permute-start(bf16[32,1024]{1,0:T(8,128)(2,1)S(1)} %merge.7), channel_id=1, source_target_pairs={{0,1},{1,0},{2,3},{3,2},{4,5},{5,4},{6,7},{7,6},{8,9},{9,8},{10,11... | collective-permute-start | bytes 196616 | tf_op jit(solution)/shard_map/ppermute | solution.py:22
  67.8 4.5 %collective-permute-start.16 = (bf16[32,1024]{1,0:T(8,128)(2,1)S(1)}, bf16[32,1024]{1,0:T(8,128)(2,1)S(1)}, u32[]{:S(2)}, u32[]{:S(2)}) collective-permute-start(bf16[32,1024]{1,0:T(8,128)(2,1)S(1)} %merge.7), channel_id=1, source_target_pairs={{0,2},{1,3},{2,0},{3,1},{4,6},{5,7},{6,4},{7,5},{8,10},{9,11},{10,... | collective-permute-start | bytes 196616 | tf_op jit(solution)/shard_map/ppermute | solution.py:22
  72.5 1.3 %collective-permute-start.17 = (bf16[32,1024]{1,0:T(8,128)(2,1)S(1)}, bf16[32,1024]{1,0:T(8,128)(2,1)S(1)}, u32[]{:S(2)}, u32[]{:S(2)}) collective-permute-start(bf16[32,1024]{1,0:T(8,128)(2,1)S(1)} %collective-permute-done.16), channel_id=1, source_target_pairs={{0,1},{1,0},{2,3},{3,2},{4,5},{5,4},{6,7},{7,6},{8,9},{9,8},{10,11... | collective-permute-start | bytes 196616 | tf_op jit(solution)/shard_map/ppermute | solution.py:22
  74.0 4.0 %collective-permute-start.22 = (f32[64,128]{1,0:T(8,128)S(1)}, f32[64,128]{1,0:T(8,128)S(1)}, u32[]{:S(2)}, u32[]{:S(2)}) collective-permute-start(f32[64,128]{1,0:T(8,128)S(1)} %fusion.7), channel_id=1, source_target_pairs={{0,16},{16,0},{1,17},{17,1},{2,18},{18,2},{3,19},{19,3},{4,20},{20... | collective-permute-start | bytes 98312 | tf_op jit(solution)/shard_map/ppermute | solution.py:22

commit v5 on v4

--- a/solution.py
+++ b/solution.py
@@ -433,12 +433,15 @@
     kv_own = jnp.concatenate(
         [jnp.where(takes_value, far, part), jnp.where(takes_value, part, far)], axis=1
     )
-    keep = keep.reshape(-1, width + LANES)
-    send = send.reshape(-1, width + LANES)
-    cached = merge(keep, swap(send, axis, split[0]), width)
+    pieces = [[keep[k]] for k in range(keep.shape[0])]
+    arrived = swap(send, axis, split[0])
+    for k, piece in enumerate(pieces):
+        piece.append(arrived[k])
     for bit in split[1:]:
-        middle = cached.shape[0] // 2
-        cached = merge(cached[:middle], swap(cached[middle:], axis, bit), width)
+        middle = len(pieces) // 2
+        sent = [merged(piece, width, False) for piece in pieces[middle:]]
+        pieces = [piece + [swap(one, axis, bit)] for piece, one in zip(pieces[:middle], sent)]
+    cached = merged(pieces[0], width, False)
     for bit in whole[:-1]:
         cached = merge(cached, swap(cached, axis, bit), width)
     tree = tree_attention(query_own, kv_own, ancestors, scale)

time: 78.8 us -> 78.8 us (level)
  no operation moved by 1% of the time
where the time goes in v5:
time: 78.8 us; the launch traced here: 78.6 us
  waiting for transfers between devices  28.2 us (36%)
  starting transfers between devices  22.3 us (28%)
  Pallas kernels  17.9 us (23%)
  matrix products  4.1 us (5%)
  local copies, waits for them, and re-layouts  2.73 us (3%)
  other arithmetic  2.25 us (3%)
  between operations  1.11 us (1%)
    ppermute x23, waiting for transfers between devices, swap(): return lax.ppermute(value, axis, [(i, i ^ bit) for i in range(size)])  28.2 us
    ppermute x23, starting transfers between devices, swap(): return lax.ppermute(value, axis, [(i, i ^ bit) for i in range(size)])  22.3 us
    pallas_call x1, Pallas kernels, cache_attention(): pl.pallas_call(functools.partial(cache_kernel, scale), in_specs=[smem, sm...  12.1 us
    pallas_call x1, Pallas kernels, patch(): pl.pallas_call(functools.partial(patch_kernel, rows), in_specs=[smem] * 3...  3.69 us
    dot_general x3, matrix products, first_sum(): jnp.dot(rows, w, preferred_element_type=jnp.float32)  2.53 us
  transfers between devices with their start and end apart: 23, of which 16 were waited for; matrix products, arithmetic and copies ran while one was open for 9% of the time, Pallas kernels for 22%

profile of v5, /device:TPU:0, one launch (start us, length us, event | category | flops | bytes accessed | tf_op | source)
XLA Modules:
  0.0 78.6 jit_solution(11022288786191487882)
XLA Ops:
  0.7 0.8 %dynamic-slice_bitcast_fusion.3 = (bf16[32,128]{1,0:T(8,128)(2,1)S(1)}, bf16[32,128]{1,0:T(8,128)(2,1)S(1)}, bf16[32,128]{1,0:T(8,128)(2,1)S(1)}, bf16[32,128]{1,0:T(8,128)(2,1)S(1)}) fusion(bf16[4,32,128]{2,1,0:T(8,128)(2,1)} %bitcast.83, s32[]{:T(128)S(6)} %select_n.167, s32[]{:T(128)S(6)} %select_n.170, s32[]{:T(128)S(6)} %select_n.169, s32[]{:T(128)S(6)} %select_n.168), kind=kLoop, calls=%fused_computation.58 | loop fusion | bytes 65552 | tf_op jit(solution)/shard_map/jit(dynamic_index_in_dim)/squeeze | solution.py:388
  1.5 0.1 copy-done
  1.6 0.2 fusion.24
  1.8 0.5 collective-permute-start
  2.4 1.1 %collective-permute-done = f32[64,1024]{1,0:T(8,128)S(1)} collective-permute-done((f32[64,1024]{1,0:T(8,128)S(1)}, f32[64,1024]{1,0:T(8,128)S(1)}, u32[]{:S(2)}, u32[]{:S(2)}) %collective-permute-start) | collective-permute-done | bytes 262176 | tf_op jit(solution)/shard_map/ppermute | solution.py:22
  3.6 2.9 %collective-permute-start.1 = (f32[32,1024]{1,0:T(8,128)S(1)}, f32[32,1024]{1,0:T(8,128)S(1)}, u32[]{:S(2)}, u32[]{:S(2)}) collective-permute-start(f32[32,1024]{1,0:T(8,128)S(1)} %slice.122), channel_id=1, source_target_pairs={{0,2},{1,3},{2,0},{3,1},{4,6},{5,7},{6,4},{7,5},{8,10},{9,11},{10,... | collective-permute-start | bytes 393224 | tf_op jit(solution)/shard_map/ppermute | solution.py:22
  6.5 1.2 %fusion.31 = f32[128,1024]{1,0:T(8,128)S(1)} fusion(bf16[128,128]{1,0:T(8,128)(2,1)S(1)} %pad_maximum_fusion.2, bf16[128,1024]{1,0:T(8,128)(2,1)} %param.13), kind=kOutput, calls=%fused_computation.91 | convolution fusion | flops 33554432 | bytes 819200 | tf_op jit(solution)/shard_map/dot_general | solution.py:392
  7.7 1.2 %fusion.32 = f32[128,1024]{1,0:T(8,128)S(1)} fusion(bf16[128,128]{1,0:T(8,128)(2,1)S(1)} %pad_maximum_fusion.2, bf16[128,1024]{1,0:T(8,128)(2,1)} %param.14), kind=kOutput, calls=%fused_computation.92 | convolution fusion | flops 33554432 | bytes 819200 | tf_op jit(solution)/shard_map/dot_general | solution.py:392
  9.0 1.3 %collective-permute-done.1 = f32[32,1024]{1,0:T(8,128)S(1)} collective-permute-done((f32[32,1024]{1,0:T(8,128)S(1)}, f32[32,1024]{1,0:T(8,128)S(1)}, u32[]{:S(2)}, u32[]{:S(2)}) %collective-permute-start.1) | collective-permute-done | bytes 131104 | tf_op jit(solution)/shard_map/ppermute | solution.py:22
  10.3 1.9 %collective-permute-start.2 = (f32[32,1024]{1,0:T(8,128)S(1)}, f32[32,1024]{1,0:T(8,128)S(1)}, u32[]{:S(2)}, u32[]{:S(2)}) collective-permute-start(f32[32,1024]{1,0:T(8,128)S(1)} %slice_add_fusion.2), channel_id=1, source_target_pairs={{0,4},{1,5},{2,6},{3,7},{4,0},{5,1},{6,2},{7,3},{8,12},{9,13},{10,... | collective-permute-start | bytes 393224 | tf_op jit(solution)/shard_map/ppermute | solution.py:22
  12.2 0.7 fusion.19
  12.9 0.2 convolution_minimum_fusion.5
  13.1 0.1 convolution_minimum_fusion.4
  13.3 0.1 convolution_minimum_fusion.3
  13.4 0.1 convolution_minimum_fusion.2
  13.6 0.1 convolution_minimum_fusion.1
  13.7 0.1 convolution_minimum_fusion.tree_ref
  13.9 1.5 %collective-permute-done.2 = f32[32,1024]{1,0:T(8,128)S(1)} collective-permute-done((f32[32,1024]{1,0:T(8,128)S(1)}, f32[32,1024]{1,0:T(8,128)S(1)}, u32[]{:S(2)}, u32[]{:S(2)}) %collective-permute-start.2) | collective-permute-done | bytes 131104 | tf_op jit(solution)/shard_map/ppermute | solution.py:22
  15.5 2.8 %collective-permute-start.4 = (f32[32,1024]{1,0:T(8,128)S(1)}, f32[32,1024]{1,0:T(8,128)S(1)}, u32[]{:S(2)}, u32[]{:S(2)}) collective-permute-start(f32[32,1024]{1,0:T(8,128)S(1)} %add.109), channel_id=1, source_target_pairs={{0,8},{1,9},{2,10},{3,11},{4,12},{5,13},{6,14},{7,15},{8,0},{9,1},... | collective-permute-start | bytes 393224 | tf_op jit(solution)/shard_map/ppermute | solution.py:22
  18.4 0.1 select_reduce_fusion
  18.5 0.6 dynamic_slice.26
  19.1 1.6 %collective-permute-start.8 = (f32[32,2048]{1,0:T(8,128)S(1)}, f32[32,2048]{1,0:T(8,128)S(1)}, u32[]{:S(2)}, u32[]{:S(2)}) collective-permute-start(f32[32,2048]{1,0:T(8,128)S(1)} %slice.108), channel_id=1, source_target_pairs={{0,2},{1,3},{2,0},{3,1},{4,6},{5,7},{6,4},{7,5},{8,10},{9,11},{10,... | collective-permute-start | bytes 786440 | tf_op jit(solution)/shard_map/ppermute | solution.py:22
  20.6 0.1 reduce_sum.19
  20.8 0.7 add_convert_fusion.1
  21.4 0.1 fusion.11
  21.6 1.8 %collective-permute-done.4 = f32[32,1024]{1,0:T(8,128)S(1)} collective-permute-done((f32[32,1024]{1,0:T(8,128)S(1)}, f32[32,1024]{1,0:T(8,128)S(1)}, u32[]{:S(2)}, u32[]{:S(2)}) %collective-permute-start.4) | collective-permute-done | bytes 131104 | tf_op jit(solution)/shard_map/ppermute | solution.py:22
  23.7 0.1 fusion.1.refs_0_.q_ref
  23.8 1.2 %collective-permute-start.5 = (bf16[32,1024]{1,0:T(8,128)(2,1)S(1)}, bf16[32,1024]{1,0:T(8,128)(2,1)S(1)}, u32[]{:S(2)}, u32[]{:S(2)}) collective-permute-start(bf16[32,1024]{1,0:T(8,128)(2,1)S(1)} %fusion.1.refs_0_.q_ref), channel_id=1, source_target_pairs={{0,2},{1,3},{2,0},{3,1},{4,6},{5,7},{6,4},{7,5},{8,10},{9,11},{10,... | collective-permute-start | bytes 196616 | tf_op jit(solution)/shard_map/ppermute | solution.py:22
  25.0 1.3 %collective-permute-done.8 = f32[32,2048]{1,0:T(8,128)S(1)} collective-permute-done((f32[32,2048]{1,0:T(8,128)S(1)}, f32[32,2048]{1,0:T(8,128)S(1)}, u32[]{:S(2)}, u32[]{:S(2)}) %collective-permute-start.8) | collective-permute-done | bytes 262176 | tf_op jit(solution)/shard_map/ppermute | solution.py:22
  26.3 1.4 %collective-permute-start.9 = (f32[32,1024]{1,0:T(8,128)S(1)}, f32[32,1024]{1,0:T(8,128)S(1)}, u32[]{:S(2)}, u32[]{:S(2)}) collective-permute-start(f32[32,1024]{1,0:T(8,128)S(1)} %slice_select_fusion), channel_id=1, source_target_pairs={{0,4},{1,5},{2,6},{3,7},{4,0},{5,1},{6,2},{7,3},{8,12},{9,13},{10,... | collective-permute-start | bytes 393224 | tf_op jit(solution)/shard_map/ppermute | solution.py:22
  27.7 0.4 collective-permute-done.5.refs_1_
  28.2 3.1 %collective-permute-done.9 = f32[32,1024]{1,0:T(8,128)S(1)} collective-permute-done((f32[32,1024]{1,0:T(8,128)S(1)}, f32[32,1024]{1,0:T(8,128)S(1)}, u32[]{:S(2)}, u32[]{:S(2)}) %collective-permute-start.9) | collective-permute-done | bytes 131104 | tf_op jit(solution)/shard_map/ppermute | solution.py:22
  31.4 0.8 %collective-permute-start.10 = (f32[32,1024]{1,0:T(8,128)S(1)}, f32[32,1024]{1,0:T(8,128)S(1)}, u32[]{:S(2)}, u32[]{:S(2)}) collective-permute-start(f32[32,1024]{1,0:T(8,128)S(1)} %select_add_fusion), channel_id=1, source_target_pairs={{0,8},{1,9},{2,10},{3,11},{4,12},{5,13},{6,14},{7,15},{8,0},{9,1},... | collective-permute-start | bytes 393224 | tf_op jit(solution)/shard_map/ppermute | solution.py:22
  32.2 12.1 %cache_attention.1 = (f32[2,32,1152]{2,1,0:T(8,128)S(1)}, f32[2,32,1152]{2,1,0:T(8,128)S(1)}, bf16[4,1024,1024]{2,1,0:T(8,128)(2,1)}, bf16[4,1024,1024]{2,1,0:T(8,128)(2,1)}) custom-call(s32[4]{0:T(128)S(1)} %iota_xor_fusion.reqs, s32[4]{0:T(128)S(1)} %broadcast_clamp_fusion.live, bf16[32,1024]{1,0:T(8,128)(2,1)S(1)} %fusion.1.refs_0_.q_ref, ...), custom_call_target="tpu_custom_call" | custom-call | flops 2147483648 | bytes 33554432 | tf_op jit(solution)/shard_map/cache_attention/pallas_call | solution.py:162
  44.5 0.1 fusion.28
  44.6 0.1 fusion.4
  44.8 2.1 %collective-permute-start.15 = (bf16[32,1024]{1,0:T(8,128)(2,1)S(1)}, bf16[32,1024]{1,0:T(8,128)(2,1)S(1)}, u32[]{:S(2)}, u32[]{:S(2)}) collective-permute-start(bf16[32,1024]{1,0:T(8,128)(2,1)S(1)} %fusion.4), channel_id=1, source_target_pairs={{0,4},{1,5},{2,6},{3,7},{4,0},{5,1},{6,2},{7,3},{8,12},{9,13},{10,... | collective-permute-start | bytes 196616 | tf_op jit(solution)/shard_map/ppermute | solution.py:22
  46.9 0.3 merge.4
  47.2 0.6 collective-permute-start.12
  47.8 1.8 %collective-permute-done.15 = bf16[32,1024]{1,0:T(8,128)(2,1)S(1)} collective-permute-done((bf16[32,1024]{1,0:T(8,128)(2,1)S(1)}, bf16[32,1024]{1,0:T(8,128)(2,1)S(1)}, u32[]{:S(2)}, u32[]{:S(2)}) %collective-permute-start.15) | collective-permute-done | bytes 65568 | tf_op jit(solution)/shard_map/ppermute | solution.py:22
  49.6 3.6 %collective-permute-done.12.refs_2_ = f32[32,1152]{1,0:T(8,128)S(1)} collective-permute-done((f32[32,1152]{1,0:T(8,128)S(1)}, f32[32,1152]{1,0:T(8,128)S(1)}, u32[]{:S(2)}, u32[]{:S(2)}) %collective-permute-start.12) | collective-permute-done | bytes 147488 | tf_op jit(solution)/shard_map/ppermute | solution.py:22
  53.2 0.4 merge.5.refs_0_
  53.6 1.3 %collective-permute-start.13 = (f32[32,1152]{1,0:T(8,128)S(1)}, f32[32,1152]{1,0:T(8,128)S(1)}, u32[]{:S(2)}, u32[]{:S(2)}) collective-permute-start(f32[32,1152]{1,0:T(8,128)S(1)} %merge.5.refs_0_), channel_id=1, source_target_pairs={{0,4},{1,5},{2,6},{3,7},{4,0},{5,1},{6,2},{7,3},{8,12},{9,13},{10,... | collective-permute-start | bytes 442376 | tf_op jit(solution)/shard_map/ppermute | solution.py:22
  54.9 0.6 collective-permute-start.19
  55.5 3.3 %collective-permute-done.13.refs_1_ = f32[32,1152]{1,0:T(8,128)S(1)} collective-permute-done((f32[32,1152]{1,0:T(8,128)S(1)}, f32[32,1152]{1,0:T(8,128)S(1)}, u32[]{:S(2)}, u32[]{:S(2)}) %collective-permute-start.13) | collective-permute-done | bytes 147488 | tf_op jit(solution)/shard_map/ppermute | solution.py:22
  58.8 0.3 merge.6.refs_0_
  59.1 1.5 %collective-permute-start.14 = (f32[32,1152]{1,0:T(8,128)S(1)}, f32[32,1152]{1,0:T(8,128)S(1)}, u32[]{:S(2)}, u32[]{:S(2)}) collective-permute-start(f32[32,1152]{1,0:T(8,128)S(1)} %merge.6.refs_0_), channel_id=1, source_target_pairs={{0,8},{1,9},{2,10},{3,11},{4,12},{5,13},{6,14},{7,15},{8,0},{9,1},... | collective-permute-start | bytes 442376 | tf_op jit(solution)/shard_map/ppermute | solution.py:22
  60.6 0.5 collective-permute-start.21
  61.1 0.7 tree_attention.1.refs_2_
  61.8 0.1 collective-permute-done.20.refs_2_
  61.9 0.2 collective-permute-done.21.refs_3_
  62.1 3.7 %patch.1 = (bf16[4,1024,1024]{2,1,0:T(8,128)(2,1)}, bf16[4,1024,1024]{2,1,0:T(8,128)(2,1)}) custom-call(s32[4]{0:T(128)S(1)} %iota_xor_fusion.reqs, s32[4]{0:T(128)S(1)} %get-tuple-element.59.firsts, s32[4]{0:T(128)S(1)} %get-tuple-element.60.starts, ...), custom_call_target="tpu_custom_call", output_to_operand_aliasing={{0}: (8, {}), {1}: (9, {})} | custom-call | bytes 1572864 | tf_op jit(solution)/shard_map/patch/pallas_call | solution.py:318
  65.8 1.4 %collective-permute-done.14.refs_1_ = f32[32,1152]{1,0:T(8,128)S(1)} collective-permute-done((f32[32,1152]{1,0:T(8,128)S(1)}, f32[32,1152]{1,0:T(8,128)S(1)}, u32[]{:S(2)}, u32[]{:S(2)}) %collective-permute-start.14) | collective-permute-done | bytes 147488 | tf_op jit(solution)/shard_map/ppermute | solution.py:22
  67.2 0.5 merge.7
  67.8 0.6 collective-permute-start.16
  68.4 0.2 fusion.35
  68.5 3.7 %collective-permute-done.16 = bf16[32,1024]{1,0:T(8,128)(2,1)S(1)} collective-permute-done((bf16[32,1024]{1,0:T(8,128)(2,1)S(1)}, bf16[32,1024]{1,0:T(8,128)(2,1)S(1)}, u32[]{:S(2)}, u32[]{:S(2)}) %collective-permute-start.16) | collective-permute-done | bytes 65568 | tf_op jit(solution)/shard_map/ppermute | solution.py:22
  72.3 0.2 fusion.34
  72.5 0.2 fusion.33
  72.7 1.1 %collective-permute-done.17 = bf16[32,1024]{1,0:T(8,128)(2,1)S(1)} collective-permute-done((bf16[32,1024]{1,0:T(8,128)(2,1)S(1)}, bf16[32,1024]{1,0:T(8,128)(2,1)S(1)}, u32[]{:S(2)}, u32[]{:S(2)}) %collective-permute-start.17) | collective-permute-done | bytes 65568 | tf_op jit(solution)/shard_map/ppermute | solution.py:22
  73.8 0.2 select_select_fusion.3
  74.0 1.6 %collective-permute-start.22 = (f32[64,128]{1,0:T(8,128)S(1)}, f32[64,128]{1,0:T(8,128)S(1)}, u32[]{:S(2)}, u32[]{:S(2)}) collective-permute-start(f32[64,128]{1,0:T(8,128)S(1)} %fusion.7), channel_id=1, source_target_pairs={{0,16},{16,0},{1,17},{17,1},{2,18},{18,2},{3,19},{19,3},{4,20},{20... | collective-permute-start | bytes 98312 | tf_op jit(solution)/shard_map/ppermute | solution.py:22
  75.6 2.4 %collective-permute-done.22 = f32[64,128]{1,0:T(8,128)S(1)} collective-permute-done((f32[64,128]{1,0:T(8,128)S(1)}, f32[64,128]{1,0:T(8,128)S(1)}, u32[]{:S(2)}, u32[]{:S(2)}) %collective-permute-start.22) | collective-permute-done | bytes 32800 | tf_op jit(solution)/shard_map/ppermute | solution.py:22
  77.9 0.6 add_convert_fusion
  (57 shorter events, 1.2 us)
Async XLA Ops:
  0.6 1.0 %copy-start = (bf16[128,1024]{1,0:T(8,128)(2,1)S(1)}, bf16[128,1024]{1,0:T(8,128)(2,1)}, u32[]{:S(2)}) copy-start(bf16[128,1024]{1,0:T(8,128)(2,1)} %param.12) | copy-start | bytes 786436
  0.6 17.7 %copy-start.3 = (s32[4,16]{1,0:T(4,128)S(1)}, s32[4,16]{1,0:T(4,128)}, u32[]{:S(2)}) copy-start(s32[4,16]{1,0:T(4,128)} %param.20) | copy-start | bytes 772
  0.7 17.8 %copy-start.4 = (s32[4]{0:T(128)S(1)}, s32[4]{0:T(128)}, u32[]{:S(2)}) copy-start(s32[4]{0:T(128)} %param.19) | copy-start | bytes 52
  1.8 1.7 %collective-permute-start = (f32[64,1024]{1,0:T(8,128)S(1)}, f32[64,1024]{1,0:T(8,128)S(1)}, u32[]{:S(2)}, u32[]{:S(2)}) collective-permute-start(f32[64,1024]{1,0:T(8,128)S(1)} %slice.120), channel_id=1, source_target_pairs={{0,1},{1,0},{2,3},{3,2},{4,5},{5,4},{6,7},{7,6},{8,9},{9,8},{10,11... | collective-permute-start | bytes 786440 | tf_op jit(solution)/shard_map/ppermute | solution.py:22
  3.6 6.7 %collective-permute-start.1 = (f32[32,1024]{1,0:T(8,128)S(1)}, f32[32,1024]{1,0:T(8,128)S(1)}, u32[]{:S(2)}, u32[]{:S(2)}) collective-permute-start(f32[32,1024]{1,0:T(8,128)S(1)} %slice.122), channel_id=1, source_target_pairs={{0,2},{1,3},{2,0},{3,1},{4,6},{5,7},{6,4},{7,5},{8,10},{9,11},{10,... | collective-permute-start | bytes 393224 | tf_op jit(solution)/shard_map/ppermute | solution.py:22
  9.0 6.5 %collective-permute-start.3 = (f32[64,2048]{1,0:T(8,128)S(1)}, f32[64,2048]{1,0:T(8,128)S(1)}, u32[]{:S(2)}, u32[]{:S(2)}) collective-permute-start(f32[64,2048]{1,0:T(8,128)S(1)} %pad_maximum_fusion), channel_id=1, source_target_pairs={{0,1},{1,0},{2,3},{3,2},{4,5},{5,4},{6,7},{7,6},{8,9},{9,8},{10,11... | collective-permute-start | bytes 1572872 | tf_op jit(solution)/shard_map/ppermute | solution.py:22
  10.3 5.1 %collective-permute-start.2 = (f32[32,1024]{1,0:T(8,128)S(1)}, f32[32,1024]{1,0:T(8,128)S(1)}, u32[]{:S(2)}, u32[]{:S(2)}) collective-permute-start(f32[32,1024]{1,0:T(8,128)S(1)} %slice_add_fusion.2), channel_id=1, source_target_pairs={{0,4},{1,5},{2,6},{3,7},{4,0},{5,1},{6,2},{7,3},{8,12},{9,13},{10,... | collective-permute-start | bytes 393224 | tf_op jit(solution)/shard_map/ppermute | solution.py:22
  15.5 7.9 %collective-permute-start.4 = (f32[32,1024]{1,0:T(8,128)S(1)}, f32[32,1024]{1,0:T(8,128)S(1)}, u32[]{:S(2)}, u32[]{:S(2)}) collective-permute-start(f32[32,1024]{1,0:T(8,128)S(1)} %add.109), channel_id=1, source_target_pairs={{0,8},{1,9},{2,10},{3,11},{4,12},{5,13},{6,14},{7,15},{8,0},{9,1},... | collective-permute-start | bytes 393224 | tf_op jit(solution)/shard_map/ppermute | solution.py:22
  19.1 7.1 %collective-permute-start.8 = (f32[32,2048]{1,0:T(8,128)S(1)}, f32[32,2048]{1,0:T(8,128)S(1)}, u32[]{:S(2)}, u32[]{:S(2)}) collective-permute-start(f32[32,2048]{1,0:T(8,128)S(1)} %slice.108), channel_id=1, source_target_pairs={{0,2},{1,3},{2,0},{3,1},{4,6},{5,7},{6,4},{7,5},{8,10},{9,11},{10,... | collective-permute-start | bytes 786440 | tf_op jit(solution)/shard_map/ppermute | solution.py:22
  23.8 4.3 %collective-permute-start.5 = (bf16[32,1024]{1,0:T(8,128)(2,1)S(1)}, bf16[32,1024]{1,0:T(8,128)(2,1)S(1)}, u32[]{:S(2)}, u32[]{:S(2)}) collective-permute-start(bf16[32,1024]{1,0:T(8,128)(2,1)S(1)} %fusion.1.refs_0_.q_ref), channel_id=1, source_target_pairs={{0,2},{1,3},{2,0},{3,1},{4,6},{5,7},{6,4},{7,5},{8,10},{9,11},{10,... | collective-permute-start | bytes 196616 | tf_op jit(solution)/shard_map/ppermute | solution.py:22
  26.3 5.0 %collective-permute-start.9 = (f32[32,1024]{1,0:T(8,128)S(1)}, f32[32,1024]{1,0:T(8,128)S(1)}, u32[]{:S(2)}, u32[]{:S(2)}) collective-permute-start(f32[32,1024]{1,0:T(8,128)S(1)} %slice_select_fusion), channel_id=1, source_target_pairs={{0,4},{1,5},{2,6},{3,7},{4,0},{5,1},{6,2},{7,3},{8,12},{9,13},{10,... | collective-permute-start | bytes 393224 | tf_op jit(solution)/shard_map/ppermute | solution.py:22
  27.7 3.7 %collective-permute-start.6 = (bf16[32,1024]{1,0:T(8,128)(2,1)S(1)}, bf16[32,1024]{1,0:T(8,128)(2,1)S(1)}, u32[]{:S(2)}, u32[]{:S(2)}) collective-permute-start(bf16[32,1024]{1,0:T(8,128)(2,1)S(1)} %fusion.1.refs_0_.q_ref), channel_id=1, source_target_pairs={{0,1},{1,0},{2,3},{3,2},{4,5},{5,4},{6,7},{7,6},{8,9},{9,8},{10,11... | collective-permute-start | bytes 196616 | tf_op jit(solution)/shard_map/ppermute | solution.py:22
  28.1 3.3 %collective-permute-start.7 = (bf16[32,1024]{1,0:T(8,128)(2,1)S(1)}, bf16[32,1024]{1,0:T(8,128)(2,1)S(1)}, u32[]{:S(2)}, u32[]{:S(2)}) collective-permute-start(bf16[32,1024]{1,0:T(8,128)(2,1)S(1)} %collective-permute-done.5.refs_1_), channel_id=1, source_target_pairs={{0,1},{1,0},{2,3},{3,2},{4,5},{5,4},{6,7},{7,6},{8,9},{9,8},{10,11... | collective-permute-start | bytes 196616 | tf_op jit(solution)/shard_map/ppermute | solution.py:22
  31.3 29.8 %copy-start.2 = (s32[4,32,32]{2,1,0:T(8,128)S(1)}, s32[4,32,32]{2,1,0:T(8,128)}, u32[]{:S(2)}) copy-start(s32[4,32,32]{2,1,0:T(8,128)} %param.21) | copy-start | bytes 49156
  31.4 13.0 %collective-permute-start.10 = (f32[32,1024]{1,0:T(8,128)S(1)}, f32[32,1024]{1,0:T(8,128)S(1)}, u32[]{:S(2)}, u32[]{:S(2)}) collective-permute-start(f32[32,1024]{1,0:T(8,128)S(1)} %select_add_fusion), channel_id=1, source_target_pairs={{0,8},{1,9},{2,10},{3,11},{4,12},{5,13},{6,14},{7,15},{8,0},{9,1},... | collective-permute-start | bytes 393224 | tf_op jit(solution)/shard_map/ppermute | solution.py:22
  44.6 2.3 %collective-permute-start.11 = (f32[2,32,1152]{2,1,0:T(8,128)S(1)}, f32[2,32,1152]{2,1,0:T(8,128)S(1)}, u32[]{:S(2)}, u32[]{:S(2)}) collective-permute-start(f32[2,32,1152]{2,1,0:T(8,128)S(1)} %get-tuple-element.48), channel_id=1, source_target_pairs={{0,1},{1,0},{2,3},{3,2},{4,5},{5,4},{6,7},{7,6},{8,9},{9,8},{10,11... | collective-permute-start | bytes 884744 | tf_op jit(solution)/shard_map/ppermute | solution.py:22
  44.8 4.8 %collective-permute-start.15 = (bf16[32,1024]{1,0:T(8,128)(2,1)S(1)}, bf16[32,1024]{1,0:T(8,128)(2,1)S(1)}, u32[]{:S(2)}, u32[]{:S(2)}) collective-permute-start(bf16[32,1024]{1,0:T(8,128)(2,1)S(1)} %fusion.4), channel_id=1, source_target_pairs={{0,4},{1,5},{2,6},{3,7},{4,0},{5,1},{6,2},{7,3},{8,12},{9,13},{10,... | collective-permute-start | bytes 196616 | tf_op jit(solution)/shard_map/ppermute | solution.py:22
  47.2 6.0 %collective-permute-start.12 = (f32[32,1152]{1,0:T(8,128)S(1)}, f32[32,1152]{1,0:T(8,128)S(1)}, u32[]{:S(2)}, u32[]{:S(2)}) collective-permute-start(f32[32,1152]{1,0:T(8,128)S(1)} %merge.4), channel_id=1, source_target_pairs={{0,2},{1,3},{2,0},{3,1},{4,6},{5,7},{6,4},{7,5},{8,10},{9,11},{10,... | collective-permute-start | bytes 442376 | tf_op jit(solution)/shard_map/ppermute | solution.py:22
  53.6 5.2 %collective-permute-start.13 = (f32[32,1152]{1,0:T(8,128)S(1)}, f32[32,1152]{1,0:T(8,128)S(1)}, u32[]{:S(2)}, u32[]{:S(2)}) collective-permute-start(f32[32,1152]{1,0:T(8,128)S(1)} %merge.5.refs_0_), channel_id=1, source_target_pairs={{0,4},{1,5},{2,6},{3,7},{4,0},{5,1},{6,2},{7,3},{8,12},{9,13},{10,... | collective-permute-start | bytes 442376 | tf_op jit(solution)/shard_map/ppermute | solution.py:22
  54.9 5.7 %collective-permute-start.19 = (bf16[32,2048]{1,0:T(8,128)(2,1)S(1)}, bf16[32,2048]{1,0:T(8,128)(2,1)S(1)}, u32[]{:S(2)}, u32[]{:S(2)}) collective-permute-start(bf16[32,2048]{1,0:T(8,128)(2,1)S(1)} %pad_maximum_fusion.1.kv_ref.refs_0_), channel_id=1, source_target_pairs={{0,2},{1,3},{2,0},{3,1},{4,6},{5,7},{6,4},{7,5},{8,10},{9,11},{10,... | collective-permute-start | bytes 393224 | tf_op jit(solution)/shard_map/ppermute | solution.py:22
  59.1 8.1 %collective-permute-start.14 = (f32[32,1152]{1,0:T(8,128)S(1)}, f32[32,1152]{1,0:T(8,128)S(1)}, u32[]{:S(2)}, u32[]{:S(2)}) collective-permute-start(f32[32,1152]{1,0:T(8,128)S(1)} %merge.6.refs_0_), channel_id=1, source_target_pairs={{0,8},{1,9},{2,10},{3,11},{4,12},{5,13},{6,14},{7,15},{8,0},{9,1},... | collective-permute-start | bytes 442376 | tf_op jit(solution)/shard_map/ppermute | solution.py:22
  60.6 1.3 %collective-permute-start.20 = (bf16[32,2048]{1,0:T(8,128)(2,1)S(1)}, bf16[32,2048]{1,0:T(8,128)(2,1)S(1)}, u32[]{:S(2)}, u32[]{:S(2)}) collective-permute-start(bf16[32,2048]{1,0:T(8,128)(2,1)S(1)} %pad_maximum_fusion.1.kv_ref.refs_0_), channel_id=1, source_target_pairs={{0,1},{1,0},{2,3},{3,2},{4,5},{5,4},{6,7},{7,6},{8,9},{9,8},{10,11... | collective-permute-start | bytes 393224 | tf_op jit(solution)/shard_map/ppermute | solution.py:22
  60.6 1.5 %collective-permute-start.21 = (bf16[32,2048]{1,0:T(8,128)(2,1)S(1)}, bf16[32,2048]{1,0:T(8,128)(2,1)S(1)}, u32[]{:S(2)}, u32[]{:S(2)}) collective-permute-start(bf16[32,2048]{1,0:T(8,128)(2,1)S(1)} %collective-permute-done.19.refs_1_), channel_id=1, source_target_pairs={{0,1},{1,0},{2,3},{3,2},{4,5},{5,4},{6,7},{7,6},{8,9},{9,8},{10,11... | collective-permute-start | bytes 393224 | tf_op jit(solution)/shard_map/ppermute | solution.py:22
  62.1 6.3 %copy-start.1 = (bf16[1024,128]{1,0:T(8,128)(2,1)S(1)}, bf16[1024,128]{1,0:T(8,128)(2,1)}, u32[]{:S(2)}) copy-start(bf16[1024,128]{1,0:T(8,128)(2,1)} %param.15) | copy-start | bytes 786436
  67.7 4.8 %collective-permute-start.18 = (bf16[32,1024]{1,0:T(8,128)(2,1)S(1)}, bf16[32,1024]{1,0:T(8,128)(2,1)S(1)}, u32[]{:S(2)}, u32[]{:S(2)}) collective-permute-start(bf16[32,1024]{1,0:T(8,128)(2,1)S(1)} %merge.7), channel_id=1, source_target_pairs={{0,1},{1,0},{2,3},{3,2},{4,5},{5,4},{6,7},{7,6},{8,9},{9,8},{10,11... | collective-permute-start | bytes 196616 | tf_op jit(solution)/shard_map/ppermute | solution.py:22
  67.8 4.5 %collective-permute-start.16 = (bf16[32,1024]{1,0:T(8,128)(2,1)S(1)}, bf16[32,1024]{1,0:T(8,128)(2,1)S(1)}, u32[]{:S(2)}, u32[]{:S(2)}) collective-permute-start(bf16[32,1024]{1,0:T(8,128)(2,1)S(1)} %merge.7), channel_id=1, source_target_pairs={{0,2},{1,3},{2,0},{3,1},{4,6},{5,7},{6,4},{7,5},{8,10},{9,11},{10,... | collective-permute-start | bytes 196616 | tf_op jit(solution)/shard_map/ppermute | solution.py:22
  72.4 1.3 %collective-permute-start.17 = (bf16[32,1024]{1,0:T(8,128)(2,1)S(1)}, bf16[32,1024]{1,0:T(8,128)(2,1)S(1)}, u32[]{:S(2)}, u32[]{:S(2)}) collective-permute-start(bf16[32,1024]{1,0:T(8,128)(2,1)S(1)} %collective-permute-done.16), channel_id=1, source_target_pairs={{0,1},{1,0},{2,3},{3,2},{4,5},{5,4},{6,7},{7,6},{8,9},{9,8},{10,11... | collective-permute-start | bytes 196616 | tf_op jit(solution)/shard_map/ppermute | solution.py:22
  74.0 4.0 %collective-permute-start.22 = (f32[64,128]{1,0:T(8,128)S(1)}, f32[64,128]{1,0:T(8,128)S(1)}, u32[]{:S(2)}, u32[]{:S(2)}) collective-permute-start(f32[64,128]{1,0:T(8,128)S(1)} %fusion.7), channel_id=1, source_target_pairs={{0,16},{16,0},{1,17},{17,1},{2,18},{18,2},{3,19},{19,3},{4,20},{20... | collective-permute-start | bytes 98312 | tf_op jit(solution)/shard_map/ppermute | solution.py:22
